TPU v7x, 256 devices: a whole 4x4x8 slice. The times are simulated.
256 devices in a mesh: ctx: 32 (over x, y, core), head: 8 (over z).
Axes of the slice: x: 4, y: 4, z: 8, core: 2. Of those that a mesh axis runs over, the one named last changes fastest.
Arguments:
- lin_q: bfloat16 [8192, 8192], P('ctx', 'head'), may hold values from -4 to 4
- lin_k: bfloat16 [8192, 8192], P('ctx', 'head'), may hold values from -4 to 4
- lin_v: bfloat16 [8192, 8192], P('ctx', 'head'), may hold values from -6 to 6
- log_decay: float32 [64, 8192], P('head', 'ctx'), may hold values from -1 to 0
- lin_gain: float32 [8192], P('head'), may hold values from 0.1 to 1.9
- soft_q: bfloat16 [8192, 8192], P(('ctx', 'head')), may hold values from -200 to 200
- soft_kv: bfloat16 [8192, 2048], P(('ctx', 'head')), may hold values from -8 to 8
Outputs:
- lin_out: bfloat16 [8192, 8192], P('ctx', 'head')
- soft_out: bfloat16 [8192, 8192], P(('ctx', 'head'))
All inputs are finite; a program needn't handle non-finite values.
Results may differ from a plain program's by a relative error of at most 0.013.
Values may be sent and summed in bfloat16 or wider, within the bound.
No kernel may reach another device: no remote copies, remote signals or barrier semaphores. Data moves between devices by JAX's collectives and lax.ppermute only.
A program may use at most 64 MiB of HBM per device.

v0:
```python
import math

import jax
import jax.numpy as jnp
from jax import lax
from jax.sharding import Mesh
from jax.sharding import PartitionSpec as P

CTX = ("ctx_0", "ctx_1", "ctx_2")
CTX_HEAD = ("ctx_0", "ctx_1", "ctx_2", "head")


def filled_with(value, identity):
    return jax.tree.map(
        lambda part, zero: jnp.zeros_like(part) + jnp.asarray(zero, part.dtype), value, identity
    )


def carried_in(value, axes, combine, identity):
    before = start = filled_with(value, identity)
    so_far = value
    for axis in reversed(axes):
        devices, index = (lax.axis_size(axis), lax.axis_index(axis))
        pieces = jax.tree.map(
            lambda part, kind: lax.all_gather(part.astype(kind), axis),
            so_far,
            (jnp.bfloat16, jnp.bfloat16),
        )
        inside, so_far = (start, start)
        for k in range(devices):
            passed = k < index
            so_far = combine(
                so_far, jax.tree.map(lambda part, own: part[k].astype(own.dtype), pieces, value)
            )
            inside = jax.tree.map(lambda new, old: jnp.where(passed, new, old), so_far, inside)
        before = combine(inside, before)
    return before


def block_local(kb, gb):
    cum = jnp.cumsum(gb, axis=1)
    keys_scaled = (kb.astype(jnp.float32) * jnp.exp(cum[:, -1:] - cum).T[:, :, None]).astype(
        jnp.bfloat16
    )
    return (cum, keys_scaled)


def block_output(qb, kb, vb, cum, state):
    size = cum.shape[1]
    pos = jnp.arange(size)
    causal = pos[:, None] >= pos[None, :]
    diff = cum[:, :, None] - cum[:, None, :]
    weight = jnp.where(causal[None], jnp.exp(jnp.minimum(diff, 0.0)), 0.0)
    scores = jnp.einsum("thd,shd->hts", qb, kb, preferred_element_type=jnp.float32)
    probs = (scores * weight).astype(jnp.bfloat16)
    intra = jnp.einsum("hts,shd->thd", probs, vb, preferred_element_type=jnp.float32)
    inter = jnp.einsum(
        "thd,hde->the", qb, state.astype(jnp.bfloat16), preferred_element_type=jnp.float32
    )
    return intra + jnp.exp(cum).T[:, :, None] * inter


def join_states(earlier, later):
    return (earlier[0] + later[0], jnp.exp(later[0])[:, None, None] * earlier[1] + later[1])


def lightning_part(lin_q, lin_k, lin_v, log_decay, lin_gain):
    tok, width = lin_q.shape
    heads = log_decay.shape[0]
    dim = width // heads
    q = lin_q.reshape(tok, heads, dim)
    k = lin_k.reshape(tok, heads, dim)
    v = lin_v.reshape(tok, heads, dim)
    total = (jnp.zeros((heads,), jnp.float32), jnp.zeros((heads, dim, dim), jnp.float32))
    cum, keys_scaled = block_local(k, log_decay)
    local = jnp.einsum("shd,she->hde", keys_scaled, v, preferred_element_type=jnp.float32)
    total = join_states(total, (cum[:, -1], local))
    identity = (jnp.zeros((heads,), jnp.float32), jnp.zeros((heads, dim, dim), jnp.float32))
    entering = carried_in((total[0], total[1]), CTX, join_states, identity)
    state = entering[1]
    mixed = block_output(q, k, v, cum, state)
    rms = jnp.sqrt(jnp.mean(mixed * mixed, axis=-1, keepdims=True) + 1e-05)
    outputs = mixed / rms * lin_gain.reshape(heads, dim)
    return outputs.reshape(tok, width).astype(jnp.bfloat16)


def softmax_part(soft_q, soft_kv, dim):
    local_q, local_kv = (
        lax.all_to_all(soft_q, "head", split_axis=1, concat_axis=0, tiled=True),
        lax.all_to_all(soft_kv, "head", split_axis=1, concat_axis=0, tiled=True),
    )
    tok = local_q.shape[0]
    half = tok // 2
    kvl = local_kv.shape[1] // (2 * dim)
    group = local_q.shape[1] // (dim * kvl)
    mine = lax.axis_index(CTX)
    first_q = local_q[:half]
    second_q = local_q[half:]
    second_start = mine * tok + half
    first_start = mine * tok
    first_pos = first_start + jnp.arange(half)
    second_pos = second_start + jnp.arange(half)
    first_heads = first_q.reshape(half, kvl, group, dim)
    second_heads = second_q.reshape(half, kvl, group, dim)
    scale = dim ** (-0.5)

    def update(carry, queries, qpos, kblock, kstart):
        peak, total, acc = carry
        size = kblock.shape[0]
        pair = kblock.reshape(size, kvl, 2, dim)
        key_matrix = pair[:, :, 0]
        value_rows = pair[:, :, 1]
        kpos = kstart + jnp.arange(size)
        mask = (kpos[None, :] <= qpos[:, None])[None, None]
        scores = (
            jnp.einsum("qngd,knd->ngqk", queries, key_matrix, preferred_element_type=jnp.float32)
            * scale
        )
        scores = jnp.where(mask, scores, -1e30)
        newpeak = jnp.maximum(peak, jnp.max(scores, axis=-1))
        weights = jnp.where(mask, jnp.exp(scores - newpeak[..., None]), 0.0)
        decay_factor = jnp.exp(peak - newpeak)
        total = total * decay_factor + jnp.sum(weights, axis=-1)
        acc = acc * decay_factor[..., None] + jnp.einsum(
            "ngqk,knd->ngqd",
            weights.astype(jnp.bfloat16),
            value_rows,
            preferred_element_type=jnp.float32,
        )
        return (newpeak, total, acc)

    def guarded(carry, queries, qpos, qlast, kblock, kstart):
        return lax.cond(
            kstart <= qlast, lambda c: update(c, queries, qpos, kblock, kstart), lambda c: c, carry
        )

    def start_carry():
        return (
            jnp.full((kvl, group, half), -1e30, jnp.float32),
            jnp.zeros((kvl, group, half), jnp.float32),
            jnp.zeros((kvl, group, half, dim), jnp.float32),
        )

    def finish(carry):
        peak, total, acc = carry
        result = acc / total[..., None]
        return result.transpose(2, 0, 1, 3).reshape(half, kvl * group * dim).astype(jnp.bfloat16)

    piece = lax.all_gather(local_kv, CTX, axis=0, tiled=True)
    rows = piece.shape[0]
    width = math.gcd(rows, 512)

    def step(index, inner):
        kblock = lax.dynamic_slice_in_dim(piece, index * width, width, 0)
        kstart = index * width
        early = guarded(inner[0], first_heads, first_pos, first_start + half - 1, kblock, kstart)
        later = guarded(inner[1], second_heads, second_pos, second_start + half - 1, kblock, kstart)
        return (early, later)

    early, later = lax.fori_loop(0, rows // width, step, (start_carry(), start_carry()))
    first_out = finish(early)
    second_out = finish(later)
    result = jnp.concatenate([first_out, second_out], axis=0)
    return lax.all_to_all(result, "head", split_axis=0, concat_axis=1, tiled=True)


def body(lin_q, lin_k, lin_v, log_decay, lin_gain, soft_q, soft_kv):
    heads = log_decay.shape[0]
    dim = lin_q.shape[1] // heads
    lin_out = lightning_part(lin_q, lin_k, lin_v, log_decay, lin_gain)
    soft_out = softmax_part(soft_q, soft_kv, dim)
    return (lin_out, soft_out)


def solution(mesh):
    finer = Mesh(
        mesh.devices.reshape(4, 4, 2, mesh.shape["head"]), ("ctx_0", "ctx_1", "ctx_2", "head")
    )
    placed = (
        P(CTX, "head"),
        P(CTX, "head"),
        P(CTX, "head"),
        P("head", CTX),
        P("head"),
        P(CTX_HEAD, None),
        P(CTX_HEAD, None),
    )
    return jax.shard_map(
        body,
        mesh=finer,
        in_specs=placed,
        out_specs=(P(CTX, "head"), P(CTX_HEAD, None)),
        check_vma=False,
    )
```

profile of v0, /device:TPU:31, one launch (start us, length us, event | category | flops | bytes accessed | tf_op | source)
XLA Modules:
  0.0 221.1 jit_solution(15442327545542827741)
XLA Ops:
  11.4 2.8 %all-reduce = bf16[16]{0:T(256)(128)(2,1)S(1)} all-reduce(bf16[16]{0:T(256)(128)(2,1)S(1)} %dynamic-update-slice), channel_id=2, replica_groups=mesh['ctx_0'=4,'ctx_1'=4,'ctx_2'=2,'head'=8] {'ctx_2'}, use_global_device_ids=true, to_apply=%add | all-reduce | flops 16 | bytes 64
  17.7 2.2 all-gather.1
  20.9 16.0 %all_to_all.54 = bf16[32,8,256]{2,0,1:T(8,128)(2,1)} all-to-all(bf16[32,8,256]{2,0,1:T(8,128)(2,1)S(1)} %bitcast.354), channel_id=1, replica_groups=mesh['ctx_0'=4,'ctx_1'=4,'ctx_2'=2,'head'=8] {'head'}, dimensions={1} | all-to-all | bytes 262144 | tf_op jit(solution)/shard_map/all_to_all | solution.py:90
  37.8 3.5 %all-to-all-start.1 = ((bf16[32,8,1024]{2,0,1:T(8,128)(2,1)}), bf16[32,8,1024]{2,0,1:T(8,128)(2,1)S(1)}, u32[]{:S(2)}, u32[]{:S(2)}) async-start(bf16[32,8,1024]{2,0,1:T(8,128)(2,1)} %bitcast.330), calls=%async_computation.1 | async-start | bytes 1048576 | tf_op jit(solution)/shard_map/all_to_all | solution.py:89
  41.4 5.2 %all-gather.2 = bf16[4,1,8]{2,1,0:T(2,128)(2,1)S(1)} all-gather(bf16[1,1,8]{2,1,0:T(2,128)(2,1)S(1)} %get-tuple-element.626), channel_id=1, replica_groups=mesh['ctx_0'=4,'ctx_1'=4,'ctx_2'=2,'head'=8] {'ctx_1'}, dimensions={0}, use_global_device_ids=true | all-gather | bytes 80 | tf_op jit(solution)/shard_map/all_gather | solution.py:25
  46.6 5.3 %all-gather.3 = bf16[4,1,8]{2,1,0:T(2,128)(2,1)S(1)} all-gather(bf16[1,1,8]{2,1,0:T(2,128)(2,1)S(1)} %get-tuple-element.620), channel_id=1, replica_groups=mesh['ctx_0'=4,'ctx_1'=4,'ctx_2'=2,'head'=8] {'ctx_0'}, dimensions={0}, use_global_device_ids=true | all-gather | bytes 80 | tf_op jit(solution)/shard_map/all_gather | solution.py:25
  52.0 5.0 %all-to-all-done.1 = bf16[32,8,1024]{2,0,1:T(8,128)(2,1)S(1)} async-done(((bf16[32,8,1024]{2,0,1:T(8,128)(2,1)}), bf16[32,8,1024]{2,0,1:T(8,128)(2,1)S(1)}, u32[]{:S(2)}, u32[]{:S(2)}) %all-to-all-start.1) | async-done | bytes 524320 | tf_op jit(solution)/shard_map/all_to_all | solution.py:89
  57.3 2.3 %fusion.66 = bf16[1,8,128,128]{3,2,1,0:T(8,128)(2,1)} fusion(f32[8]{0:T(128)S(1)} %get-tuple-element.624, f32[8]{0:T(128)S(1)} %get-tuple-element.623, f32[8]{0:T(128)S(1)} %get-tuple-element.622, f32[8]{0:T(128)S(1)} %get-tuple-element.621, bf16[4,8,128,128]{3,2,1,0:T(8,128)(2,1)} %all-gather.8.cloned.1.call-done), kind=kLoop, calls=%fused_computation.103 | loop fusion | flops 1572864 | bytes 1310848 | tf_op jit(solution)/shard_map/convert_element_type | solution.py:25
  59.6 42.5 %all-gather.12.cloned.1.call-done = bf16[8192,256]{1,0:T(8,128)(2,1)} async-done(((bf16[256,256]{1,0:T(8,128)(2,1)}), bf16[8192,256]{1,0:T(8,128)(2,1)}) %all-gather.12.cloned.1.call-update) | async-done | bytes 4194320 | tf_op jit(solution)/shard_map/all_gather | solution.py:149
  102.3 85.3 %while.27 = (s32[]{:T(128)}, f32[1,8,128]{2,1,0:T(8,128)S(1)}, f32[1,8,128]{2,1,0:T(8,128)S(1)}, f32[1,8,128,128]{3,2,1,0:T(8,128)S(1)}, f32[1,8,128]{2,1,0:T(8,...) while((s32[]{:T(128)}, f32[1,8,128]{2,1,0:T(8,128)S(1)}, ...), condition=%wide.region_12.13_spmd.clone, body=%wide.region_3.12_spmd.clone.sunk | while | flops 551165184 | bytes 17445364 | solution.py:160
  130.1 2.1 conditional.7
  135.4 2.1 conditional.7
  140.7 2.1 conditional.7
  146.1 2.1 conditional.7
  151.4 2.1 conditional.7
  156.7 2.1 conditional.7
  162.0 2.1 conditional.7
  167.4 2.1 conditional.7
  172.7 2.1 conditional.7
  178.0 2.1 conditional.7
  189.2 6.7 %all-to-all-start.2 = ((bf16[8,32,1024]{2,1,0:T(8,128)(2,1)}), bf16[8,32,1024]{2,1,0:T(8,128)(2,1)S(1)}, u32[]{:S(2)}, u32[]{:S(2)}) async-start(bf16[8,32,1024]{2,1,0:T(8,128)(2,1)} %bitcast.73), calls=%async_computation.2 | async-start | bytes 1048576 | tf_op jit(solution)/shard_map/all_to_all | solution.py:164
  195.9 3.6 %fusion.41 = f32[256,8,128]{0,2,1:T(8,128)} fusion(f32[256,8]{0,1:T(8,128)S(1)} %get-tuple-element.608, bf16[4,8,128,128]{3,2,1,0:T(8,128)(2,1)} %all-gather.10.cloned.1.call-done, f32[8]{0:T(128)S(1)} %get-tuple-element.627, f32[8]{0:T(128)S(1)} %get-tuple-element.625, f32[8]{0:T(128)S(1)} %get-tuple-element.624, f32[8]{0:T(128)S(1)} %get-tuple-element.623, ...), kind=kOutput, calls=%fused_computation.62 | convolution fusion | flops 72876032 | bytes 4202890 | tf_op jit(solution)/shard_map/thd,hde->the/dot_general | solution.py:57
  199.5 2.4 %multiply_reduce_fusion = (f32[256,8]{0,1:T(8,128)S(1)}, f32[256,8,128]{0,2,1:T(8,128)S(1)}) fusion(f32[256,8,128]{0,2,1:T(8,128)} %fusion.41, bf16[256,8,128]{0,2,1:T(8,128)(2,1)S(1)} %bitcast.351, f32[8,256]{1,0:T(8,128)S(1)} %get-tuple-element.609, pred[256,256]{1,0:T(8,128)(4,1)S(1)} %iota_compare_fusion, bf16[256,1024]{1,0:T(8,128)(2,1)} %param.15, ...), kind=kOutput, calls=%fused_computation.66 | convolution fusion | flops 271841280 | bytes 3751936 | tf_op jit(solution)/shard_map/hts,shd->thd/dot_general | solution.py:56
  203.1 10.7 %all-to-all-done.2 = bf16[8,32,1024]{2,1,0:T(8,128)(2,1)S(1)} async-done(((bf16[8,32,1024]{2,1,0:T(8,128)(2,1)}), bf16[8,32,1024]{2,1,0:T(8,128)(2,1)S(1)}, u32[]{:S(2)}, u32[]{:S(2)}) %all-to-all-start.2) | async-done | bytes 524320 | tf_op jit(solution)/shard_map/all_to_all | solution.py:164
  (438 shorter events, 139.9 us)
Async XLA Ops:
  7.2 188.7 %copy-start = (bf16[256,1024]{1,0:T(8,128)(2,1)S(1)}, bf16[256,1024]{1,0:T(8,128)(2,1)}, u32[]{:S(2)}) copy-start(bf16[256,1024]{1,0:T(8,128)(2,1)} %param.13) | copy-start | bytes 1572868
  7.2 50.1 %all-gather.8.cloned.1.call-start = ((), (), s32[]{:S(2)}) async-start(), calls=%async_computation.3 | async-start | bytes 1310720 | tf_op jit(solution)/shard_map/all_gather | solution.py:25
  14.3 6.6 %copy-start.4 = (bf16[32,2048]{1,0:T(8,128)(2,1)S(1)}, bf16[32,2048]{1,0:T(8,128)(2,1)}, u32[]{:S(2)}) copy-start(bf16[32,2048]{1,0:T(8,128)(2,1)} %param.19) | copy-start | bytes 393220
  15.6 0.8 copy-start.2
  15.6 21.4 %copy-start.1 = (bf16[32,8192]{1,0:T(8,128)(2,1)S(1)}, bf16[32,8192]{1,0:T(8,128)(2,1)}, u32[]{:S(2)}) copy-start(bf16[32,8192]{1,0:T(8,128)(2,1)} %param.18) | copy-start | bytes 1572868
  20.8 81.3 %all-gather.12.cloned.1.call-start = ((), (), s32[]{:S(2)}) async-start(), calls=%async_computation.5 | async-start | bytes 4325376 | tf_op jit(solution)/shard_map/all_gather | solution.py:149
  37.8 19.2 %all-to-all-start.1 = ((bf16[32,8,1024]{2,0,1:T(8,128)(2,1)}), bf16[32,8,1024]{2,0,1:T(8,128)(2,1)S(1)}, u32[]{:S(2)}, u32[]{:S(2)}) async-start(bf16[32,8,1024]{2,0,1:T(8,128)(2,1)} %bitcast.330), calls=%async_computation.1 | async-start | bytes 1048576 | tf_op jit(solution)/shard_map/all_to_all | solution.py:89
  41.3 154.5 %all-gather.10.cloned.1.call-start = ((), (), s32[]{:S(2)}) async-start(), calls=%async_computation.4 | async-start | bytes 1310720 | tf_op jit(solution)/shard_map/all_gather | solution.py:25
  189.2 24.6 %all-to-all-start.2 = ((bf16[8,32,1024]{2,1,0:T(8,128)(2,1)}), bf16[8,32,1024]{2,1,0:T(8,128)(2,1)S(1)}, u32[]{:S(2)}, u32[]{:S(2)}) async-start(bf16[8,32,1024]{2,1,0:T(8,128)(2,1)} %bitcast.73), calls=%async_computation.2 | async-start | bytes 1048576 | tf_op jit(solution)/shard_map/all_to_all | solution.py:164
  195.9 3.6 %copy-start.3 = (bf16[256,1024]{0,1:T(8,128)(2,1)S(1)}, bf16[256,1024]{0,1:T(8,128)(2,1)}, u32[]{:S(2)}) copy-start(bf16[256,1024]{0,1:T(8,128)(2,1)} %copy-done.2) | copy-start | bytes 1572868
  199.5 2.4 %copy-start.5 = (f32[1024]{0:T(1024)S(1)}, f32[1024]{0:T(1024)}, u32[]{:S(2)}) copy-start(f32[1024]{0:T(1024)} %param.17) | copy-start | bytes 12292
Sparse Core Ops, SparseCore 0:
  20.9 26.1 all-gather.7
  49.7 52.4 all-gather.11
  104.5 25.1 all-gather.9
where the time goes:
time: 222 us; the launch traced here: 221 us
  waiting for transfers between devices  58.3 us (26%)
  matrix products  49.3 us (22%)
  blocking collectives  31.5 us (14%)
  other arithmetic  26.8 us (12%)
  local copies, waits for them, and re-layouts  26.5 us (12%)
  between operations  14.7 us (7%)
  starting transfers between devices  10.3 us (5%)
  loops' own time  3.78 us (2%)
    all_gather x1, waiting for transfers between devices, softmax_part(): piece = lax.all_gather(local_kv, CTX, axis=0, tiled=True)  42.5 us
    dot_general x32, matrix products, update(): jnp.einsum('ngqk,knd->ngqd', weights.astype(jnp.bfloat16), value_rows, pr...  26.6 us
    dynamic_slice x32, local copies, waits for them, and re-layouts, step(): kblock = lax.dynamic_slice_in_dim(piece, index * width, width, 0)  17.8 us
    reduce_sum x32, other arithmetic, update(): total = total * decay_factor + jnp.sum(weights, axis=-1)  16.4 us
    all_to_all x1, blocking collectives, softmax_part(): lax.all_to_all(soft_kv, 'head', split_axis=1, concat_axis=0, tiled=True)  16 us
    dot_general x32, matrix products, update(): jnp.einsum('qngd,knd->ngqk', queries, key_matrix, preferred_element_type=...  15.3 us
    all_gather x3, blocking collectives, carried_in(): lax.all_gather(part.astype(kind), axis)  12.7 us
    all_to_all x1, waiting for transfers between devices, softmax_part(): lax.all_to_all(result, 'head', split_axis=0, concat_axis=1, tiled=True)  10.7 us
  transfers between devices with their start and end apart: 5, of which 3 were waited for; matrix products, arithmetic and copies ran while one was open for 42% of the time, Pallas kernels for 0%

commit v1 on v0

v1 whole, which is shorter than its diff:
```python
import functools
import math

import jax
import jax.numpy as jnp
from jax import lax
from jax.experimental import pallas as pl
from jax.experimental.pallas import tpu as pltpu
from jax.sharding import Mesh
from jax.sharding import PartitionSpec as P

CTX = ("ctx_0", "ctx_1", "ctx_2")
CTX_HEAD = ("ctx_0", "ctx_1", "ctx_2", "head")
NX, NY, NC, NZ = 4, 4, 2, 8
CH = 256
DIM = 128
HEADS = 8
MSG = 48

NT = (((1,), (1,)), ((), ()))
NN = (((1,), (0,)), ((), ()))
TN = (((0,), (0,)), ((), ()))


def dot(a, b, dims):
    return lax.dot_general(a, b, dims, preferred_element_type=jnp.float32)


def running_sum(g):
    lane = lax.broadcasted_iota(jnp.int32, g.shape, 1)
    step = 1
    while step < g.shape[1]:
        g = g + jnp.where(lane >= step, pltpu.roll(g, step, 1), 0.0)
        step *= 2
    return g


def columns(cum):
    wide = jnp.concatenate([cum, jnp.zeros((DIM - cum.shape[0], cum.shape[1]), cum.dtype)], 0)
    return wide.T


def local_state_kernel(k_ref, v_ref, g_ref, msg_ref):
    cum = running_sum(g_ref[...])
    cum_t = columns(cum)
    row = lax.broadcasted_iota(jnp.int32, (16, DIM), 0)
    for h in range(HEADS):
        cols = slice(h * DIM, (h + 1) * DIM)
        last = cum[h : h + 1, CH - 1 : CH]
        scale = jnp.exp(last - cum_t[:, h : h + 1])
        ks = (k_ref[:, cols].astype(jnp.float32) * scale).astype(jnp.bfloat16)
        local = dot(ks, v_ref[:, cols], TN).astype(jnp.bfloat16)
        total = jnp.broadcast_to(last, (16, DIM))
        hi = total.astype(jnp.bfloat16).astype(jnp.float32)
        extra = jnp.where(row == 0, hi, jnp.where(row == 1, total - hi, 0.0)).astype(jnp.bfloat16)
        for piece in range(4):
            msg_ref[h * 4 + piece, 0:32, :] = local[piece * 32 : (piece + 1) * 32]
            msg_ref[h * 4 + piece, 32:48, :] = extra


def scan_kernel(msg_ref, out_ref):
    state = jnp.zeros((32, DIM), jnp.float32)
    for j in range(msg_ref.shape[0]):
        out_ref[j] = state.astype(jnp.bfloat16)
        extra = msg_ref[j, 32:48, :].astype(jnp.float32)
        decay = jnp.exp(extra[0:1] + extra[1:2])
        state = decay * state + msg_ref[j, 0:32, :].astype(jnp.float32)


def lightning_kernel(q_ref, k_ref, v_ref, g_ref, gain_ref, state_ref, out_ref):
    cum = running_sum(g_ref[...])
    cum_t = columns(cum)
    causal = lax.broadcasted_iota(jnp.int32, (CH, CH), 0) >= lax.broadcasted_iota(
        jnp.int32, (CH, CH), 1
    )
    for h in range(HEADS):
        cols = slice(h * DIM, (h + 1) * DIM)
        q, k, v = q_ref[:, cols], k_ref[:, cols], v_ref[:, cols]
        col = cum_t[:, h : h + 1]
        diff = jnp.minimum(col - cum[h : h + 1, :], 0.0)
        weight = jnp.where(causal, jnp.exp(diff), 0.0)
        probs = (dot(q, k, NT) * weight).astype(jnp.bfloat16)
        mix = dot(probs, v, NN) + jnp.exp(col) * dot(q, state_ref[h], NN)
        norm = lax.rsqrt(jnp.mean(mix * mix, axis=1, keepdims=True) + 1e-05)
        out_ref[:, cols] = (mix * norm * gain_ref[:, cols]).astype(jnp.bfloat16)


ROWS = HEADS * 64
SUB = 128
KEYS = 1024


def softmax_kernel(*refs):
    q_ref = refs[0]
    pieces = refs[1:11]
    out_ref, kv_ref, qq_ref, m_ref, acc_ref, sems = refs[11:]
    mx, my, mc = (lax.axis_index(a) for a in CTX)

    copies = []
    for other in range(2):
        row, plus, minus, far_a, far_b = pieces[5 * other : 5 * other + 5]
        core = mc if other == 0 else 1 - mc
        for ds, source in ((0, row), (1, plus), (3, minus), (2, None)):
            for slot, df in enumerate((0, 1, 3, 2)):
                ref = source
                at = slot
                if source is None:
                    ref, at = (far_a, slot) if slot < 2 else (far_b, slot - 2)
                dx = jnp.where(core == 0, df, ds)
                dy = jnp.where(core == 0, ds, df)
                chunk = ((mx + NX - dx) % NX * NY + (my + NY - dy) % NY) * NC + core
                n = len(copies)
                copy = pltpu.make_async_copy(
                    ref.at[pl.ds(at * CH, CH), :],
                    kv_ref.at[pl.ds(pl.multiple_of(chunk * CH, CH), CH), :],
                    sems.at[n],
                )
                copy.start()
                copies.append(copy)

    scale = math.log2(math.e) / math.sqrt(DIM)
    for x in range(NX):
        for g in range(HEADS):
            q = q_ref[x * 64 : (x + 1) * 64, g * DIM : (g + 1) * DIM].astype(jnp.float32) * scale
            high = q.astype(jnp.bfloat16)
            low = (q - high.astype(jnp.float32)).astype(jnp.bfloat16)
            rows = slice(x * ROWS + g * 64, x * ROWS + (g + 1) * 64)
            qq_ref[rows, 0:DIM] = high
            qq_ref[rows, DIM : 2 * DIM] = low
    for copy in copies:
        copy.wait()

    yc = my * NC + mc

    def step(x, start, masked, first):
        keys = kv_ref[pl.ds(pl.multiple_of(start, KEYS), KEYS), 0:DIM]
        values = kv_ref[pl.ds(pl.multiple_of(start, KEYS), KEYS), DIM : 2 * DIM]
        keys2 = jnp.concatenate([keys, keys], axis=1)
        values2 = jnp.concatenate([values, jnp.ones_like(values)], axis=1)
        for sub in range(ROWS // SUB):
            rows = slice(sub * SUB, (sub + 1) * SUB)
            qq = qq_ref[pl.ds(pl.multiple_of(x * ROWS + sub * SUB, SUB), SUB), :]
            s = dot(qq, keys2, NT)
            if masked:
                r = lax.broadcasted_iota(jnp.int32, (SUB, 1), 0) % 64
                pos = (x * 8 + yc) * CH + (r // 8) * 32 + mx * 8 + r % 8 - start
                s = jnp.where(lax.broadcasted_iota(jnp.int32, s.shape, 1) <= pos, s, -1e30)
            peak = jnp.max(s, axis=1, keepdims=True)
            if first:
                p = jnp.exp2(s - peak).astype(jnp.bfloat16)
                acc_ref[rows, :] = dot(p, values2, NN)
                m_ref[rows, :] = jnp.broadcast_to(peak, (SUB, DIM))
            else:
                old = m_ref[rows, 0:1]
                new = jnp.maximum(old, peak)
                p = jnp.exp2(s - new).astype(jnp.bfloat16)
                alpha = jnp.exp2(old - new)
                acc_ref[rows, :] = acc_ref[rows, :] * alpha + dot(p, values2, NN)
                m_ref[rows, :] = jnp.broadcast_to(new, (SUB, DIM))

    @pl.loop(0, NX)
    def _(x):
        step(x, x * 2048, True, True)
        step(x, x * 2048 + KEYS, True, False)

        @pl.loop(0, x * (2048 // KEYS))
        def _(i):
            step(x, i * KEYS, False, False)

        for g in range(HEADS):
            rows = slice(g * 64, (g + 1) * 64)
            o = acc_ref[rows, 0:DIM] / acc_ref[rows, DIM : 2 * DIM]
            out_ref[pl.ds(pl.multiple_of(x * 64, 64), 64), g * DIM : (g + 1) * DIM] = o.astype(
                jnp.bfloat16
            )


def vmem(n):
    return [pl.BlockSpec(memory_space=pltpu.VMEM)] * n


def call(kernel, shape, dtype, n, name, flops, **kw):
    return pl.pallas_call(
        kernel,
        out_shape=jax.ShapeDtypeStruct(shape, dtype),
        in_specs=kw.pop("in_specs", vmem(n)),
        out_specs=pl.BlockSpec(memory_space=pltpu.VMEM),
        compiler_params=pltpu.CompilerParams(vmem_limit_bytes=kw.pop("limit", 32 << 20)),
        cost_estimate=pl.CostEstimate(flops=flops, bytes_accessed=2 << 20, transcendentals=0),
        name=name,
        **kw,
    )


def ctx_index(x, y, c):
    return (x % NX * NY + y % NY) * NC + c


def ring(first, sign):
    pairs = []
    for x in range(NX):
        for y in range(NY):
            for c in range(NC):
                along_x = (c == 0) == first
                to = (x + sign, y) if along_x else (x, y + sign)
                pairs.append((ctx_index(x, y, c), ctx_index(*to, c)))
    return pairs


def gather_kv(own):
    half = CH // 2
    r1 = lax.ppermute(own, CTX, ring(True, 1))
    r2 = lax.ppermute(own, CTX, ring(True, -1))
    h1 = lax.ppermute(r1[:half], CTX, ring(True, 1))
    h2 = lax.ppermute(r2[half:], CTX, ring(True, -1))
    row = jnp.concatenate([own, r1, r2, h1, h2], axis=0)
    s1 = lax.ppermute(row, CTX, ring(False, 1))
    s2 = lax.ppermute(row, CTX, ring(False, -1))
    t1 = lax.ppermute(s1[: 2 * CH], CTX, ring(False, 1))
    t2 = lax.ppermute(s2[2 * CH :], CTX, ring(False, -1))
    mine = [row, s1, s2, t1, t2]
    return mine + [lax.ppermute(p, "ctx_2", [(0, 1), (1, 0)]) for p in mine]


def body(lin_q, lin_k, lin_v, log_decay, lin_gain, soft_q, soft_kv):
    kv = lax.all_to_all(
        soft_kv.reshape(32, NZ, 2 * DIM).swapaxes(0, 1), "head", 0, 0, tiled=True
    ).reshape(CH, 2 * DIM)
    q = soft_q.reshape(NX, 8, NZ, HEADS * DIM).swapaxes(1, 2).reshape(NX * NZ, 8, HEADS * DIM)
    q = lax.all_to_all(q, ("ctx_0", "head"), 0, 0, tiled=True).reshape(CH, HEADS * DIM)

    msg = call(local_state_kernel, (32, MSG, DIM), jnp.bfloat16, 3, "local_state", 1 << 28)(
        lin_k, lin_v, log_decay
    )
    msg = lax.all_to_all(msg, CTX, 0, 0, tiled=True)
    state = call(scan_kernel, (32, 32, DIM), jnp.bfloat16, 1, "scan_state", 1 << 20)(msg)
    state = lax.all_to_all(state, CTX, 0, 0, tiled=True).reshape(HEADS, DIM, DIM)

    pieces = gather_kv(kv)
    soft = call(
        softmax_kernel,
        (CH, HEADS * DIM),
        jnp.bfloat16,
        11,
        "softmax",
        1 << 34,
        in_specs=vmem(1) + [pl.BlockSpec(memory_space=pl.ANY)] * 10,
        scratch_shapes=[
            pltpu.VMEM((NX * NY * NC * CH, 2 * DIM), jnp.bfloat16),
            pltpu.VMEM((NX * ROWS, 2 * DIM), jnp.bfloat16),
            pltpu.VMEM((ROWS, DIM), jnp.float32),
            pltpu.VMEM((ROWS, 2 * DIM), jnp.float32),
            pltpu.SemaphoreType.DMA((32,)),
        ],
    )(q, *pieces)
    soft = lax.all_to_all(
        soft.reshape(NX * NZ, 8, HEADS * DIM), ("ctx_0", "head"), 0, 0, tiled=True
    )
    soft_out = soft.reshape(NX, NZ, 8, HEADS * DIM).swapaxes(1, 2).reshape(32, NZ * HEADS * DIM)

    lin_out = call(lightning_kernel, (CH, HEADS * DIM), jnp.bfloat16, 6, "lightning", 1 << 29)(
        lin_q, lin_k, lin_v, log_decay, lin_gain.reshape(1, -1), state
    )
    return (lin_out, soft_out)


def solution(mesh):
    finer = Mesh(
        mesh.devices.reshape(NX, NY, NC, NZ), ("ctx_0", "ctx_1", "ctx_2", "head")
    )
    placed = (
        P(CTX, "head"),
        P(CTX, "head"),
        P(CTX, "head"),
        P("head", CTX),
        P("head"),
        P(CTX_HEAD, None),
        P(CTX_HEAD, None),
    )
    return jax.shard_map(
        body,
        mesh=finer,
        in_specs=placed,
        out_specs=(P(CTX, "head"), P(CTX_HEAD, None)),
        check_vma=False,
    )
```

time: 222 us -> 142 us (0.64)
  the two profiles are of different devices: /device:TPU:31 before, /device:TPU:32 now
where the time goes in v1:
time: 142 us; the launch traced here: 141 us
  Pallas kernels  51.6 us (36%)
  starting transfers between devices  36.7 us (26%)
  waiting for transfers between devices  32.6 us (23%)
  blocking collectives  15.8 us (11%)
  local copies, waits for them, and re-layouts  3.62 us (3%)
    pallas_call x1, Pallas kernels, body(): call(softmax_kernel, (CH, HEADS * DIM), jnp.bfloat16, 11, 'softmax', 1 <<...  45.8 us
    all_to_all x1, blocking collectives, body(): lax.all_to_all(soft_kv.reshape(32, NZ, 2 * DIM).swapaxes(0, 1), 'head', 0...  15.8 us
    all_to_all x1, waiting for transfers between devices, body(): lax.all_to_all(soft.reshape(NX * NZ, 8, HEADS * DIM), ('ctx_0', 'head'),...  15.3 us
    all_to_all x1, starting transfers between devices, body(): lax.all_to_all(soft.reshape(NX * NZ, 8, HEADS * DIM), ('ctx_0', 'head'),...  6.74 us
    all_to_all x1, starting transfers between devices, body(): msg = lax.all_to_all(msg, CTX, 0, 0, tiled=True)  6.11 us
    all_to_all x1, waiting for transfers between devices, body(): lax.all_to_all(q, ('ctx_0', 'head'), 0, 0, tiled=True)  6.1 us
    ppermute x1, waiting for transfers between devices, gather_kv(): h1 = lax.ppermute(r1[:half], CTX, ring(True, 1))  5.55 us
    all_to_all x1, starting transfers between devices, body(): lax.all_to_all(q, ('ctx_0', 'head'), 0, 0, tiled=True)  5.2 us
  transfers between devices with their start and end apart: 17, of which 5 were waited for; matrix products, arithmetic and copies ran while one was open for 0% of the time, Pallas kernels for 37%

profile of v1, /device:TPU:32, one launch (start us, length us, event | category | flops | bytes accessed | tf_op | source)
XLA Modules:
  0.0 141.2 jit_solution(3799292217820601303)
XLA Ops:
  0.6 1.0 copy.12
  1.6 15.8 %all_to_all.25 = bf16[8,32,256]{2,1,0:T(8,128)(2,1)S(1)} all-to-all(bf16[8,32,256]{2,1,0:T(8,128)(2,1)S(1)} %bitcast.29), channel_id=1, replica_groups=mesh['ctx_0'=4,'ctx_1'=4,'ctx_2'=2,'head'=8] {'head'}, dimensions={0} | all-to-all | bytes 262144 | tf_op jit(solution)/shard_map/all_to_all | solution.py:226
  17.4 1.5 %collective-permute-start = (bf16[256,256]{1,0:T(8,128)(2,1)S(1)}, bf16[256,256]{1,0:T(8,128)(2,1)S(1)}, u32[]{:S(2)}, u32[]{:S(2)}) collective-permute-start(bf16[256,256]{1,0:T(8,128)(2,1)S(1)} %bitcast.26), channel_id=1, source_target_pairs={{0,64},{8,24},{16,80},{24,40},{32,96},{40,56},{48,112},{56,8},{64,... | collective-permute-start | bytes 393224 | tf_op jit(solution)/shard_map/ppermute | solution.py:212
  18.9 1.7 %collective-permute-start.1 = (bf16[256,256]{1,0:T(8,128)(2,1)S(1)}, bf16[256,256]{1,0:T(8,128)(2,1)S(1)}, u32[]{:S(2)}, u32[]{:S(2)}) collective-permute-start(bf16[256,256]{1,0:T(8,128)(2,1)S(1)} %bitcast.27), channel_id=1, source_target_pairs={{0,192},{8,56},{16,208},{24,8},{32,224},{40,24},{48,240},{56,40},{... | collective-permute-start | bytes 393224 | tf_op jit(solution)/shard_map/ppermute | solution.py:213
  20.7 1.0 copy-done.1
  22.4 2.4 %local_state.1 = bf16[32,48,128]{2,1,0:T(8,128)(2,1)} custom-call(bf16[256,1024]{1,0:T(8,128)(2,1)S(1)} %copy-done, bf16[256,1024]{1,0:T(8,128)(2,1)S(1)} %copy-done.1, f32[8,256]{1,0:T(8,128)S(1)} %copy-done.4), custom_call_target="tpu_custom_call" | custom-call | flops 268435456 | bytes 2097152 | tf_op jit(solution)/shard_map/local_state/pallas_call | solution.py:232
  24.8 6.1 %all-to-all-start = ((bf16[32,48,128]{2,1,0:T(8,128)(2,1)}), bf16[32,48,128]{2,1,0:T(8,128)(2,1)S(1)}, u32[]{:S(2)}, u32[]{:S(2)}) async-start(bf16[32,48,128]{2,1,0:T(8,128)(2,1)} %local_state.1), calls=%async_computation | async-start | bytes 786432 | tf_op jit(solution)/shard_map/all_to_all | solution.py:235
  30.9 1.9 %collective-permute-start.2 = (bf16[128,256]{1,0:T(8,128)(2,1)S(1)}, bf16[128,256]{1,0:T(8,128)(2,1)S(1)}, u32[]{:S(2)}, u32[]{:S(2)}) collective-permute-start(bf16[128,256]{1,0:T(8,128)(2,1)S(1)} %slice.16), channel_id=1, source_target_pairs={{0,64},{8,24},{16,80},{24,40},{32,96},{40,56},{48,112},{56,8},{64,... | collective-permute-start | bytes 196616 | tf_op jit(solution)/shard_map/ppermute | solution.py:214
  32.8 1.5 %collective-permute-start.3 = (bf16[128,256]{1,0:T(8,128)(2,1)S(1)}, bf16[128,256]{1,0:T(8,128)(2,1)S(1)}, u32[]{:S(2)}, u32[]{:S(2)}) collective-permute-start(bf16[128,256]{1,0:T(8,128)(2,1)S(1)} %slice.17), channel_id=1, source_target_pairs={{0,192},{8,56},{16,208},{24,8},{32,224},{40,24},{48,240},{56,40},{... | collective-permute-start | bytes 196616 | tf_op jit(solution)/shard_map/ppermute | solution.py:215
  34.4 5.5 %collective-permute-done.2 = bf16[128,256]{1,0:T(8,128)(2,1)S(1)} collective-permute-done((bf16[128,256]{1,0:T(8,128)(2,1)S(1)}, bf16[128,256]{1,0:T(8,128)(2,1)S(1)}, u32[]{:S(2)}, u32[]{:S(2)}) %collective-permute-start.2) | collective-permute-done | bytes 65568 | tf_op jit(solution)/shard_map/ppermute | solution.py:214
  39.9 1.6 %collective-permute-start.4 = (bf16[1024,256]{1,0:T(8,128)(2,1)S(1)}, bf16[1024,256]{1,0:T(8,128)(2,1)S(1)}, u32[]{:S(2)}, u32[]{:S(2)}) collective-permute-start(bf16[1024,256]{1,0:T(8,128)(2,1)S(1)} %constant_dynamic-update-slice_fusion.refs_1_), channel_id=1, source_target_pairs={{0,16},{8,72},{16,32},{24,88},{32,48},{40,104},{48,0},{56,120},{64... | collective-permute-start | bytes 1572872 | tf_op jit(solution)/shard_map/ppermute | solution.py:217
  41.5 1.8 %collective-permute-start.5 = (bf16[1024,256]{1,0:T(8,128)(2,1)S(1)}, bf16[1024,256]{1,0:T(8,128)(2,1)S(1)}, u32[]{:S(2)}, u32[]{:S(2)}) collective-permute-start(bf16[1024,256]{1,0:T(8,128)(2,1)S(1)} %constant_dynamic-update-slice_fusion.refs_1_), channel_id=1, source_target_pairs={{0,48},{8,200},{16,0},{24,216},{32,16},{40,232},{48,32},{56,248},{... | collective-permute-start | bytes 1572872 | tf_op jit(solution)/shard_map/ppermute | solution.py:218
  43.3 5.2 %all-to-all-start.2 = ((bf16[32,8,1024]{2,1,0:T(8,128)(2,1)}), bf16[32,8,1024]{2,1,0:T(8,128)(2,1)S(1)}, u32[]{:S(2)}, u32[]{:S(2)}) async-start(bf16[32,8,1024]{2,1,0:T(8,128)(2,1)} %bitcast.4), calls=%async_computation.2 | async-start | bytes 1048576 | tf_op jit(solution)/shard_map/all_to_all | solution.py:230
  48.6 1.8 %collective-permute-done.4.refs_2_ = bf16[1024,256]{1,0:T(8,128)(2,1)S(1)} collective-permute-done((bf16[1024,256]{1,0:T(8,128)(2,1)S(1)}, bf16[1024,256]{1,0:T(8,128)(2,1)S(1)}, u32[]{:S(2)}, u32[]{:S(2)}) %collective-permute-start.4) | collective-permute-done | bytes 524320 | tf_op jit(solution)/shard_map/ppermute | solution.py:217
  50.8 3.0 %collective-permute-start.7 = (bf16[512,256]{1,0:T(8,128)(2,1)S(1)}, bf16[512,256]{1,0:T(8,128)(2,1)}, u32[]{:S(2)}, u32[]{:S(2)}) collective-permute-start(bf16[512,256]{1,0:T(8,128)(2,1)S(1)} %slice.19), channel_id=1, source_target_pairs={{0,48},{8,200},{16,0},{24,216},{32,16},{40,232},{48,32},{56,248},{... | collective-permute-start | bytes 786440 | tf_op jit(solution)/shard_map/ppermute | solution.py:220
  54.4 3.8 %collective-permute-done.6.refs_4_ = bf16[512,256]{1,0:T(8,128)(2,1)} collective-permute-done((bf16[512,256]{1,0:T(8,128)(2,1)S(1)}, bf16[512,256]{1,0:T(8,128)(2,1)}, u32[]{:S(2)}, u32[]{:S(2)}) %collective-permute-start.6) | collective-permute-done | bytes 262176 | tf_op jit(solution)/shard_map/ppermute | solution.py:219
  58.7 0.8 scan_state.1
  59.5 6.1 %all-to-all-done.2 = bf16[32,8,1024]{2,1,0:T(8,128)(2,1)S(1)} async-done(((bf16[32,8,1024]{2,1,0:T(8,128)(2,1)}), bf16[32,8,1024]{2,1,0:T(8,128)(2,1)S(1)}, u32[]{:S(2)}, u32[]{:S(2)}) %all-to-all-start.2) | async-done | bytes 524320 | tf_op jit(solution)/shard_map/all_to_all | solution.py:230
  65.6 4.2 %all-to-all-start.1 = ((bf16[32,32,128]{2,1,0:T(8,128)(2,1)}), bf16[32,32,128]{2,1,0:T(8,128)(2,1)S(1)}, u32[]{:S(2)}, u32[]{:S(2)}) async-start(bf16[32,32,128]{2,1,0:T(8,128)(2,1)} %scan_state.1), calls=%async_computation.1 | async-start | bytes 524288 | tf_op jit(solution)/shard_map/all_to_all | solution.py:237
  69.9 45.8 %softmax.1 = bf16[256,1024]{1,0:T(8,128)(2,1)} custom-call(bf16[256,1024]{1,0:T(8,128)(2,1)S(1)} %bitcast.23, bf16[1024,256]{1,0:T(8,128)(2,1)S(1)} %constant_dynamic-update-slice_fusion.refs_1_, bf16[1024,256]{1,0:T(8,128)(2,1)S(1)} %collective-permute-done.4.refs_2_, bf16[1024,256]{1,0:T(8,128)(2,1)S(1)} %collective-permute-done.5.refs_3_, ...), custom_call_target="tpu_custom_call" | custom-call | flops 17179869184 | bytes 2097152 | tf_op jit(solution)/shard_map/softmax/pallas_call | solution.py:240
  115.7 6.7 %all-to-all-start.4 = ((bf16[32,8,1024]{2,1,0:T(8,128)(2,1)}), bf16[32,8,1024]{2,1,0:T(8,128)(2,1)S(1)}, u32[]{:S(2)}, u32[]{:S(2)}) async-start(bf16[32,8,1024]{2,1,0:T(8,128)(2,1)} %bitcast.8), calls=%async_computation.4 | async-start | bytes 1048576 | tf_op jit(solution)/shard_map/all_to_all | solution.py:256
  122.5 2.6 %lightning.1 = bf16[256,1024]{1,0:T(8,128)(2,1)} custom-call(bf16[256,1024]{1,0:T(8,128)(2,1)S(1)} %copy-done.3, bf16[256,1024]{1,0:T(8,128)(2,1)S(1)} %copy-done, bf16[256,1024]{1,0:T(8,128)(2,1)S(1)} %copy-done.2, f32[8,256]{1,0:T(8,128)S(1)} %copy-done.5, f32[1,1024]{1,0:T(1,128)S(1)} %bitcast.24, bf16[8,128,128]{2,1,0:T(8,128)(2,1)S(1)} %bitcast.22), custom_call_target="tpu_custom_call" | custom-call | flops 536870912 | bytes 2097152 | tf_op jit(solution)/shard_map/lightning/pallas_call | solution.py:261
  125.1 15.3 %all-to-all-done.4 = bf16[32,8,1024]{2,1,0:T(8,128)(2,1)S(1)} async-done(((bf16[32,8,1024]{2,1,0:T(8,128)(2,1)}), bf16[32,8,1024]{2,1,0:T(8,128)(2,1)S(1)}, u32[]{:S(2)}, u32[]{:S(2)}) %all-to-all-start.4) | async-done | bytes 524320 | tf_op jit(solution)/shard_map/all_to_all | solution.py:256
  140.4 0.8 copy.18
  (40 shorter events, 2.3 us)
Async XLA Ops:
  0.6 20.0 %copy-start = (bf16[256,1024]{1,0:T(8,128)(2,1)S(1)}, bf16[256,1024]{1,0:T(8,128)(2,1)}, u32[]{:S(2)}) copy-start(bf16[256,1024]{1,0:T(8,128)(2,1)} %k_ref.3) | copy-start | bytes 1572868
  17.4 13.5 %collective-permute-start = (bf16[256,256]{1,0:T(8,128)(2,1)S(1)}, bf16[256,256]{1,0:T(8,128)(2,1)S(1)}, u32[]{:S(2)}, u32[]{:S(2)}) collective-permute-start(bf16[256,256]{1,0:T(8,128)(2,1)S(1)} %bitcast.26), channel_id=1, source_target_pairs={{0,64},{8,24},{16,80},{24,40},{32,96},{40,56},{48,112},{56,8},{64,... | collective-permute-start | bytes 393224 | tf_op jit(solution)/shard_map/ppermute | solution.py:212
  18.9 13.9 %collective-permute-start.1 = (bf16[256,256]{1,0:T(8,128)(2,1)S(1)}, bf16[256,256]{1,0:T(8,128)(2,1)S(1)}, u32[]{:S(2)}, u32[]{:S(2)}) collective-permute-start(bf16[256,256]{1,0:T(8,128)(2,1)S(1)} %bitcast.27), channel_id=1, source_target_pairs={{0,192},{8,56},{16,208},{24,8},{32,224},{40,24},{48,240},{56,40},{... | collective-permute-start | bytes 393224 | tf_op jit(solution)/shard_map/ppermute | solution.py:213
  20.7 1.0 copy-start.1
  21.7 0.7 copy-start.4
  24.8 18.5 %all-to-all-start = ((bf16[32,48,128]{2,1,0:T(8,128)(2,1)}), bf16[32,48,128]{2,1,0:T(8,128)(2,1)S(1)}, u32[]{:S(2)}, u32[]{:S(2)}) async-start(bf16[32,48,128]{2,1,0:T(8,128)(2,1)} %local_state.1), calls=%async_computation | async-start | bytes 786432 | tf_op jit(solution)/shard_map/all_to_all | solution.py:235
  30.9 9.0 %collective-permute-start.2 = (bf16[128,256]{1,0:T(8,128)(2,1)S(1)}, bf16[128,256]{1,0:T(8,128)(2,1)S(1)}, u32[]{:S(2)}, u32[]{:S(2)}) collective-permute-start(bf16[128,256]{1,0:T(8,128)(2,1)S(1)} %slice.16), channel_id=1, source_target_pairs={{0,64},{8,24},{16,80},{24,40},{32,96},{40,56},{48,112},{56,8},{64,... | collective-permute-start | bytes 196616 | tf_op jit(solution)/shard_map/ppermute | solution.py:214
  32.8 7.1 %collective-permute-start.3 = (bf16[128,256]{1,0:T(8,128)(2,1)S(1)}, bf16[128,256]{1,0:T(8,128)(2,1)S(1)}, u32[]{:S(2)}, u32[]{:S(2)}) collective-permute-start(bf16[128,256]{1,0:T(8,128)(2,1)S(1)} %slice.17), channel_id=1, source_target_pairs={{0,192},{8,56},{16,208},{24,8},{32,224},{40,24},{48,240},{56,40},{... | collective-permute-start | bytes 196616 | tf_op jit(solution)/shard_map/ppermute | solution.py:215
  39.9 10.5 %collective-permute-start.4 = (bf16[1024,256]{1,0:T(8,128)(2,1)S(1)}, bf16[1024,256]{1,0:T(8,128)(2,1)S(1)}, u32[]{:S(2)}, u32[]{:S(2)}) collective-permute-start(bf16[1024,256]{1,0:T(8,128)(2,1)S(1)} %constant_dynamic-update-slice_fusion.refs_1_), channel_id=1, source_target_pairs={{0,16},{8,72},{16,32},{24,88},{32,48},{40,104},{48,0},{56,120},{64... | collective-permute-start | bytes 1572872 | tf_op jit(solution)/shard_map/ppermute | solution.py:217
  41.5 9.3 %collective-permute-start.5 = (bf16[1024,256]{1,0:T(8,128)(2,1)S(1)}, bf16[1024,256]{1,0:T(8,128)(2,1)S(1)}, u32[]{:S(2)}, u32[]{:S(2)}) collective-permute-start(bf16[1024,256]{1,0:T(8,128)(2,1)S(1)} %constant_dynamic-update-slice_fusion.refs_1_), channel_id=1, source_target_pairs={{0,48},{8,200},{16,0},{24,216},{32,16},{40,232},{48,32},{56,248},{... | collective-permute-start | bytes 1572872 | tf_op jit(solution)/shard_map/ppermute | solution.py:218
  43.3 22.4 %all-to-all-start.2 = ((bf16[32,8,1024]{2,1,0:T(8,128)(2,1)}), bf16[32,8,1024]{2,1,0:T(8,128)(2,1)S(1)}, u32[]{:S(2)}, u32[]{:S(2)}) async-start(bf16[32,8,1024]{2,1,0:T(8,128)(2,1)} %bitcast.4), calls=%async_computation.2 | async-start | bytes 1048576 | tf_op jit(solution)/shard_map/all_to_all | solution.py:230
  48.5 21.3 %collective-permute-start.8 = (bf16[1024,256]{1,0:T(8,128)(2,1)S(1)}, bf16[1024,256]{1,0:T(8,128)(2,1)}, u32[]{:S(2)}, u32[]{:S(2)}) collective-permute-start(bf16[1024,256]{1,0:T(8,128)(2,1)S(1)} %constant_dynamic-update-slice_fusion.refs_1_), channel_id=1, source_target_pairs={{0,8},{8,0},{1,9},{9,1},{2,10},{10,2},{3,11},{11,3},{4,12},{12,4},... | collective-permute-start | bytes 1572872 | tf_op jit(solution)/shard_map/ppermute | solution.py:222
  50.4 7.8 %collective-permute-start.6 = (bf16[512,256]{1,0:T(8,128)(2,1)S(1)}, bf16[512,256]{1,0:T(8,128)(2,1)}, u32[]{:S(2)}, u32[]{:S(2)}) collective-permute-start(bf16[512,256]{1,0:T(8,128)(2,1)S(1)} %slice.18), channel_id=1, source_target_pairs={{0,16},{8,72},{16,32},{24,88},{32,48},{40,104},{48,0},{56,120},{64... | collective-permute-start | bytes 786440 | tf_op jit(solution)/shard_map/ppermute | solution.py:219
  50.8 7.8 %collective-permute-start.7 = (bf16[512,256]{1,0:T(8,128)(2,1)S(1)}, bf16[512,256]{1,0:T(8,128)(2,1)}, u32[]{:S(2)}, u32[]{:S(2)}) collective-permute-start(bf16[512,256]{1,0:T(8,128)(2,1)S(1)} %slice.19), channel_id=1, source_target_pairs={{0,48},{8,200},{16,0},{24,216},{32,16},{40,232},{48,32},{56,248},{... | collective-permute-start | bytes 786440 | tf_op jit(solution)/shard_map/ppermute | solution.py:220
  53.8 16.0 %collective-permute-start.10 = (bf16[1024,256]{1,0:T(8,128)(2,1)S(1)}, bf16[1024,256]{1,0:T(8,128)(2,1)}, u32[]{:S(2)}, u32[]{:S(2)}) collective-permute-start(bf16[1024,256]{1,0:T(8,128)(2,1)S(1)} %collective-permute-done.5.refs_3_), channel_id=1, source_target_pairs={{0,8},{8,0},{1,9},{9,1},{2,10},{10,2},{3,11},{11,3},{4,12},{12,4},... | collective-permute-start | bytes 1572872 | tf_op jit(solution)/shard_map/ppermute | solution.py:222
  53.8 16.0 %collective-permute-start.9 = (bf16[1024,256]{1,0:T(8,128)(2,1)S(1)}, bf16[1024,256]{1,0:T(8,128)(2,1)}, u32[]{:S(2)}, u32[]{:S(2)}) collective-permute-start(bf16[1024,256]{1,0:T(8,128)(2,1)S(1)} %collective-permute-done.4.refs_2_), channel_id=1, source_target_pairs={{0,8},{8,0},{1,9},{9,1},{2,10},{10,2},{3,11},{11,3},{4,12},{12,4},... | collective-permute-start | bytes 1572872 | tf_op jit(solution)/shard_map/ppermute | solution.py:222
  58.2 11.6 %collective-permute-start.11 = (bf16[512,256]{1,0:T(8,128)(2,1)}, bf16[512,256]{1,0:T(8,128)(2,1)}, u32[]{:S(2)}, u32[]{:S(2)}) collective-permute-start(bf16[512,256]{1,0:T(8,128)(2,1)} %collective-permute-done.6.refs_4_), channel_id=1, source_target_pairs={{0,8},{8,0},{1,9},{9,1},{2,10},{10,2},{3,11},{11,3},{4,12},{12,4},... | collective-permute-start | bytes 786440 | tf_op jit(solution)/shard_map/ppermute | solution.py:222
  58.6 11.2 %collective-permute-start.12 = (bf16[512,256]{1,0:T(8,128)(2,1)}, bf16[512,256]{1,0:T(8,128)(2,1)}, u32[]{:S(2)}, u32[]{:S(2)}) collective-permute-start(bf16[512,256]{1,0:T(8,128)(2,1)} %collective-permute-done.7.refs_5_), channel_id=1, source_target_pairs={{0,8},{8,0},{1,9},{9,1},{2,10},{10,2},{3,11},{11,3},{4,12},{12,4},... | collective-permute-start | bytes 786440 | tf_op jit(solution)/shard_map/ppermute | solution.py:222
  65.6 50.1 %all-to-all-start.1 = ((bf16[32,32,128]{2,1,0:T(8,128)(2,1)}), bf16[32,32,128]{2,1,0:T(8,128)(2,1)S(1)}, u32[]{:S(2)}, u32[]{:S(2)}) async-start(bf16[32,32,128]{2,1,0:T(8,128)(2,1)} %scan_state.1), calls=%async_computation.1 | async-start | bytes 524288 | tf_op jit(solution)/shard_map/all_to_all | solution.py:237
  69.8 52.7 %copy-start.5 = (f32[8,256]{1,0:T(8,128)S(1)}, f32[8,256]{1,0:T(8,128)}, u32[]{:S(2)}) copy-start(f32[8,256]{1,0:T(8,128)} %g_ref.3) | copy-start | bytes 24580
  69.9 52.6 %copy-start.6 = (f32[1024]{0:T(1024)S(1)}, f32[1024]{0:T(1024)}, u32[]{:S(2)}) copy-start(f32[1024]{0:T(1024)} %param.11) | copy-start | bytes 12292
  115.7 6.8 %copy-start.2 = (bf16[256,1024]{1,0:T(8,128)(2,1)S(1)}, bf16[256,1024]{1,0:T(8,128)(2,1)}, u32[]{:S(2)}) copy-start(bf16[256,1024]{1,0:T(8,128)(2,1)} %v_ref.3) | copy-start | bytes 1572868
  115.7 6.8 %copy-start.3 = (bf16[256,1024]{1,0:T(8,128)(2,1)S(1)}, bf16[256,1024]{1,0:T(8,128)(2,1)}, u32[]{:S(2)}) copy-start(bf16[256,1024]{1,0:T(8,128)(2,1)} %q_ref.1) | copy-start | bytes 1572868
  115.7 24.7 %all-to-all-start.4 = ((bf16[32,8,1024]{2,1,0:T(8,128)(2,1)}), bf16[32,8,1024]{2,1,0:T(8,128)(2,1)S(1)}, u32[]{:S(2)}, u32[]{:S(2)}) async-start(bf16[32,8,1024]{2,1,0:T(8,128)(2,1)} %bitcast.8), calls=%async_computation.4 | async-start | bytes 1048576 | tf_op jit(solution)/shard_map/all_to_all | solution.py:256

commit v2 on v1

--- a/solution.py
+++ b/solution.py
@@ -1,4 +1,3 @@
-import functools
 import math
 
 import jax
@@ -86,15 +85,16 @@
 
 
 ROWS = HEADS * 64
-SUB = 128
-KEYS = 1024
+KEYS = NY * NC * CH
+SCALE = math.log2(math.e) / math.sqrt(DIM)
 
 
 def softmax_kernel(*refs):
     q_ref = refs[0]
     pieces = refs[1:11]
-    out_ref, kv_ref, qq_ref, m_ref, acc_ref, sems = refs[11:]
+    out_ref, kv_ref, qq_ref, s_ref, p_ref, pm_ref, al_ref, m_ref, acc_ref, sems = refs[11:]
     mx, my, mc = (lax.axis_index(a) for a in CTX)
+    yc = my * NC + mc
 
     copies = []
     for other in range(2):
@@ -118,68 +118,96 @@
                 copy.start()
                 copies.append(copy)
 
-    scale = math.log2(math.e) / math.sqrt(DIM)
     for x in range(NX):
         for g in range(HEADS):
-            q = q_ref[x * 64 : (x + 1) * 64, g * DIM : (g + 1) * DIM].astype(jnp.float32) * scale
-            high = q.astype(jnp.bfloat16)
-            low = (q - high.astype(jnp.float32)).astype(jnp.bfloat16)
             rows = slice(x * ROWS + g * 64, x * ROWS + (g + 1) * 64)
-            qq_ref[rows, 0:DIM] = high
-            qq_ref[rows, DIM : 2 * DIM] = low
+            qq_ref[rows, :] = q_ref[x * 64 : (x + 1) * 64, g * DIM : (g + 1) * DIM]
+    acc_ref[...] = jnp.zeros_like(acc_ref)
     for copy in copies:
         copy.wait()
 
-    yc = my * NC + mc
-
-    def step(x, start, masked, first):
-        keys = kv_ref[pl.ds(pl.multiple_of(start, KEYS), KEYS), 0:DIM]
+    tiles = NX * (NX + 1) // 2
+
+    def tile(t):
+        t = jnp.int32(t)
+        x = sum((t >= n).astype(jnp.int32) for n in (1, 3, 6))
+        u = t - x * (x + 1) // 2
+        return x, u, jnp.where(u == 0, x, u - 1) * KEYS, t % 2
+
+    def scores(t):
+        x, _, start, slot = tile(t)
+        r = lax.broadcasted_iota(jnp.int32, (ROWS, 1), 0) % 64
+        pos = (x * 8 + yc) * CH + (r // 8) * 32 + mx * 8 + r % 8 - start
+        qq = qq_ref[pl.ds(pl.multiple_of(x * ROWS, ROWS), ROWS), :]
+        for k in range(KEYS // 256):
+            keys = kv_ref[pl.ds(pl.multiple_of(start + k * 256, 256), 256), 0:DIM]
+            s = dot(qq, keys, NT) * SCALE
+            lane = lax.broadcasted_iota(jnp.int32, s.shape, 1)
+            s = jnp.where(lane <= pos - k * 256, s, -1e30)
+            s_ref[slot, :, k * 256 : (k + 1) * 256] = s
+            peak = jnp.maximum(s[:, :DIM], s[:, DIM:])
+            if k > 0:
+                peak = jnp.maximum(peak, pm_ref[slot])
+            if k == KEYS // 256 - 1:
+                peak = jnp.broadcast_to(jnp.max(peak, axis=1, keepdims=True), (ROWS, DIM))
+            pm_ref[slot] = peak
+
+    def weights(t):
+        _, u, _, slot = tile(t)
+        for i in range(ROWS // 64):
+            rows = slice(i * 64, (i + 1) * 64)
+            old = jnp.where(u == 0, -1e30, m_ref[rows, :])
+            new = jnp.maximum(old, pm_ref[slot, rows, :])
+            al_ref[slot, rows, :] = jnp.exp2(old - new)
+            m_ref[rows, :] = new
+            for k in range(KEYS // DIM):
+                cols = slice(k * DIM, (k + 1) * DIM)
+                p_ref[slot, rows, cols] = jnp.exp2(s_ref[slot, rows, cols] - new).astype(
+                    jnp.bfloat16
+                )
+
+    def mix(t):
+        _, _, start, slot = tile(t)
         values = kv_ref[pl.ds(pl.multiple_of(start, KEYS), KEYS), DIM : 2 * DIM]
-        keys2 = jnp.concatenate([keys, keys], axis=1)
-        values2 = jnp.concatenate([values, jnp.ones_like(values)], axis=1)
-        for sub in range(ROWS // SUB):
-            rows = slice(sub * SUB, (sub + 1) * SUB)
-            qq = qq_ref[pl.ds(pl.multiple_of(x * ROWS + sub * SUB, SUB), SUB), :]
-            s = dot(qq, keys2, NT)
-            if masked:
-                r = lax.broadcasted_iota(jnp.int32, (SUB, 1), 0) % 64
-                pos = (x * 8 + yc) * CH + (r // 8) * 32 + mx * 8 + r % 8 - start
-                s = jnp.where(lax.broadcasted_iota(jnp.int32, s.shape, 1) <= pos, s, -1e30)
-            peak = jnp.max(s, axis=1, keepdims=True)
-            if first:
-                p = jnp.exp2(s - peak).astype(jnp.bfloat16)
-                acc_ref[rows, :] = dot(p, values2, NN)
-                m_ref[rows, :] = jnp.broadcast_to(peak, (SUB, DIM))
-            else:
-                old = m_ref[rows, 0:1]
-                new = jnp.maximum(old, peak)
-                p = jnp.exp2(s - new).astype(jnp.bfloat16)
-                alpha = jnp.exp2(old - new)
-                acc_ref[rows, :] = acc_ref[rows, :] * alpha + dot(p, values2, NN)
-                m_ref[rows, :] = jnp.broadcast_to(new, (SUB, DIM))
-
-    @pl.loop(0, NX)
-    def _(x):
-        step(x, x * 2048, True, True)
-        step(x, x * 2048 + KEYS, True, False)
-
-        @pl.loop(0, x * (2048 // KEYS))
-        def _(i):
-            step(x, i * KEYS, False, False)
-
-        for g in range(HEADS):
-            rows = slice(g * 64, (g + 1) * 64)
-            o = acc_ref[rows, 0:DIM] / acc_ref[rows, DIM : 2 * DIM]
-            out_ref[pl.ds(pl.multiple_of(x * 64, 64), 64), g * DIM : (g + 1) * DIM] = o.astype(
-                jnp.bfloat16
-            )
+        values = jnp.concatenate([values, jnp.ones_like(values)], axis=1)
+        alpha = al_ref[slot]
+        alpha = jnp.concatenate([alpha, alpha], axis=1)
+        acc_ref[...] = acc_ref[...] * alpha + dot(p_ref[slot], values, NN)
+
+    def finish(t):
+        x, u, _, _ = tile(t)
+
+        @pl.when(u == x)
+        def _():
+            for g in range(HEADS):
+                rows = slice(g * 64, (g + 1) * 64)
+                o = acc_ref[rows, 0:DIM] / acc_ref[rows, DIM : 2 * DIM]
+                out_ref[pl.ds(pl.multiple_of(x * 64, 64), 64), g * DIM : (g + 1) * DIM] = o.astype(
+                    jnp.bfloat16
+                )
+
+    scores(0)
+    weights(0)
+    scores(1)
+
+    @pl.loop(0, tiles - 2)
+    def _(t):
+        mix(t)
+        scores(t + 2)
+        weights(t + 1)
+        finish(t)
+
+    mix(tiles - 2)
+    weights(tiles - 1)
+    mix(tiles - 1)
+    finish(tiles - 1)
 
 
 def vmem(n):
     return [pl.BlockSpec(memory_space=pltpu.VMEM)] * n
 
 
-def call(kernel, shape, dtype, n, name, flops, **kw):
+def call(kernel, shape, dtype, n, flops, **kw):
     return pl.pallas_call(
         kernel,
         out_shape=jax.ShapeDtypeStruct(shape, dtype),
@@ -187,7 +215,6 @@
         out_specs=pl.BlockSpec(memory_space=pltpu.VMEM),
         compiler_params=pltpu.CompilerParams(vmem_limit_bytes=kw.pop("limit", 32 << 20)),
         cost_estimate=pl.CostEstimate(flops=flops, bytes_accessed=2 << 20, transcendentals=0),
-        name=name,
         **kw,
     )
 
@@ -207,58 +234,66 @@
     return pairs
 
 
+def permute(value, pairs, axes=CTX):
+    return lax.ppermute(value, axes, pairs)
+
+
+def exchange(value, axes):
+    return lax.all_to_all(value, axes, 0, 0, tiled=True)
+
+
 def gather_kv(own):
-    half = CH // 2
-    r1 = lax.ppermute(own, CTX, ring(True, 1))
-    r2 = lax.ppermute(own, CTX, ring(True, -1))
-    h1 = lax.ppermute(r1[:half], CTX, ring(True, 1))
-    h2 = lax.ppermute(r2[half:], CTX, ring(True, -1))
-    row = jnp.concatenate([own, r1, r2, h1, h2], axis=0)
-    s1 = lax.ppermute(row, CTX, ring(False, 1))
-    s2 = lax.ppermute(row, CTX, ring(False, -1))
-    t1 = lax.ppermute(s1[: 2 * CH], CTX, ring(False, 1))
-    t2 = lax.ppermute(s2[2 * CH :], CTX, ring(False, -1))
+    r1 = permute(own, ring(True, 1))
+    r2 = permute(own, ring(True, -1))
+    r3 = permute(own, ring(True, 2))
+    row = jnp.concatenate([own, r1, r2, r3], axis=0)
+    s1 = permute(row, ring(False, 1))
+    s2 = permute(row, ring(False, -1))
+    t1 = permute(s1[: 2 * CH], ring(False, 1))
+    t2 = permute(s2[2 * CH :], ring(False, -1))
     mine = [row, s1, s2, t1, t2]
-    return mine + [lax.ppermute(p, "ctx_2", [(0, 1), (1, 0)]) for p in mine]
-
-
-def body(lin_q, lin_k, lin_v, log_decay, lin_gain, soft_q, soft_kv):
-    kv = lax.all_to_all(
-        soft_kv.reshape(32, NZ, 2 * DIM).swapaxes(0, 1), "head", 0, 0, tiled=True
-    ).reshape(CH, 2 * DIM)
+    swap = [(0, 1), (1, 0)]
+    return mine + [permute(p, swap, "ctx_2") for p in mine]
+
+
+def both(lin_q, lin_k, lin_v, log_decay, lin_gain, soft_q, soft_kv):
+    kv = soft_kv.reshape(32, NZ, 2 * DIM).swapaxes(0, 1)
+    kv = exchange(kv, "head").reshape(CH, 2 * DIM)
     q = soft_q.reshape(NX, 8, NZ, HEADS * DIM).swapaxes(1, 2).reshape(NX * NZ, 8, HEADS * DIM)
-    q = lax.all_to_all(q, ("ctx_0", "head"), 0, 0, tiled=True).reshape(CH, HEADS * DIM)
-
-    msg = call(local_state_kernel, (32, MSG, DIM), jnp.bfloat16, 3, "local_state", 1 << 28)(
+    q = exchange(q, ("ctx_0", "head")).reshape(CH, HEADS * DIM)
+    pieces = gather_kv(kv)
+
+    msg = call(local_state_kernel, (32, MSG, DIM), jnp.bfloat16, 3, 1 << 28)(
         lin_k, lin_v, log_decay
     )
-    msg = lax.all_to_all(msg, CTX, 0, 0, tiled=True)
-    state = call(scan_kernel, (32, 32, DIM), jnp.bfloat16, 1, "scan_state", 1 << 20)(msg)
-    state = lax.all_to_all(state, CTX, 0, 0, tiled=True).reshape(HEADS, DIM, DIM)
-
-    pieces = gather_kv(kv)
+    msg = exchange(msg, CTX)
+    state = call(scan_kernel, (32, 32, DIM), jnp.bfloat16, 1, 1 << 20)(msg)
+    state = exchange(state, CTX).reshape(HEADS, DIM, DIM)
+
     soft = call(
         softmax_kernel,
         (CH, HEADS * DIM),
         jnp.bfloat16,
         11,
-        "softmax",
         1 << 34,
         in_specs=vmem(1) + [pl.BlockSpec(memory_space=pl.ANY)] * 10,
+        limit=28 << 20,
         scratch_shapes=[
             pltpu.VMEM((NX * NY * NC * CH, 2 * DIM), jnp.bfloat16),
-            pltpu.VMEM((NX * ROWS, 2 * DIM), jnp.bfloat16),
+            pltpu.VMEM((NX * ROWS, DIM), jnp.bfloat16),
+            pltpu.VMEM((2, ROWS, KEYS), jnp.float32),
+            pltpu.VMEM((2, ROWS, KEYS), jnp.bfloat16),
+            pltpu.VMEM((2, ROWS, DIM), jnp.float32),
+            pltpu.VMEM((2, ROWS, DIM), jnp.float32),
             pltpu.VMEM((ROWS, DIM), jnp.float32),
             pltpu.VMEM((ROWS, 2 * DIM), jnp.float32),
             pltpu.SemaphoreType.DMA((32,)),
         ],
     )(q, *pieces)
-    soft = lax.all_to_all(
-        soft.reshape(NX * NZ, 8, HEADS * DIM), ("ctx_0", "head"), 0, 0, tiled=True
-    )
+    soft = exchange(soft.reshape(NX * NZ, 8, HEADS * DIM), ("ctx_0", "head"))
     soft_out = soft.reshape(NX, NZ, 8, HEADS * DIM).swapaxes(1, 2).reshape(32, NZ * HEADS * DIM)
 
-    lin_out = call(lightning_kernel, (CH, HEADS * DIM), jnp.bfloat16, 6, "lightning", 1 << 29)(
+    lin_out = call(lightning_kernel, (CH, HEADS * DIM), jnp.bfloat16, 6, 1 << 29)(
         lin_q, lin_k, lin_v, log_decay, lin_gain.reshape(1, -1), state
     )
     return (lin_out, soft_out)
@@ -278,7 +313,7 @@
         P(CTX_HEAD, None),
     )
     return jax.shard_map(
-        body,
+        both,
         mesh=finer,
         in_specs=placed,
         out_specs=(P(CTX, "head"), P(CTX_HEAD, None)),

time: 142 us -> 117 us (0.82)
  Pallas kernels: 51.6 us -> 29.5 us
  blocking collectives: 15.8 us -> 0 us
  starting transfers between devices: 36.7 us -> 45.2 us
  waiting for transfers between devices: 32.6 us -> 37 us
    pallas_call x4, Pallas kernels: 51.6 us -> 29.5 us  [the longest x1 23.7 us: both(): call(softmax_kernel, (CH, HEADS * DIM), jnp.bfloat16, 11, 1 << 34, in_spe...]
    all_to_all x1 -> x0, blocking collectives: 15.8 us -> none  [body(): lax.all_to_all(soft_kv.reshape(32, NZ, 2 * DIM).swapaxes(0, 1), 'head', 0...]
    all_to_all x4 -> x5, starting transfers between devices: 22.2 us -> 31.9 us  [exchange(): return lax.all_to_all(value, axes, 0, 0, tiled=True)]
    all_to_all x4 -> x5, waiting for transfers between devices: 21.4 us -> 25.3 us  [exchange(): return lax.all_to_all(value, axes, 0, 0, tiled=True)]
    ppermute x13 -> x12, starting transfers between devices: 14.4 us -> 13.2 us  [permute(): return lax.ppermute(value, axes, pairs)]
    ppermute x13 -> x12, waiting for transfers between devices: 11.3 us -> 11.7 us  [permute(): return lax.ppermute(value, axes, pairs)]
  transfers between devices with their start and end apart: 17 -> 17, of which waited for: 5 -> 7; matrix products, arithmetic and copies ran while one was open for 0% -> 0% of each run, Pallas kernels for 37% -> 25%
where the time goes in v2:
time: 117 us
  starting transfers between devices  45.2 us (39%)
  waiting for transfers between devices  37 us (32%)
  Pallas kernels  29.5 us (25%)
  local copies, waits for them, and re-layouts  4.22 us (4%)
    all_to_all x5, starting transfers between devices, exchange(): return lax.all_to_all(value, axes, 0, 0, tiled=True)  31.9 us
    all_to_all x5, waiting for transfers between devices, exchange(): return lax.all_to_all(value, axes, 0, 0, tiled=True)  25.3 us
    pallas_call x1, Pallas kernels, both(): call(softmax_kernel, (CH, HEADS * DIM), jnp.bfloat16, 11, 1 << 34, in_spe...  23.7 us
    ppermute x12, starting transfers between devices, permute(): return lax.ppermute(value, axes, pairs)  13.2 us
    ppermute x12, waiting for transfers between devices, permute(): return lax.ppermute(value, axes, pairs)  11.7 us
    pallas_call x1, Pallas kernels, both(): call(lightning_kernel, (CH, HEADS * DIM), jnp.bfloat16, 6, 1 << 29)  2.59 us
    unnamed x15, local copies, waits for them, and re-layouts  2.56 us
    pallas_call x1, Pallas kernels, both(): call(local_state_kernel, (32, MSG, DIM), jnp.bfloat16, 3, 1 << 28)  2.35 us
  transfers between devices with their start and end apart: 17, of which 7 were waited for; matrix products, arithmetic and copies ran while one was open for 0% of the time, Pallas kernels for 25%

profile of v2, /device:TPU:32, one launch (start us, length us, event | category | flops | bytes accessed | tf_op | source)
XLA Modules:
  0.0 116.7 jit_solution(1687657479119550076)
XLA Ops:
  0.6 1.6 %copy.12 = bf16[4,8,8,256]{3,2,0,1:T(8,128)(2,1)} copy(bf16[4,8,8,256]{3,2,1,0:T(8,128)(2,1)} %bitcast.30) | data formatting | bytes 262144 | tf_op jit(solution)/shard_map/reshape | solution.py:260
  2.3 8.6 %all-to-all-start.3 = ((bf16[8,32,256]{2,1,0:T(8,128)(2,1)}), bf16[8,32,256]{2,1,0:T(8,128)(2,1)S(1)}, u32[]{:S(2)}, u32[]{:S(2)}) async-start(bf16[8,32,256]{2,1,0:T(8,128)(2,1)} %bitcast.21), calls=%async_computation.3 | async-start | bytes 262144 | tf_op jit(solution)/shard_map/all_to_all | solution.py:242
  10.8 1.0 copy-done.1
  12.6 2.4 %shard_map.86 = bf16[32,48,128]{2,1,0:T(8,128)(2,1)} custom-call(bf16[256,1024]{1,0:T(8,128)(2,1)S(1)} %copy-done, bf16[256,1024]{1,0:T(8,128)(2,1)S(1)} %copy-done.1, f32[8,256]{1,0:T(8,128)S(1)} %copy-done.4), custom_call_target="tpu_custom_call" | custom-call | flops 268435456 | bytes 2097152 | tf_op jit(solution)/shard_map/pallas_call | solution.py:266
  14.9 3.3 %all-to-all-done.3 = bf16[8,32,256]{2,1,0:T(8,128)(2,1)S(1)} async-done(((bf16[8,32,256]{2,1,0:T(8,128)(2,1)}), bf16[8,32,256]{2,1,0:T(8,128)(2,1)S(1)}, u32[]{:S(2)}, u32[]{:S(2)}) %all-to-all-start.3) | async-done | bytes 131104 | tf_op jit(solution)/shard_map/all_to_all | solution.py:242
  18.3 7.3 %all-to-all-start = ((bf16[32,48,128]{2,1,0:T(8,128)(2,1)}), bf16[32,48,128]{2,1,0:T(8,128)(2,1)S(1)}, u32[]{:S(2)}, u32[]{:S(2)}) async-start(bf16[32,48,128]{2,1,0:T(8,128)(2,1)} %shard_map.86), calls=%async_computation | async-start | bytes 786432 | tf_op jit(solution)/shard_map/all_to_all | solution.py:242
  25.6 1.9 %collective-permute-start = (bf16[256,256]{1,0:T(8,128)(2,1)S(1)}, bf16[256,256]{1,0:T(8,128)(2,1)S(1)}, u32[]{:S(2)}, u32[]{:S(2)}) collective-permute-start(bf16[256,256]{1,0:T(8,128)(2,1)S(1)} %bitcast.26), channel_id=1, source_target_pairs={{0,64},{8,24},{16,80},{24,40},{32,96},{40,56},{48,112},{56,8},{64,... | collective-permute-start | bytes 393224 | tf_op jit(solution)/shard_map/ppermute | solution.py:238
  27.5 1.4 %collective-permute-start.1 = (bf16[256,256]{1,0:T(8,128)(2,1)S(1)}, bf16[256,256]{1,0:T(8,128)(2,1)S(1)}, u32[]{:S(2)}, u32[]{:S(2)}) collective-permute-start(bf16[256,256]{1,0:T(8,128)(2,1)S(1)} %bitcast.27), channel_id=1, source_target_pairs={{0,192},{8,56},{16,208},{24,8},{32,224},{40,24},{48,240},{56,40},{... | collective-permute-start | bytes 393224 | tf_op jit(solution)/shard_map/ppermute | solution.py:238
  28.9 2.1 %collective-permute-start.2 = (bf16[256,256]{1,0:T(8,128)(2,1)S(1)}, bf16[256,256]{1,0:T(8,128)(2,1)S(1)}, u32[]{:S(2)}, u32[]{:S(2)}) collective-permute-start(bf16[256,256]{1,0:T(8,128)(2,1)S(1)} %bitcast.28), channel_id=1, source_target_pairs={{0,128},{8,40},{16,144},{24,56},{32,160},{40,8},{48,176},{56,24},{... | collective-permute-start | bytes 393224 | tf_op jit(solution)/shard_map/ppermute | solution.py:238
  31.0 4.3 %collective-permute-done = bf16[256,256]{1,0:T(8,128)(2,1)S(1)} collective-permute-done((bf16[256,256]{1,0:T(8,128)(2,1)S(1)}, bf16[256,256]{1,0:T(8,128)(2,1)S(1)}, u32[]{:S(2)}, u32[]{:S(2)}) %collective-permute-start) | collective-permute-done | bytes 131104 | tf_op jit(solution)/shard_map/ppermute | solution.py:238
  35.3 1.7 %collective-permute-done.2 = bf16[256,256]{1,0:T(8,128)(2,1)S(1)} collective-permute-done((bf16[256,256]{1,0:T(8,128)(2,1)S(1)}, bf16[256,256]{1,0:T(8,128)(2,1)S(1)}, u32[]{:S(2)}, u32[]{:S(2)}) %collective-permute-start.2) | collective-permute-done | bytes 131104 | tf_op jit(solution)/shard_map/ppermute | solution.py:238
  37.0 1.5 %collective-permute-start.3 = (bf16[1024,256]{1,0:T(8,128)(2,1)S(1)}, bf16[1024,256]{1,0:T(8,128)(2,1)S(1)}, u32[]{:S(2)}, u32[]{:S(2)}) collective-permute-start(bf16[1024,256]{1,0:T(8,128)(2,1)S(1)} %pad_maximum_fusion.refs_1_), channel_id=1, source_target_pairs={{0,16},{8,72},{16,32},{24,88},{32,48},{40,104},{48,0},{56,120},{64... | collective-permute-start | bytes 1572872 | tf_op jit(solution)/shard_map/ppermute | solution.py:238
  38.6 1.8 %collective-permute-start.4 = (bf16[1024,256]{1,0:T(8,128)(2,1)S(1)}, bf16[1024,256]{1,0:T(8,128)(2,1)S(1)}, u32[]{:S(2)}, u32[]{:S(2)}) collective-permute-start(bf16[1024,256]{1,0:T(8,128)(2,1)S(1)} %pad_maximum_fusion.refs_1_), channel_id=1, source_target_pairs={{0,48},{8,200},{16,0},{24,216},{32,16},{40,232},{48,32},{56,248},{... | collective-permute-start | bytes 1572872 | tf_op jit(solution)/shard_map/ppermute | solution.py:238
  40.4 5.2 %all-to-all-start.2 = ((bf16[32,8,1024]{2,1,0:T(8,128)(2,1)}), bf16[32,8,1024]{2,1,0:T(8,128)(2,1)S(1)}, u32[]{:S(2)}, u32[]{:S(2)}) async-start(bf16[32,8,1024]{2,1,0:T(8,128)(2,1)} %bitcast.4), calls=%async_computation.2 | async-start | bytes 1048576 | tf_op jit(solution)/shard_map/all_to_all | solution.py:242
  45.7 1.8 %collective-permute-done.3.refs_2_ = bf16[1024,256]{1,0:T(8,128)(2,1)S(1)} collective-permute-done((bf16[1024,256]{1,0:T(8,128)(2,1)S(1)}, bf16[1024,256]{1,0:T(8,128)(2,1)S(1)}, u32[]{:S(2)}, u32[]{:S(2)}) %collective-permute-start.3) | collective-permute-done | bytes 524320 | tf_op jit(solution)/shard_map/ppermute | solution.py:238
  47.9 3.1 %collective-permute-start.6 = (bf16[512,256]{1,0:T(8,128)(2,1)S(1)}, bf16[512,256]{1,0:T(8,128)(2,1)}, u32[]{:S(2)}, u32[]{:S(2)}) collective-permute-start(bf16[512,256]{1,0:T(8,128)(2,1)S(1)} %slice.9), channel_id=1, source_target_pairs={{0,48},{8,200},{16,0},{24,216},{32,16},{40,232},{48,32},{56,248},{... | collective-permute-start | bytes 786440 | tf_op jit(solution)/shard_map/ppermute | solution.py:238
  51.5 3.8 %collective-permute-done.5.refs_4_ = bf16[512,256]{1,0:T(8,128)(2,1)} collective-permute-done((bf16[512,256]{1,0:T(8,128)(2,1)S(1)}, bf16[512,256]{1,0:T(8,128)(2,1)}, u32[]{:S(2)}, u32[]{:S(2)}) %collective-permute-start.5) | collective-permute-done | bytes 262176 | tf_op jit(solution)/shard_map/ppermute | solution.py:238
  56.6 6.7 %all-to-all-done.2 = bf16[32,8,1024]{2,1,0:T(8,128)(2,1)S(1)} async-done(((bf16[32,8,1024]{2,1,0:T(8,128)(2,1)}), bf16[32,8,1024]{2,1,0:T(8,128)(2,1)S(1)}, u32[]{:S(2)}, u32[]{:S(2)}) %all-to-all-start.2) | async-done | bytes 524320 | tf_op jit(solution)/shard_map/all_to_all | solution.py:242
  63.3 4.1 %all-to-all-start.1 = ((bf16[32,32,128]{2,1,0:T(8,128)(2,1)}), bf16[32,32,128]{2,1,0:T(8,128)(2,1)S(1)}, u32[]{:S(2)}, u32[]{:S(2)}) async-start(bf16[32,32,128]{2,1,0:T(8,128)(2,1)} %shard_map.87), calls=%async_computation.1 | async-start | bytes 524288 | tf_op jit(solution)/shard_map/all_to_all | solution.py:242
  67.5 23.7 %shard_map.89 = bf16[256,1024]{1,0:T(8,128)(2,1)} custom-call(bf16[256,1024]{1,0:T(8,128)(2,1)S(1)} %bitcast.23, bf16[1024,256]{1,0:T(8,128)(2,1)S(1)} %pad_maximum_fusion.refs_1_, bf16[1024,256]{1,0:T(8,128)(2,1)S(1)} %collective-permute-done.3.refs_2_, bf16[1024,256]{1,0:T(8,128)(2,1)S(1)} %collective-permute-done.4.refs_3_, ...), custom_call_target="tpu_custom_call" | custom-call | flops 17179869184 | bytes 2097152 | tf_op jit(solution)/shard_map/pallas_call | solution.py:273
  91.2 6.7 %all-to-all-start.4 = ((bf16[32,8,1024]{2,1,0:T(8,128)(2,1)}), bf16[32,8,1024]{2,1,0:T(8,128)(2,1)S(1)}, u32[]{:S(2)}, u32[]{:S(2)}) async-start(bf16[32,8,1024]{2,1,0:T(8,128)(2,1)} %bitcast.8), calls=%async_computation.4 | async-start | bytes 1048576 | tf_op jit(solution)/shard_map/all_to_all | solution.py:242
  98.0 2.6 %shard_map.88 = bf16[256,1024]{1,0:T(8,128)(2,1)} custom-call(bf16[256,1024]{1,0:T(8,128)(2,1)S(1)} %copy-done.3, bf16[256,1024]{1,0:T(8,128)(2,1)S(1)} %copy-done, bf16[256,1024]{1,0:T(8,128)(2,1)S(1)} %copy-done.2, f32[8,256]{1,0:T(8,128)S(1)} %copy-done.5, f32[1,1024]{1,0:T(1,128)S(1)} %bitcast.24, bf16[8,128,128]{2,1,0:T(8,128)(2,1)S(1)} %bitcast.22), custom_call_target="tpu_custom_call" | custom-call | flops 536870912 | bytes 2097152 | tf_op jit(solution)/shard_map/pallas_call | solution.py:296
  100.6 15.3 %all-to-all-done.4 = bf16[32,8,1024]{2,1,0:T(8,128)(2,1)S(1)} async-done(((bf16[32,8,1024]{2,1,0:T(8,128)(2,1)}), bf16[32,8,1024]{2,1,0:T(8,128)(2,1)S(1)}, u32[]{:S(2)}, u32[]{:S(2)}) %all-to-all-start.4) | async-done | bytes 524320 | tf_op jit(solution)/shard_map/all_to_all | solution.py:242
  115.9 0.8 copy.14
  (33 shorter events, 3.1 us)
Async XLA Ops:
  0.6 10.2 %copy-start = (bf16[256,1024]{1,0:T(8,128)(2,1)S(1)}, bf16[256,1024]{1,0:T(8,128)(2,1)}, u32[]{:S(2)}) copy-start(bf16[256,1024]{1,0:T(8,128)(2,1)} %k_ref.3) | copy-start | bytes 1572868
  2.3 16.0 %all-to-all-start.3 = ((bf16[8,32,256]{2,1,0:T(8,128)(2,1)}), bf16[8,32,256]{2,1,0:T(8,128)(2,1)S(1)}, u32[]{:S(2)}, u32[]{:S(2)}) async-start(bf16[8,32,256]{2,1,0:T(8,128)(2,1)} %bitcast.21), calls=%async_computation.3 | async-start | bytes 262144 | tf_op jit(solution)/shard_map/all_to_all | solution.py:242
  10.8 1.0 copy-start.1
  11.9 0.7 copy-start.4
  18.3 22.1 %all-to-all-start = ((bf16[32,48,128]{2,1,0:T(8,128)(2,1)}), bf16[32,48,128]{2,1,0:T(8,128)(2,1)S(1)}, u32[]{:S(2)}, u32[]{:S(2)}) async-start(bf16[32,48,128]{2,1,0:T(8,128)(2,1)} %shard_map.86), calls=%async_computation | async-start | bytes 786432 | tf_op jit(solution)/shard_map/all_to_all | solution.py:242
  25.6 9.7 %collective-permute-start = (bf16[256,256]{1,0:T(8,128)(2,1)S(1)}, bf16[256,256]{1,0:T(8,128)(2,1)S(1)}, u32[]{:S(2)}, u32[]{:S(2)}) collective-permute-start(bf16[256,256]{1,0:T(8,128)(2,1)S(1)} %bitcast.26), channel_id=1, source_target_pairs={{0,64},{8,24},{16,80},{24,40},{32,96},{40,56},{48,112},{56,8},{64,... | collective-permute-start | bytes 393224 | tf_op jit(solution)/shard_map/ppermute | solution.py:238
  27.5 7.9 %collective-permute-start.1 = (bf16[256,256]{1,0:T(8,128)(2,1)S(1)}, bf16[256,256]{1,0:T(8,128)(2,1)S(1)}, u32[]{:S(2)}, u32[]{:S(2)}) collective-permute-start(bf16[256,256]{1,0:T(8,128)(2,1)S(1)} %bitcast.27), channel_id=1, source_target_pairs={{0,192},{8,56},{16,208},{24,8},{32,224},{40,24},{48,240},{56,40},{... | collective-permute-start | bytes 393224 | tf_op jit(solution)/shard_map/ppermute | solution.py:238
  28.9 8.1 %collective-permute-start.2 = (bf16[256,256]{1,0:T(8,128)(2,1)S(1)}, bf16[256,256]{1,0:T(8,128)(2,1)S(1)}, u32[]{:S(2)}, u32[]{:S(2)}) collective-permute-start(bf16[256,256]{1,0:T(8,128)(2,1)S(1)} %bitcast.28), channel_id=1, source_target_pairs={{0,128},{8,40},{16,144},{24,56},{32,160},{40,8},{48,176},{56,24},{... | collective-permute-start | bytes 393224 | tf_op jit(solution)/shard_map/ppermute | solution.py:238
  37.0 10.5 %collective-permute-start.3 = (bf16[1024,256]{1,0:T(8,128)(2,1)S(1)}, bf16[1024,256]{1,0:T(8,128)(2,1)S(1)}, u32[]{:S(2)}, u32[]{:S(2)}) collective-permute-start(bf16[1024,256]{1,0:T(8,128)(2,1)S(1)} %pad_maximum_fusion.refs_1_), channel_id=1, source_target_pairs={{0,16},{8,72},{16,32},{24,88},{32,48},{40,104},{48,0},{56,120},{64... | collective-permute-start | bytes 1572872 | tf_op jit(solution)/shard_map/ppermute | solution.py:238
  38.6 9.3 %collective-permute-start.4 = (bf16[1024,256]{1,0:T(8,128)(2,1)S(1)}, bf16[1024,256]{1,0:T(8,128)(2,1)S(1)}, u32[]{:S(2)}, u32[]{:S(2)}) collective-permute-start(bf16[1024,256]{1,0:T(8,128)(2,1)S(1)} %pad_maximum_fusion.refs_1_), channel_id=1, source_target_pairs={{0,48},{8,200},{16,0},{24,216},{32,16},{40,232},{48,32},{56,248},{... | collective-permute-start | bytes 1572872 | tf_op jit(solution)/shard_map/ppermute | solution.py:238
  40.4 22.9 %all-to-all-start.2 = ((bf16[32,8,1024]{2,1,0:T(8,128)(2,1)}), bf16[32,8,1024]{2,1,0:T(8,128)(2,1)S(1)}, u32[]{:S(2)}, u32[]{:S(2)}) async-start(bf16[32,8,1024]{2,1,0:T(8,128)(2,1)} %bitcast.4), calls=%async_computation.2 | async-start | bytes 1048576 | tf_op jit(solution)/shard_map/all_to_all | solution.py:242
  45.6 21.8 %collective-permute-start.7 = (bf16[1024,256]{1,0:T(8,128)(2,1)S(1)}, bf16[1024,256]{1,0:T(8,128)(2,1)}, u32[]{:S(2)}, u32[]{:S(2)}) collective-permute-start(bf16[1024,256]{1,0:T(8,128)(2,1)S(1)} %pad_maximum_fusion.refs_1_), channel_id=1, source_target_pairs={{0,8},{8,0},{1,9},{9,1},{2,10},{10,2},{3,11},{11,3},{4,12},{12,4},... | collective-permute-start | bytes 1572872 | tf_op jit(solution)/shard_map/ppermute | solution.py:238
  47.5 7.8 %collective-permute-start.5 = (bf16[512,256]{1,0:T(8,128)(2,1)S(1)}, bf16[512,256]{1,0:T(8,128)(2,1)}, u32[]{:S(2)}, u32[]{:S(2)}) collective-permute-start(bf16[512,256]{1,0:T(8,128)(2,1)S(1)} %slice.8), channel_id=1, source_target_pairs={{0,16},{8,72},{16,32},{24,88},{32,48},{40,104},{48,0},{56,120},{64... | collective-permute-start | bytes 786440 | tf_op jit(solution)/shard_map/ppermute | solution.py:238
  47.9 7.9 %collective-permute-start.6 = (bf16[512,256]{1,0:T(8,128)(2,1)S(1)}, bf16[512,256]{1,0:T(8,128)(2,1)}, u32[]{:S(2)}, u32[]{:S(2)}) collective-permute-start(bf16[512,256]{1,0:T(8,128)(2,1)S(1)} %slice.9), channel_id=1, source_target_pairs={{0,48},{8,200},{16,0},{24,216},{32,16},{40,232},{48,32},{56,248},{... | collective-permute-start | bytes 786440 | tf_op jit(solution)/shard_map/ppermute | solution.py:238
  50.9 16.5 %collective-permute-start.8 = (bf16[1024,256]{1,0:T(8,128)(2,1)S(1)}, bf16[1024,256]{1,0:T(8,128)(2,1)}, u32[]{:S(2)}, u32[]{:S(2)}) collective-permute-start(bf16[1024,256]{1,0:T(8,128)(2,1)S(1)} %collective-permute-done.3.refs_2_), channel_id=1, source_target_pairs={{0,8},{8,0},{1,9},{9,1},{2,10},{10,2},{3,11},{11,3},{4,12},{12,4},... | collective-permute-start | bytes 1572872 | tf_op jit(solution)/shard_map/ppermute | solution.py:238
  50.9 16.5 %collective-permute-start.9 = (bf16[1024,256]{1,0:T(8,128)(2,1)S(1)}, bf16[1024,256]{1,0:T(8,128)(2,1)}, u32[]{:S(2)}, u32[]{:S(2)}) collective-permute-start(bf16[1024,256]{1,0:T(8,128)(2,1)S(1)} %collective-permute-done.4.refs_3_), channel_id=1, source_target_pairs={{0,8},{8,0},{1,9},{9,1},{2,10},{10,2},{3,11},{11,3},{4,12},{12,4},... | collective-permute-start | bytes 1572872 | tf_op jit(solution)/shard_map/ppermute | solution.py:238
  55.3 12.1 %collective-permute-start.10 = (bf16[512,256]{1,0:T(8,128)(2,1)}, bf16[512,256]{1,0:T(8,128)(2,1)}, u32[]{:S(2)}, u32[]{:S(2)}) collective-permute-start(bf16[512,256]{1,0:T(8,128)(2,1)} %collective-permute-done.5.refs_4_), channel_id=1, source_target_pairs={{0,8},{8,0},{1,9},{9,1},{2,10},{10,2},{3,11},{11,3},{4,12},{12,4},... | collective-permute-start | bytes 786440 | tf_op jit(solution)/shard_map/ppermute | solution.py:238
  55.8 11.6 %collective-permute-start.11 = (bf16[512,256]{1,0:T(8,128)(2,1)}, bf16[512,256]{1,0:T(8,128)(2,1)}, u32[]{:S(2)}, u32[]{:S(2)}) collective-permute-start(bf16[512,256]{1,0:T(8,128)(2,1)} %collective-permute-done.6.refs_5_), channel_id=1, source_target_pairs={{0,8},{8,0},{1,9},{9,1},{2,10},{10,2},{3,11},{11,3},{4,12},{12,4},... | collective-permute-start | bytes 786440 | tf_op jit(solution)/shard_map/ppermute | solution.py:238
  63.3 27.9 %all-to-all-start.1 = ((bf16[32,32,128]{2,1,0:T(8,128)(2,1)}), bf16[32,32,128]{2,1,0:T(8,128)(2,1)S(1)}, u32[]{:S(2)}, u32[]{:S(2)}) async-start(bf16[32,32,128]{2,1,0:T(8,128)(2,1)} %shard_map.87), calls=%async_computation.1 | async-start | bytes 524288 | tf_op jit(solution)/shard_map/all_to_all | solution.py:242
  67.4 30.5 %copy-start.5 = (f32[8,256]{1,0:T(8,128)S(1)}, f32[8,256]{1,0:T(8,128)}, u32[]{:S(2)}) copy-start(f32[8,256]{1,0:T(8,128)} %g_ref.3) | copy-start | bytes 24580
  67.4 30.5 %copy-start.6 = (f32[1024]{0:T(1024)S(1)}, f32[1024]{0:T(1024)}, u32[]{:S(2)}) copy-start(f32[1024]{0:T(1024)} %param.11) | copy-start | bytes 12292
  91.2 6.8 %copy-start.2 = (bf16[256,1024]{1,0:T(8,128)(2,1)S(1)}, bf16[256,1024]{1,0:T(8,128)(2,1)}, u32[]{:S(2)}) copy-start(bf16[256,1024]{1,0:T(8,128)(2,1)} %v_ref.3) | copy-start | bytes 1572868
  91.2 6.8 %copy-start.3 = (bf16[256,1024]{1,0:T(8,128)(2,1)S(1)}, bf16[256,1024]{1,0:T(8,128)(2,1)}, u32[]{:S(2)}) copy-start(bf16[256,1024]{1,0:T(8,128)(2,1)} %q_ref.1) | copy-start | bytes 1572868
  91.2 24.7 %all-to-all-start.4 = ((bf16[32,8,1024]{2,1,0:T(8,128)(2,1)}), bf16[32,8,1024]{2,1,0:T(8,128)(2,1)S(1)}, u32[]{:S(2)}, u32[]{:S(2)}) async-start(bf16[32,8,1024]{2,1,0:T(8,128)(2,1)} %bitcast.8), calls=%async_computation.4 | async-start | bytes 1048576 | tf_op jit(solution)/shard_map/all_to_all | solution.py:242

commit v3 on v2

--- a/solution.py
+++ b/solution.py
@@ -1,3 +1,4 @@
+import functools
 import math
 
 import jax
@@ -14,7 +15,8 @@
 CH = 256
 DIM = 128
 HEADS = 8
-MSG = 48
+HALF = HEADS // 2
+TOTAL = 16
 
 NT = (((1,), (1,)), ((), ()))
 NN = (((1,), (0,)), ((), ()))
@@ -39,34 +41,97 @@
     return wide.T
 
 
-def local_state_kernel(k_ref, v_ref, g_ref, msg_ref):
+def total_rows(total):
+    row = lax.broadcasted_iota(jnp.int32, (TOTAL, DIM), 0)
+    total = jnp.broadcast_to(total, (TOTAL, DIM))
+    high = total.astype(jnp.bfloat16).astype(jnp.float32)
+    return jnp.where(row == 0, high, jnp.where(row == 1, total - high, 0.0)).astype(jnp.bfloat16)
+
+
+def read_total(ref, h):
+    rows = ref[h, DIM : DIM + TOTAL, :].astype(jnp.float32)
+    return rows[0:1] + rows[1:2]
+
+
+def read_state(ref, h):
+    return ref[h, 0:DIM, :].astype(jnp.float32)
+
+
+def write(ref, h, state, total):
+    ref[h, 0:DIM, :] = state.astype(jnp.bfloat16)
+    ref[h, DIM : DIM + TOTAL, :] = total_rows(total)
+
+
+def local_state_kernel(k_ref, v_ref, g_ref, mine_ref, theirs_ref):
+    core = lax.axis_index("ctx_2")
     cum = running_sum(g_ref[...])
     cum_t = columns(cum)
-    row = lax.broadcasted_iota(jnp.int32, (16, DIM), 0)
     for h in range(HEADS):
         cols = slice(h * DIM, (h + 1) * DIM)
         last = cum[h : h + 1, CH - 1 : CH]
         scale = jnp.exp(last - cum_t[:, h : h + 1])
         ks = (k_ref[:, cols].astype(jnp.float32) * scale).astype(jnp.bfloat16)
-        local = dot(ks, v_ref[:, cols], TN).astype(jnp.bfloat16)
-        total = jnp.broadcast_to(last, (16, DIM))
-        hi = total.astype(jnp.bfloat16).astype(jnp.float32)
-        extra = jnp.where(row == 0, hi, jnp.where(row == 1, total - hi, 0.0)).astype(jnp.bfloat16)
-        for piece in range(4):
-            msg_ref[h * 4 + piece, 0:32, :] = local[piece * 32 : (piece + 1) * 32]
-            msg_ref[h * 4 + piece, 32:48, :] = extra
-
-
-def scan_kernel(msg_ref, out_ref):
-    state = jnp.zeros((32, DIM), jnp.float32)
-    for j in range(msg_ref.shape[0]):
-        out_ref[j] = state.astype(jnp.bfloat16)
-        extra = msg_ref[j, 32:48, :].astype(jnp.float32)
-        decay = jnp.exp(extra[0:1] + extra[1:2])
-        state = decay * state + msg_ref[j, 0:32, :].astype(jnp.float32)
-
-
-def lightning_kernel(q_ref, k_ref, v_ref, g_ref, gain_ref, state_ref, out_ref):
+        local = dot(ks, v_ref[:, cols], TN)
+
+        @pl.when(core == h // HALF)
+        def _():
+            write(mine_ref, h % HALF, local, last)
+
+        @pl.when(core != h // HALF)
+        def _():
+            write(theirs_ref, h % HALF, local, last)
+
+
+def in_order(core, mine_ref, other_ref, h):
+    a, b = read_state(mine_ref, h), read_state(other_ref, h)
+    ta, tb = read_total(mine_ref, h), read_total(other_ref, h)
+    own = core == 0
+    return jnp.where(own, a, b), jnp.where(own, ta, tb), jnp.where(own, b, a), jnp.where(own, tb, ta)
+
+
+def chip_state_kernel(mine_ref, other_ref, chip_ref):
+    core = lax.axis_index("ctx_2")
+    for h in range(HALF):
+        s0, t0, s1, t1 = in_order(core, mine_ref, other_ref, h)
+        write(chip_ref, h, jnp.exp(t1) * s0 + s1, t0 + t1)
+
+
+def row_state_kernel(own_ref, a_ref, b_ref, c_ref, row_ref, before_ref, all_ref):
+    my = lax.axis_index("ctx_1")
+    for d, ref in enumerate((own_ref, a_ref, b_ref, c_ref)):
+        all_ref[(my + NY - d) % NY] = ref[...]
+    for h in range(HALF):
+        state = jnp.zeros((DIM, DIM), jnp.float32)
+        total = jnp.zeros((1, DIM), jnp.float32)
+        before, before_total = state, total
+        for y in range(NY):
+            here = my == y
+            before = jnp.where(here, state, before)
+            before_total = jnp.where(here, total, before_total)
+            t = read_total(all_ref.at[y], h)
+            state = jnp.exp(t) * state + read_state(all_ref.at[y], h)
+            total = total + t
+        write(row_ref, h, state, total)
+        before_ref[h, 0:DIM, :] = before
+        before_ref[h, DIM : DIM + 8, :] = jnp.broadcast_to(before_total, (8, DIM))
+
+
+def entering_kernel(a_ref, b_ref, c_ref, before_ref, mine_ref, other_ref, keep_ref, send_ref):
+    mx, core = lax.axis_index("ctx_0"), lax.axis_index("ctx_2")
+    for h in range(HALF):
+        state = jnp.zeros((DIM, DIM), jnp.float32)
+        for d, ref in ((3, c_ref), (2, b_ref), (1, a_ref)):
+            new = jnp.exp(read_total(ref, h)) * state + read_state(ref, h)
+            state = jnp.where(mx >= d, new, state)
+        state = jnp.exp(before_ref[h, DIM : DIM + 1, :]) * state + before_ref[h, 0:DIM, :]
+        s0, t0, _, _ = in_order(core, mine_ref, other_ref, h)
+        later = jnp.exp(t0) * state + s0
+        keep_ref[h] = jnp.where(core == 0, state, later).astype(jnp.bfloat16)
+        send_ref[h] = jnp.where(core == 0, later, state).astype(jnp.bfloat16)
+
+
+def lightning_kernel(q_ref, k_ref, v_ref, g_ref, gain_ref, keep_ref, got_ref, out_ref):
+    core = lax.axis_index("ctx_2")
     cum = running_sum(g_ref[...])
     cum_t = columns(cum)
     causal = lax.broadcasted_iota(jnp.int32, (CH, CH), 0) >= lax.broadcasted_iota(
@@ -79,7 +144,8 @@
         diff = jnp.minimum(col - cum[h : h + 1, :], 0.0)
         weight = jnp.where(causal, jnp.exp(diff), 0.0)
         probs = (dot(q, k, NT) * weight).astype(jnp.bfloat16)
-        mix = dot(probs, v, NN) + jnp.exp(col) * dot(q, state_ref[h], NN)
+        state = jnp.where(core == h // HALF, keep_ref[h % HALF], got_ref[h % HALF])
+        mix = dot(probs, v, NN) + jnp.exp(col) * dot(q, state, NN)
         norm = lax.rsqrt(jnp.mean(mix * mix, axis=1, keepdims=True) + 1e-05)
         out_ref[:, cols] = (mix * norm * gain_ref[:, cols]).astype(jnp.bfloat16)
 
@@ -96,35 +162,38 @@
     mx, my, mc = (lax.axis_index(a) for a in CTX)
     yc = my * NC + mc
 
-    copies = []
-    for other in range(2):
-        row, plus, minus, far_a, far_b = pieces[5 * other : 5 * other + 5]
-        core = mc if other == 0 else 1 - mc
-        for ds, source in ((0, row), (1, plus), (3, minus), (2, None)):
-            for slot, df in enumerate((0, 1, 3, 2)):
-                ref = source
-                at = slot
-                if source is None:
-                    ref, at = (far_a, slot) if slot < 2 else (far_b, slot - 2)
-                dx = jnp.where(core == 0, df, ds)
-                dy = jnp.where(core == 0, ds, df)
-                chunk = ((mx + NX - dx) % NX * NY + (my + NY - dy) % NY) * NC + core
-                n = len(copies)
-                copy = pltpu.make_async_copy(
-                    ref.at[pl.ds(at * CH, CH), :],
-                    kv_ref.at[pl.ds(pl.multiple_of(chunk * CH, CH), CH), :],
-                    sems.at[n],
-                )
-                copy.start()
-                copies.append(copy)
+    def fetch(ref, at, chunk):
+        return pltpu.make_async_copy(
+            ref.at[pl.ds(at * CH, CH), :],
+            kv_ref.at[pl.ds(pl.multiple_of(chunk * CH, CH), CH), :],
+            sems.at[chunk],
+        )
+
+    for late in (False, True):
+        for other in range(2):
+            row, plus, minus, far_a, far_b = pieces[5 * other : 5 * other + 5]
+            core = mc if other == 0 else 1 - mc
+            for ds, source in ((0, row), (1, plus), (3, minus), (2, None)):
+                for slot, df in enumerate((0, 1, 3, 2)):
+                    ref, at = source, slot
+                    if source is None:
+                        ref, at = (far_a, slot) if slot < 2 else (far_b, slot - 2)
+                    x = (mx + NX - jnp.where(core == 0, df, ds)) % NX
+                    y = (my + NY - jnp.where(core == 0, ds, df)) % NY
+
+                    @pl.when((x >= 2) == late)
+                    def _():
+                        fetch(ref, at, (x * NY + y) * NC + core).start()
+
+    def arrived(x):
+        for i in range(NY * NC):
+            fetch(pieces[0], 0, x * NY * NC + i).wait()
 
     for x in range(NX):
         for g in range(HEADS):
             rows = slice(x * ROWS + g * 64, x * ROWS + (g + 1) * 64)
             qq_ref[rows, :] = q_ref[x * 64 : (x + 1) * 64, g * DIM : (g + 1) * DIM]
     acc_ref[...] = jnp.zeros_like(acc_ref)
-    for copy in copies:
-        copy.wait()
 
     tiles = NX * (NX + 1) // 2
 
@@ -186,12 +255,16 @@
                     jnp.bfloat16
                 )
 
+    arrived(0)
     scores(0)
+    arrived(1)
     weights(0)
     scores(1)
 
     @pl.loop(0, tiles - 2)
     def _(t):
+        for x, first in ((2, 3), (3, 6)):
+            pl.when(t + 2 == first)(functools.partial(arrived, x))
         mix(t)
         scores(t + 2)
         weights(t + 1)
@@ -207,12 +280,12 @@
     return [pl.BlockSpec(memory_space=pltpu.VMEM)] * n
 
 
-def call(kernel, shape, dtype, n, flops, **kw):
+def call(kernel, outs, n, flops, **kw):
     return pl.pallas_call(
         kernel,
-        out_shape=jax.ShapeDtypeStruct(shape, dtype),
+        out_shape=[jax.ShapeDtypeStruct(*o) for o in outs],
         in_specs=kw.pop("in_specs", vmem(n)),
-        out_specs=pl.BlockSpec(memory_space=pltpu.VMEM),
+        out_specs=vmem(len(outs)),
         compiler_params=pltpu.CompilerParams(vmem_limit_bytes=kw.pop("limit", 32 << 20)),
         cost_estimate=pl.CostEstimate(flops=flops, bytes_accessed=2 << 20, transcendentals=0),
         **kw,
@@ -263,21 +336,33 @@
     q = exchange(q, ("ctx_0", "head")).reshape(CH, HEADS * DIM)
     pieces = gather_kv(kv)
 
-    msg = call(local_state_kernel, (32, MSG, DIM), jnp.bfloat16, 3, 1 << 28)(
-        lin_k, lin_v, log_decay
-    )
-    msg = exchange(msg, CTX)
-    state = call(scan_kernel, (32, 32, DIM), jnp.bfloat16, 1, 1 << 20)(msg)
-    state = exchange(state, CTX).reshape(HEADS, DIM, DIM)
-
-    soft = call(
+    swap = [(0, 1), (1, 0)]
+    msg = (HALF, DIM + TOTAL, DIM)
+    msg16 = (msg, jnp.bfloat16)
+    entering = ((HALF, DIM, DIM), jnp.bfloat16)
+    mine, theirs = call(local_state_kernel, [msg16] * 2, 3, 1 << 28)(lin_k, lin_v, log_decay)
+    other = permute(theirs, swap, "ctx_2")
+    (chip,) = call(chip_state_kernel, [msg16], 2, 1 << 20)(mine, other)
+    around = [permute(chip, [(y, (y + d) % NY) for y in range(NY)], "ctx_1") for d in (1, 2, 3)]
+    row_state, before = call(
+        row_state_kernel,
+        [msg16, (msg, jnp.float32)],
+        4,
+        1 << 20,
+        scratch_shapes=[pltpu.VMEM((NY, *msg), jnp.bfloat16)],
+    )(chip, *around)
+    earlier = [permute(row_state, [(x, x + d) for x in range(NX - d)], "ctx_0") for d in (1, 2, 3)]
+    keep, send = call(entering_kernel, [entering] * 2, 6, 1 << 20)(*earlier, before, mine, other)
+    got = permute(send, swap, "ctx_2")
+
+    block = ((CH, HEADS * DIM), jnp.bfloat16)
+    (soft,) = call(
         softmax_kernel,
-        (CH, HEADS * DIM),
-        jnp.bfloat16,
+        [block],
         11,
         1 << 34,
         in_specs=vmem(1) + [pl.BlockSpec(memory_space=pl.ANY)] * 10,
-        limit=28 << 20,
+        limit=22 << 20,
         scratch_shapes=[
             pltpu.VMEM((NX * NY * NC * CH, 2 * DIM), jnp.bfloat16),
             pltpu.VMEM((NX * ROWS, DIM), jnp.bfloat16),
@@ -293,8 +378,8 @@
     soft = exchange(soft.reshape(NX * NZ, 8, HEADS * DIM), ("ctx_0", "head"))
     soft_out = soft.reshape(NX, NZ, 8, HEADS * DIM).swapaxes(1, 2).reshape(32, NZ * HEADS * DIM)
 
-    lin_out = call(lightning_kernel, (CH, HEADS * DIM), jnp.bfloat16, 6, 1 << 29)(
-        lin_q, lin_k, lin_v, log_decay, lin_gain.reshape(1, -1), state
+    (lin_out,) = call(lightning_kernel, [block], 7, 1 << 29)(
+        lin_q, lin_k, lin_v, log_decay, lin_gain.reshape(1, -1), keep, got
     )
     return (lin_out, soft_out)
 

time: 117 us -> 119 us (1.017)
  the two profiles are of different devices: /device:TPU:32 before, /device:TPU:31 now
where the time goes in v3:
time: 119 us; the launch traced here: 118 us
  starting transfers between devices  37.7 us (32%)
  Pallas kernels  32.8 us (28%)
  waiting for transfers between devices  29.2 us (25%)
  blocking collectives  15.7 us (13%)
  local copies, waits for them, and re-layouts  1.77 us (1%)
    ppermute x20, waiting for transfers between devices, permute(): return lax.ppermute(value, axes, pairs)  29.2 us
    pallas_call x1, Pallas kernels, both(): call(softmax_kernel, [block], 11, 1 << 34, in_specs=vmem(1) + [pl.BlockSp...  25.5 us
    ppermute x20, starting transfers between devices, permute(): return lax.ppermute(value, axes, pairs)  25 us
    all_to_all x1, blocking collectives, exchange(): return lax.all_to_all(value, axes, 0, 0, tiled=True)  15.7 us
    all_to_all x2, starting transfers between devices, exchange(): return lax.all_to_all(value, axes, 0, 0, tiled=True)  12.6 us
    pallas_call x1, Pallas kernels, both(): call(local_state_kernel, [msg16] * 2, 3, 1 << 28)(lin_k, lin_v, log_decay)  4.23 us
    pallas_call x1, Pallas kernels, both(): call(lightning_kernel, [block], 7, 1 << 29)  2.6 us
  transfers between devices with their start and end apart: 22, of which 13 were waited for; matrix products, arithmetic and copies ran while one was open for 0% of the time, Pallas kernels for 6%

profile of v3, /device:TPU:31, one launch (start us, length us, event | category | flops | bytes accessed | tf_op | source)
XLA Modules:
  0.0 118.0 jit_solution(7254632913755143570)
XLA Ops:
  1.5 15.7 %all_to_all.15 = bf16[8,32,256]{2,1,0:T(8,128)(2,1)S(1)} all-to-all(bf16[8,32,256]{2,1,0:T(8,128)(2,1)S(1)} %bitcast.24), channel_id=1, replica_groups=mesh['ctx_0'=4,'ctx_1'=4,'ctx_2'=2,'head'=8] {'head'}, dimensions={0} | all-to-all | bytes 262144 | tf_op jit(solution)/shard_map/all_to_all | solution.py:315
  18.2 1.9 %collective-permute-start.8 = (bf16[256,256]{1,0:T(8,128)(2,1)S(1)}, bf16[256,256]{1,0:T(8,128)(2,1)S(1)}, u32[]{:S(2)}, u32[]{:S(2)}) collective-permute-start(bf16[256,256]{1,0:T(8,128)(2,1)S(1)} %bitcast.26), channel_id=1, source_target_pairs={{0,64},{8,24},{16,80},{24,40},{32,96},{40,56},{48,112},{56,8},{64,... | collective-permute-start | bytes 393224 | tf_op jit(solution)/shard_map/ppermute | solution.py:311
  20.1 2.5 %collective-permute-done.10 = bf16[256,256]{1,0:T(8,128)(2,1)S(1)} collective-permute-done((bf16[256,256]{1,0:T(8,128)(2,1)S(1)}, bf16[256,256]{1,0:T(8,128)(2,1)S(1)}, u32[]{:S(2)}, u32[]{:S(2)}) %collective-permute-start.10) | collective-permute-done | bytes 131104 | tf_op jit(solution)/shard_map/ppermute | solution.py:311
  22.6 2.9 %collective-permute-done.9 = bf16[256,256]{1,0:T(8,128)(2,1)S(1)} collective-permute-done((bf16[256,256]{1,0:T(8,128)(2,1)S(1)}, bf16[256,256]{1,0:T(8,128)(2,1)S(1)}, u32[]{:S(2)}, u32[]{:S(2)}) %collective-permute-start.9) | collective-permute-done | bytes 131104 | tf_op jit(solution)/shard_map/ppermute | solution.py:311
  27.0 5.1 %all-to-all-start = ((bf16[32,8,1024]{2,1,0:T(8,128)(2,1)}), bf16[32,8,1024]{2,1,0:T(8,128)(2,1)S(1)}, u32[]{:S(2)}, u32[]{:S(2)}) async-start(bf16[32,8,1024]{2,1,0:T(8,128)(2,1)} %bitcast.3), calls=%async_computation | async-start | bytes 1048576 | tf_op jit(solution)/shard_map/all_to_all | solution.py:315
  32.2 4.0 %collective-permute-start.15 = (bf16[1024,256]{1,0:T(8,128)(2,1)S(1)}, bf16[1024,256]{1,0:T(8,128)(2,1)S(1)}, u32[]{:S(2)}, u32[]{:S(2)}) collective-permute-start(bf16[1024,256]{1,0:T(8,128)(2,1)S(1)} %pad_maximum_fusion.refs_1_), channel_id=1, source_target_pairs={{0,8},{8,0},{1,9},{9,1},{2,10},{10,2},{3,11},{11,3},{4,12},{12,4},... | collective-permute-start | bytes 1572872 | tf_op jit(solution)/shard_map/ppermute | solution.py:311
  36.4 1.5 %collective-permute-start.14 = (bf16[512,256]{1,0:T(8,128)(2,1)S(1)}, bf16[512,256]{1,0:T(8,128)(2,1)}, u32[]{:S(2)}, u32[]{:S(2)}) collective-permute-start(bf16[512,256]{1,0:T(8,128)(2,1)S(1)} %slice.9), channel_id=1, source_target_pairs={{0,48},{8,200},{16,0},{24,216},{32,16},{40,232},{48,32},{56,248},{... | collective-permute-start | bytes 786440 | tf_op jit(solution)/shard_map/ppermute | solution.py:311
  37.9 2.9 %collective-permute-start.16 = (bf16[1024,256]{1,0:T(8,128)(2,1)S(1)}, bf16[1024,256]{1,0:T(8,128)(2,1)S(1)}, u32[]{:S(2)}, u32[]{:S(2)}) collective-permute-start(bf16[1024,256]{1,0:T(8,128)(2,1)S(1)} %collective-permute-done.11.refs_2_), channel_id=1, source_target_pairs={{0,8},{8,0},{1,9},{9,1},{2,10},{10,2},{3,11},{11,3},{4,12},{12,4},... | collective-permute-start | bytes 1572872 | tf_op jit(solution)/shard_map/ppermute | solution.py:311
  40.8 3.4 %collective-permute-done.13.refs_4_ = bf16[512,256]{1,0:T(8,128)(2,1)S(1)} collective-permute-done((bf16[512,256]{1,0:T(8,128)(2,1)S(1)}, bf16[512,256]{1,0:T(8,128)(2,1)S(1)}, u32[]{:S(2)}, u32[]{:S(2)}) %collective-permute-start.13) | collective-permute-done | bytes 262176 | tf_op jit(solution)/shard_map/ppermute | solution.py:311
  45.6 2.3 %collective-permute-start.19 = (bf16[512,256]{1,0:T(8,128)(2,1)}, bf16[512,256]{1,0:T(8,128)(2,1)}, u32[]{:S(2)}, u32[]{:S(2)}) collective-permute-start(bf16[512,256]{1,0:T(8,128)(2,1)} %collective-permute-done.14.refs_5_), channel_id=1, source_target_pairs={{0,8},{8,0},{1,9},{9,1},{2,10},{10,2},{3,11},{11,3},{4,12},{12,4},... | collective-permute-start | bytes 786440 | tf_op jit(solution)/shard_map/ppermute | solution.py:311
  47.9 1.5 %collective-permute-done.19.refs_10_ = bf16[512,256]{1,0:T(8,128)(2,1)} collective-permute-done((bf16[512,256]{1,0:T(8,128)(2,1)}, bf16[512,256]{1,0:T(8,128)(2,1)}, u32[]{:S(2)}, u32[]{:S(2)}) %collective-permute-start.19) | collective-permute-done | bytes 262176 | tf_op jit(solution)/shard_map/ppermute | solution.py:311
  49.4 25.5 %shard_map.91 = bf16[256,1024]{1,0:T(8,128)(2,1)} custom-call(bf16[256,1024]{1,0:T(8,128)(2,1)S(1)} %bitcast.21, bf16[1024,256]{1,0:T(8,128)(2,1)S(1)} %pad_maximum_fusion.refs_1_, bf16[1024,256]{1,0:T(8,128)(2,1)S(1)} %collective-permute-done.11.refs_2_, bf16[1024,256]{1,0:T(8,128)(2,1)S(1)} %collective-permute-done.12.refs_3_, ...), custom_call_target="tpu_custom_call" | custom-call | flops 17179869184 | bytes 2097152 | tf_op jit(solution)/shard_map/pallas_call | solution.py:359
  74.9 7.5 %all-to-all-start.2 = ((bf16[32,8,1024]{2,1,0:T(8,128)(2,1)}), bf16[32,8,1024]{2,1,0:T(8,128)(2,1)S(1)}, u32[]{:S(2)}, u32[]{:S(2)}) async-start(bf16[32,8,1024]{2,1,0:T(8,128)(2,1)} %bitcast.7), calls=%async_computation.2 | async-start | bytes 1048576 | tf_op jit(solution)/shard_map/all_to_all | solution.py:315
  82.5 4.2 %shard_map.86 = (bf16[4,144,128]{2,1,0:T(8,128)(2,1)S(1)}, bf16[4,144,128]{2,1,0:T(8,128)(2,1)S(1)}) custom-call(bf16[256,1024]{1,0:T(8,128)(2,1)S(1)} %copy-done, bf16[256,1024]{1,0:T(8,128)(2,1)S(1)} %copy-done.1, f32[8,256]{1,0:T(8,128)S(1)} %copy-done.3), custom_call_target="tpu_custom_call" | custom-call | flops 268435456 | bytes 2097152 | tf_op jit(solution)/shard_map/pallas_call | solution.py:343
  88.8 2.1 %collective-permute-start.2 = (bf16[4,144,128]{2,1,0:T(8,128)(2,1)S(1)}, bf16[4,144,128]{2,1,0:T(8,128)(2,1)S(1)}, u32[]{:S(2)}, u32[]{:S(2)}) collective-permute-start(bf16[4,144,128]{2,1,0:T(8,128)(2,1)S(1)} %shard_map.87.own_ref), channel_id=1, source_target_pairs={{0,32},{16,48},{32,0},{48,16},{1,33},{17,49},{33,1},{49,17},{2,34}... | collective-permute-start | bytes 442376 | tf_op jit(solution)/shard_map/ppermute | solution.py:311
  90.9 2.8 %collective-permute-done.1.a_ref = bf16[4,144,128]{2,1,0:T(8,128)(2,1)S(1)} collective-permute-done((bf16[4,144,128]{2,1,0:T(8,128)(2,1)S(1)}, bf16[4,144,128]{2,1,0:T(8,128)(2,1)S(1)}, u32[]{:S(2)}, u32[]{:S(2)}) %collective-permute-start.1) | collective-permute-done | bytes 147488 | tf_op jit(solution)/shard_map/ppermute | solution.py:311
  93.7 1.4 %collective-permute-done.2.b_ref = bf16[4,144,128]{2,1,0:T(8,128)(2,1)S(1)} collective-permute-done((bf16[4,144,128]{2,1,0:T(8,128)(2,1)S(1)}, bf16[4,144,128]{2,1,0:T(8,128)(2,1)S(1)}, u32[]{:S(2)}, u32[]{:S(2)}) %collective-permute-start.2) | collective-permute-done | bytes 147488 | tf_op jit(solution)/shard_map/ppermute | solution.py:311
  95.1 3.7 %collective-permute-done.3.c_ref = bf16[4,144,128]{2,1,0:T(8,128)(2,1)S(1)} collective-permute-done((bf16[4,144,128]{2,1,0:T(8,128)(2,1)S(1)}, bf16[4,144,128]{2,1,0:T(8,128)(2,1)S(1)}, u32[]{:S(2)}, u32[]{:S(2)}) %collective-permute-start.3) | collective-permute-done | bytes 147488 | tf_op jit(solution)/shard_map/ppermute | solution.py:311
  99.0 1.4 %collective-permute-start.4 = (bf16[4,144,128]{2,1,0:T(8,128)(2,1)S(1)}, bf16[4,144,128]{2,1,0:T(8,128)(2,1)S(1)}, u32[]{:S(2)}, u32[]{:S(2)}) collective-permute-start(bf16[4,144,128]{2,1,0:T(8,128)(2,1)S(1)} %get-tuple-element.10), channel_id=1, source_target_pairs={{0,64},{64,128},{128,192},{1,65},{65,129},{129,193},{2,66},{66,130... | collective-permute-start | bytes 442376 | tf_op jit(solution)/shard_map/ppermute | solution.py:311
  103.1 2.5 %collective-permute-done.4.a_ref = bf16[4,144,128]{2,1,0:T(8,128)(2,1)S(1)} collective-permute-done((bf16[4,144,128]{2,1,0:T(8,128)(2,1)S(1)}, bf16[4,144,128]{2,1,0:T(8,128)(2,1)S(1)}, u32[]{:S(2)}, u32[]{:S(2)}) %collective-permute-start.4) | collective-permute-done | bytes 147488 | tf_op jit(solution)/shard_map/ppermute | solution.py:311
  105.5 2.8 %collective-permute-done.5.b_ref = bf16[4,144,128]{2,1,0:T(8,128)(2,1)S(1)} collective-permute-done((bf16[4,144,128]{2,1,0:T(8,128)(2,1)S(1)}, bf16[4,144,128]{2,1,0:T(8,128)(2,1)S(1)}, u32[]{:S(2)}, u32[]{:S(2)}) %collective-permute-start.5) | collective-permute-done | bytes 147488 | tf_op jit(solution)/shard_map/ppermute | solution.py:311
  108.3 3.2 %collective-permute-done.6.c_ref = bf16[4,144,128]{2,1,0:T(8,128)(2,1)S(1)} collective-permute-done((bf16[4,144,128]{2,1,0:T(8,128)(2,1)S(1)}, bf16[4,144,128]{2,1,0:T(8,128)(2,1)S(1)}, u32[]{:S(2)}, u32[]{:S(2)}) %collective-permute-start.6) | collective-permute-done | bytes 147488 | tf_op jit(solution)/shard_map/ppermute | solution.py:311
  111.8 1.8 %collective-permute-start.7 = (bf16[4,128,128]{2,1,0:T(8,128)(2,1)S(1)}, bf16[4,128,128]{2,1,0:T(8,128)(2,1)S(1)}, u32[]{:S(2)}, u32[]{:S(2)}) collective-permute-start(bf16[4,128,128]{2,1,0:T(8,128)(2,1)S(1)} %get-tuple-element.13), channel_id=1, source_target_pairs={{0,8},{8,0},{1,9},{9,1},{2,10},{10,2},{3,11},{11,3},{4,12},{12,4},... | collective-permute-start | bytes 393224 | tf_op jit(solution)/shard_map/ppermute | solution.py:311
  114.6 2.6 %shard_map.90 = bf16[256,1024]{1,0:T(8,128)(2,1)} custom-call(bf16[256,1024]{1,0:T(8,128)(2,1)S(1)} %copy-done.2, bf16[256,1024]{1,0:T(8,128)(2,1)S(1)} %copy-done, bf16[256,1024]{1,0:T(8,128)(2,1)S(1)} %copy-done.1, f32[8,256]{1,0:T(8,128)S(1)} %copy-done.3, f32[1,1024]{1,0:T(1,128)S(1)} %bitcast.22, bf16[4,128,128]{2,1,0:T(8,128)(2,1)S(1)} %get-tuple-element.12.keep_ref, ...), custom_call_target="tpu_custom_call" | custom-call | flops 536870912 | bytes 2097152 | tf_op jit(solution)/shard_map/pallas_call | solution.py:381
  (42 shorter events, 11.9 us)
Async XLA Ops:
  17.3 5.3 %collective-permute-start.10 = (bf16[256,256]{1,0:T(8,128)(2,1)S(1)}, bf16[256,256]{1,0:T(8,128)(2,1)S(1)}, u32[]{:S(2)}, u32[]{:S(2)}) collective-permute-start(bf16[256,256]{1,0:T(8,128)(2,1)S(1)} %bitcast.25), channel_id=1, source_target_pairs={{0,128},{8,40},{16,144},{24,56},{32,160},{40,8},{48,176},{56,24},{... | collective-permute-start | bytes 393224 | tf_op jit(solution)/shard_map/ppermute | solution.py:311
  18.2 4.4 %collective-permute-start.8 = (bf16[256,256]{1,0:T(8,128)(2,1)S(1)}, bf16[256,256]{1,0:T(8,128)(2,1)S(1)}, u32[]{:S(2)}, u32[]{:S(2)}) collective-permute-start(bf16[256,256]{1,0:T(8,128)(2,1)S(1)} %bitcast.26), channel_id=1, source_target_pairs={{0,64},{8,24},{16,80},{24,40},{32,96},{40,56},{48,112},{56,8},{64,... | collective-permute-start | bytes 393224 | tf_op jit(solution)/shard_map/ppermute | solution.py:311
  20.1 5.3 %collective-permute-start.9 = (bf16[256,256]{1,0:T(8,128)(2,1)S(1)}, bf16[256,256]{1,0:T(8,128)(2,1)S(1)}, u32[]{:S(2)}, u32[]{:S(2)}) collective-permute-start(bf16[256,256]{1,0:T(8,128)(2,1)S(1)} %bitcast.27), channel_id=1, source_target_pairs={{0,192},{8,56},{16,208},{24,8},{32,224},{40,24},{48,240},{56,40},{... | collective-permute-start | bytes 393224 | tf_op jit(solution)/shard_map/ppermute | solution.py:311
  25.5 10.7 %collective-permute-start.11 = (bf16[1024,256]{1,0:T(8,128)(2,1)S(1)}, bf16[1024,256]{1,0:T(8,128)(2,1)S(1)}, u32[]{:S(2)}, u32[]{:S(2)}) collective-permute-start(bf16[1024,256]{1,0:T(8,128)(2,1)S(1)} %pad_maximum_fusion.refs_1_), channel_id=1, source_target_pairs={{0,16},{8,72},{16,32},{24,88},{32,48},{40,104},{48,0},{56,120},{64... | collective-permute-start | bytes 1572872 | tf_op jit(solution)/shard_map/ppermute | solution.py:311
  25.8 10.6 %collective-permute-start.12 = (bf16[1024,256]{1,0:T(8,128)(2,1)S(1)}, bf16[1024,256]{1,0:T(8,128)(2,1)S(1)}, u32[]{:S(2)}, u32[]{:S(2)}) collective-permute-start(bf16[1024,256]{1,0:T(8,128)(2,1)S(1)} %pad_maximum_fusion.refs_1_), channel_id=1, source_target_pairs={{0,48},{8,200},{16,0},{24,216},{32,16},{40,232},{48,32},{56,248},{... | collective-permute-start | bytes 1572872 | tf_op jit(solution)/shard_map/ppermute | solution.py:311
  27.0 20.8 %all-to-all-start = ((bf16[32,8,1024]{2,1,0:T(8,128)(2,1)}), bf16[32,8,1024]{2,1,0:T(8,128)(2,1)S(1)}, u32[]{:S(2)}, u32[]{:S(2)}) async-start(bf16[32,8,1024]{2,1,0:T(8,128)(2,1)} %bitcast.3), calls=%async_computation | async-start | bytes 1048576 | tf_op jit(solution)/shard_map/all_to_all | solution.py:315
  32.2 15.7 %collective-permute-start.15 = (bf16[1024,256]{1,0:T(8,128)(2,1)S(1)}, bf16[1024,256]{1,0:T(8,128)(2,1)S(1)}, u32[]{:S(2)}, u32[]{:S(2)}) collective-permute-start(bf16[1024,256]{1,0:T(8,128)(2,1)S(1)} %pad_maximum_fusion.refs_1_), channel_id=1, source_target_pairs={{0,8},{8,0},{1,9},{9,1},{2,10},{10,2},{3,11},{11,3},{4,12},{12,4},... | collective-permute-start | bytes 1572872 | tf_op jit(solution)/shard_map/ppermute | solution.py:311
  36.2 8.0 %collective-permute-start.13 = (bf16[512,256]{1,0:T(8,128)(2,1)S(1)}, bf16[512,256]{1,0:T(8,128)(2,1)S(1)}, u32[]{:S(2)}, u32[]{:S(2)}) collective-permute-start(bf16[512,256]{1,0:T(8,128)(2,1)S(1)} %slice.8), channel_id=1, source_target_pairs={{0,16},{8,72},{16,32},{24,88},{32,48},{40,104},{48,0},{56,120},{64... | collective-permute-start | bytes 786440 | tf_op jit(solution)/shard_map/ppermute | solution.py:311
  36.4 9.2 %collective-permute-start.14 = (bf16[512,256]{1,0:T(8,128)(2,1)S(1)}, bf16[512,256]{1,0:T(8,128)(2,1)}, u32[]{:S(2)}, u32[]{:S(2)}) collective-permute-start(bf16[512,256]{1,0:T(8,128)(2,1)S(1)} %slice.9), channel_id=1, source_target_pairs={{0,48},{8,200},{16,0},{24,216},{32,16},{40,232},{48,32},{56,248},{... | collective-permute-start | bytes 786440 | tf_op jit(solution)/shard_map/ppermute | solution.py:311
  37.9 11.5 %collective-permute-start.16 = (bf16[1024,256]{1,0:T(8,128)(2,1)S(1)}, bf16[1024,256]{1,0:T(8,128)(2,1)S(1)}, u32[]{:S(2)}, u32[]{:S(2)}) collective-permute-start(bf16[1024,256]{1,0:T(8,128)(2,1)S(1)} %collective-permute-done.11.refs_2_), channel_id=1, source_target_pairs={{0,8},{8,0},{1,9},{9,1},{2,10},{10,2},{3,11},{11,3},{4,12},{12,4},... | collective-permute-start | bytes 1572872 | tf_op jit(solution)/shard_map/ppermute | solution.py:311
  40.8 8.6 %collective-permute-start.17 = (bf16[1024,256]{1,0:T(8,128)(2,1)S(1)}, bf16[1024,256]{1,0:T(8,128)(2,1)}, u32[]{:S(2)}, u32[]{:S(2)}) collective-permute-start(bf16[1024,256]{1,0:T(8,128)(2,1)S(1)} %collective-permute-done.12.refs_3_), channel_id=1, source_target_pairs={{0,8},{8,0},{1,9},{9,1},{2,10},{10,2},{3,11},{11,3},{4,12},{12,4},... | collective-permute-start | bytes 1572872 | tf_op jit(solution)/shard_map/ppermute | solution.py:311
  44.2 3.7 %collective-permute-start.18 = (bf16[512,256]{1,0:T(8,128)(2,1)S(1)}, bf16[512,256]{1,0:T(8,128)(2,1)}, u32[]{:S(2)}, u32[]{:S(2)}) collective-permute-start(bf16[512,256]{1,0:T(8,128)(2,1)S(1)} %collective-permute-done.13.refs_4_), channel_id=1, source_target_pairs={{0,8},{8,0},{1,9},{9,1},{2,10},{10,2},{3,11},{11,3},{4,12},{12,4},... | collective-permute-start | bytes 786440 | tf_op jit(solution)/shard_map/ppermute | solution.py:311
  45.6 3.8 %collective-permute-start.19 = (bf16[512,256]{1,0:T(8,128)(2,1)}, bf16[512,256]{1,0:T(8,128)(2,1)}, u32[]{:S(2)}, u32[]{:S(2)}) collective-permute-start(bf16[512,256]{1,0:T(8,128)(2,1)} %collective-permute-done.14.refs_5_), channel_id=1, source_target_pairs={{0,8},{8,0},{1,9},{9,1},{2,10},{10,2},{3,11},{11,3},{4,12},{12,4},... | collective-permute-start | bytes 786440 | tf_op jit(solution)/shard_map/ppermute | solution.py:311
  49.4 33.0 %copy-start.3 = (f32[8,256]{1,0:T(8,128)S(1)}, f32[8,256]{1,0:T(8,128)}, u32[]{:S(2)}) copy-start(f32[8,256]{1,0:T(8,128)} %g_ref.3) | copy-start | bytes 24580
  74.9 42.3 %all-to-all-start.2 = ((bf16[32,8,1024]{2,1,0:T(8,128)(2,1)}), bf16[32,8,1024]{2,1,0:T(8,128)(2,1)S(1)}, u32[]{:S(2)}, u32[]{:S(2)}) async-start(bf16[32,8,1024]{2,1,0:T(8,128)(2,1)} %bitcast.7), calls=%async_computation.2 | async-start | bytes 1048576 | tf_op jit(solution)/shard_map/all_to_all | solution.py:315
  86.7 1.8 %collective-permute-start = (bf16[4,144,128]{2,1,0:T(8,128)(2,1)S(1)}, bf16[4,144,128]{2,1,0:T(8,128)(2,1)S(1)}, u32[]{:S(2)}, u32[]{:S(2)}) collective-permute-start(bf16[4,144,128]{2,1,0:T(8,128)(2,1)S(1)} %get-tuple-element.9), channel_id=1, source_target_pairs={{0,8},{8,0},{1,9},{9,1},{2,10},{10,2},{3,11},{11,3},{4,12},{12,4},... | collective-permute-start | bytes 442376 | tf_op jit(solution)/shard_map/ppermute | solution.py:311
  88.6 5.1 %collective-permute-start.1 = (bf16[4,144,128]{2,1,0:T(8,128)(2,1)S(1)}, bf16[4,144,128]{2,1,0:T(8,128)(2,1)S(1)}, u32[]{:S(2)}, u32[]{:S(2)}) collective-permute-start(bf16[4,144,128]{2,1,0:T(8,128)(2,1)S(1)} %shard_map.87.own_ref), channel_id=1, source_target_pairs={{0,16},{16,32},{32,48},{48,0},{1,17},{17,33},{33,49},{49,1},{2,18}... | collective-permute-start | bytes 442376 | tf_op jit(solution)/shard_map/ppermute | solution.py:311
  88.8 6.3 %collective-permute-start.2 = (bf16[4,144,128]{2,1,0:T(8,128)(2,1)S(1)}, bf16[4,144,128]{2,1,0:T(8,128)(2,1)S(1)}, u32[]{:S(2)}, u32[]{:S(2)}) collective-permute-start(bf16[4,144,128]{2,1,0:T(8,128)(2,1)S(1)} %shard_map.87.own_ref), channel_id=1, source_target_pairs={{0,32},{16,48},{32,0},{48,16},{1,33},{17,49},{33,1},{49,17},{2,34}... | collective-permute-start | bytes 442376 | tf_op jit(solution)/shard_map/ppermute | solution.py:311
  90.9 7.9 %collective-permute-start.3 = (bf16[4,144,128]{2,1,0:T(8,128)(2,1)S(1)}, bf16[4,144,128]{2,1,0:T(8,128)(2,1)S(1)}, u32[]{:S(2)}, u32[]{:S(2)}) collective-permute-start(bf16[4,144,128]{2,1,0:T(8,128)(2,1)S(1)} %shard_map.87.own_ref), channel_id=1, source_target_pairs={{0,48},{16,0},{32,16},{48,32},{1,49},{17,1},{33,17},{49,33},{2,50}... | collective-permute-start | bytes 442376 | tf_op jit(solution)/shard_map/ppermute | solution.py:311
  99.0 15.6 %copy-start.2 = (bf16[256,1024]{1,0:T(8,128)(2,1)S(1)}, bf16[256,1024]{1,0:T(8,128)(2,1)}, u32[]{:S(2)}) copy-start(bf16[256,1024]{1,0:T(8,128)(2,1)} %q_ref.1) | copy-start | bytes 1572868
  99.0 6.5 %collective-permute-start.4 = (bf16[4,144,128]{2,1,0:T(8,128)(2,1)S(1)}, bf16[4,144,128]{2,1,0:T(8,128)(2,1)S(1)}, u32[]{:S(2)}, u32[]{:S(2)}) collective-permute-start(bf16[4,144,128]{2,1,0:T(8,128)(2,1)S(1)} %get-tuple-element.10), channel_id=1, source_target_pairs={{0,64},{64,128},{128,192},{1,65},{65,129},{129,193},{2,66},{66,130... | collective-permute-start | bytes 442376 | tf_op jit(solution)/shard_map/ppermute | solution.py:311
  100.5 7.9 %collective-permute-start.5 = (bf16[4,144,128]{2,1,0:T(8,128)(2,1)S(1)}, bf16[4,144,128]{2,1,0:T(8,128)(2,1)S(1)}, u32[]{:S(2)}, u32[]{:S(2)}) collective-permute-start(bf16[4,144,128]{2,1,0:T(8,128)(2,1)S(1)} %get-tuple-element.10), channel_id=1, source_target_pairs={{0,128},{64,192},{1,129},{65,193},{2,130},{66,194},{3,131},{67,195... | collective-permute-start | bytes 442376 | tf_op jit(solution)/shard_map/ppermute | solution.py:311
  101.8 9.8 %collective-permute-start.6 = (bf16[4,144,128]{2,1,0:T(8,128)(2,1)S(1)}, bf16[4,144,128]{2,1,0:T(8,128)(2,1)S(1)}, u32[]{:S(2)}, u32[]{:S(2)}) collective-permute-start(bf16[4,144,128]{2,1,0:T(8,128)(2,1)S(1)} %get-tuple-element.10), channel_id=1, source_target_pairs={{0,192},{1,193},{2,194},{3,195},{4,196},{5,197},{6,198},{7,199},{8... | collective-permute-start | bytes 442376 | tf_op jit(solution)/shard_map/ppermute | solution.py:311
  111.8 2.8 %collective-permute-start.7 = (bf16[4,128,128]{2,1,0:T(8,128)(2,1)S(1)}, bf16[4,128,128]{2,1,0:T(8,128)(2,1)S(1)}, u32[]{:S(2)}, u32[]{:S(2)}) collective-permute-start(bf16[4,128,128]{2,1,0:T(8,128)(2,1)S(1)} %get-tuple-element.13), channel_id=1, source_target_pairs={{0,8},{8,0},{1,9},{9,1},{2,10},{10,2},{3,11},{11,3},{4,12},{12,4},... | collective-permute-start | bytes 393224 | tf_op jit(solution)/shard_map/ppermute | solution.py:311
  (3 other events, 18.0 us)

commit v4 on v3

--- a/solution.py
+++ b/solution.py
@@ -1,4 +1,3 @@
-import functools
 import math
 
 import jax
@@ -63,23 +62,26 @@
 
 
 def local_state_kernel(k_ref, v_ref, g_ref, mine_ref, theirs_ref):
-    core = lax.axis_index("ctx_2")
+    first = lax.axis_index("ctx_2") == 0
     cum = running_sum(g_ref[...])
     cum_t = columns(cum)
-    for h in range(HEADS):
+
+    def local(h):
         cols = slice(h * DIM, (h + 1) * DIM)
         last = cum[h : h + 1, CH - 1 : CH]
         scale = jnp.exp(last - cum_t[:, h : h + 1])
         ks = (k_ref[:, cols].astype(jnp.float32) * scale).astype(jnp.bfloat16)
-        local = dot(ks, v_ref[:, cols], TN)
-
-        @pl.when(core == h // HALF)
-        def _():
-            write(mine_ref, h % HALF, local, last)
-
-        @pl.when(core != h // HALF)
-        def _():
-            write(theirs_ref, h % HALF, local, last)
+        return dot(ks, v_ref[:, cols], TN), last
+
+    for h in range(HALF):
+        low, low_total = local(h)
+        high, high_total = local(HALF + h)
+        write(
+            mine_ref, h, jnp.where(first, low, high), jnp.where(first, low_total, high_total)
+        )
+        write(
+            theirs_ref, h, jnp.where(first, high, low), jnp.where(first, high_total, low_total)
+        )
 
 
 def in_order(core, mine_ref, other_ref, h):
@@ -162,38 +164,29 @@
     mx, my, mc = (lax.axis_index(a) for a in CTX)
     yc = my * NC + mc
 
-    def fetch(ref, at, chunk):
-        return pltpu.make_async_copy(
-            ref.at[pl.ds(at * CH, CH), :],
-            kv_ref.at[pl.ds(pl.multiple_of(chunk * CH, CH), CH), :],
-            sems.at[chunk],
-        )
-
-    for late in (False, True):
-        for other in range(2):
-            row, plus, minus, far_a, far_b = pieces[5 * other : 5 * other + 5]
-            core = mc if other == 0 else 1 - mc
-            for ds, source in ((0, row), (1, plus), (3, minus), (2, None)):
-                for slot, df in enumerate((0, 1, 3, 2)):
-                    ref, at = source, slot
-                    if source is None:
-                        ref, at = (far_a, slot) if slot < 2 else (far_b, slot - 2)
-                    x = (mx + NX - jnp.where(core == 0, df, ds)) % NX
-                    y = (my + NY - jnp.where(core == 0, ds, df)) % NY
-
-                    @pl.when((x >= 2) == late)
-                    def _():
-                        fetch(ref, at, (x * NY + y) * NC + core).start()
-
-    def arrived(x):
-        for i in range(NY * NC):
-            fetch(pieces[0], 0, x * NY * NC + i).wait()
+    copies = []
+    for n, ref in enumerate(pieces):
+        other, part = divmod(n, 5)
+        rows = pl.ds((other * 16 + (0, 4, 8, 12, 14)[part]) * CH, ref.shape[0])
+        copies.append(pltpu.make_async_copy(ref, kv_ref.at[rows, :], sems.at[n]))
+        copies[-1].start()
+
+    def chunk(kx, k):
+        other, i = divmod(k, 4)
+        core = mc if other == 0 else 1 - mc
+        d = (mx + NX - kx) % NX
+        d = jnp.where(d < 2, d, 5 - d)
+        slot = other * 16 + jnp.where(core == 0, i * 4 + d, d * 4 + i)
+        y = (my + NY - (0, 1, 3, 2)[i]) % NY
+        return pl.ds(pl.multiple_of(slot * CH, CH), CH), (y * NC + core) * CH
 
     for x in range(NX):
         for g in range(HEADS):
             rows = slice(x * ROWS + g * 64, x * ROWS + (g + 1) * 64)
             qq_ref[rows, :] = q_ref[x * 64 : (x + 1) * 64, g * DIM : (g + 1) * DIM]
     acc_ref[...] = jnp.zeros_like(acc_ref)
+    for copy in copies:
+        copy.wait()
 
     tiles = NX * (NX + 1) // 2
 
@@ -201,23 +194,23 @@
         t = jnp.int32(t)
         x = sum((t >= n).astype(jnp.int32) for n in (1, 3, 6))
         u = t - x * (x + 1) // 2
-        return x, u, jnp.where(u == 0, x, u - 1) * KEYS, t % 2
+        return x, u, jnp.where(u == 0, x, u - 1), t % 2
 
     def scores(t):
-        x, _, start, slot = tile(t)
+        x, _, kx, slot = tile(t)
         r = lax.broadcasted_iota(jnp.int32, (ROWS, 1), 0) % 64
-        pos = (x * 8 + yc) * CH + (r // 8) * 32 + mx * 8 + r % 8 - start
+        pos = ((x - kx) * 8 + yc) * CH + (r // 8) * 32 + mx * 8 + r % 8
         qq = qq_ref[pl.ds(pl.multiple_of(x * ROWS, ROWS), ROWS), :]
-        for k in range(KEYS // 256):
-            keys = kv_ref[pl.ds(pl.multiple_of(start + k * 256, 256), 256), 0:DIM]
-            s = dot(qq, keys, NT) * SCALE
+        for k in range(KEYS // CH):
+            rows, at = chunk(kx, k)
+            s = dot(qq, kv_ref[rows, 0:DIM], NT) * SCALE
             lane = lax.broadcasted_iota(jnp.int32, s.shape, 1)
-            s = jnp.where(lane <= pos - k * 256, s, -1e30)
-            s_ref[slot, :, k * 256 : (k + 1) * 256] = s
+            s = jnp.where(lane <= pos - at, s, -1e30)
+            s_ref[slot, :, k * CH : (k + 1) * CH] = s
             peak = jnp.maximum(s[:, :DIM], s[:, DIM:])
             if k > 0:
                 peak = jnp.maximum(peak, pm_ref[slot])
-            if k == KEYS // 256 - 1:
+            if k == KEYS // CH - 1:
                 peak = jnp.broadcast_to(jnp.max(peak, axis=1, keepdims=True), (ROWS, DIM))
             pm_ref[slot] = peak
 
@@ -236,8 +229,9 @@
                 )
 
     def mix(t):
-        _, _, start, slot = tile(t)
-        values = kv_ref[pl.ds(pl.multiple_of(start, KEYS), KEYS), DIM : 2 * DIM]
+        _, _, kx, slot = tile(t)
+        values = [kv_ref[chunk(kx, k)[0], DIM : 2 * DIM] for k in range(KEYS // CH)]
+        values = jnp.concatenate(values, axis=0)
         values = jnp.concatenate([values, jnp.ones_like(values)], axis=1)
         alpha = al_ref[slot]
         alpha = jnp.concatenate([alpha, alpha], axis=1)
@@ -255,16 +249,12 @@
                     jnp.bfloat16
                 )
 
-    arrived(0)
     scores(0)
-    arrived(1)
     weights(0)
     scores(1)
 
     @pl.loop(0, tiles - 2)
     def _(t):
-        for x, first in ((2, 3), (3, 6)):
-            pl.when(t + 2 == first)(functools.partial(arrived, x))
         mix(t)
         scores(t + 2)
         weights(t + 1)
@@ -362,7 +352,7 @@
         11,
         1 << 34,
         in_specs=vmem(1) + [pl.BlockSpec(memory_space=pl.ANY)] * 10,
-        limit=22 << 20,
+        limit=28 << 20,
         scratch_shapes=[
             pltpu.VMEM((NX * NY * NC * CH, 2 * DIM), jnp.bfloat16),
             pltpu.VMEM((NX * ROWS, DIM), jnp.bfloat16),
@@ -372,7 +362,7 @@
             pltpu.VMEM((2, ROWS, DIM), jnp.float32),
             pltpu.VMEM((ROWS, DIM), jnp.float32),
             pltpu.VMEM((ROWS, 2 * DIM), jnp.float32),
-            pltpu.SemaphoreType.DMA((32,)),
+            pltpu.SemaphoreType.DMA((10,)),
         ],
     )(q, *pieces)
     soft = exchange(soft.reshape(NX * NZ, 8, HEADS * DIM), ("ctx_0", "head"))

time: 119 us -> 112 us (0.941)
  Pallas kernels: 32.8 us -> 25.8 us
    pallas_call x1, Pallas kernels: 25.5 us -> 21.1 us  [both(): call(softmax_kernel, [block], 11, 1 << 34, in_specs=vmem(1) + [pl.BlockSp...]
    pallas_call x1, Pallas kernels: 4.23 us -> 1.56 us  [both(): call(local_state_kernel, [msg16] * 2, 3, 1 << 28)(lin_k, lin_v, log_decay)]
  transfers between devices with their start and end apart: 22 -> 22, of which waited for: 13 -> 13; matrix products, arithmetic and copies ran while one was open for 0% -> 0% of each run, Pallas kernels for 6% -> 4%
where the time goes in v4:
time: 112 us; the launch traced here: 111 us
  starting transfers between devices  37.6 us (34%)
  waiting for transfers between devices  29.3 us (26%)
  Pallas kernels  25.8 us (23%)
  blocking collectives  15.7 us (14%)
  local copies, waits for them, and re-layouts  1.77 us (2%)
    ppermute x20, waiting for transfers between devices, permute(): return lax.ppermute(value, axes, pairs)  29.2 us
    ppermute x20, starting transfers between devices, permute(): return lax.ppermute(value, axes, pairs)  25 us
    pallas_call x1, Pallas kernels, both(): call(softmax_kernel, [block], 11, 1 << 34, in_specs=vmem(1) + [pl.BlockSp...  21.1 us
    all_to_all x1, blocking collectives, exchange(): return lax.all_to_all(value, axes, 0, 0, tiled=True)  15.7 us
    all_to_all x2, starting transfers between devices, exchange(): return lax.all_to_all(value, axes, 0, 0, tiled=True)  12.7 us
    pallas_call x1, Pallas kernels, both(): call(lightning_kernel, [block], 7, 1 << 29)  2.6 us
  transfers between devices with their start and end apart: 22, of which 13 were waited for; matrix products, arithmetic and copies ran while one was open for 0% of the time, Pallas kernels for 4%

profile of v4, /device:TPU:31, one launch (start us, length us, event | category | flops | bytes accessed | tf_op | source)
XLA Modules:
  0.0 111.0 jit_solution(2041091733227718945)
XLA Ops:
  1.5 15.7 %all_to_all.15 = bf16[8,32,256]{2,1,0:T(8,128)(2,1)S(1)} all-to-all(bf16[8,32,256]{2,1,0:T(8,128)(2,1)S(1)} %bitcast.24), channel_id=1, replica_groups=mesh['ctx_0'=4,'ctx_1'=4,'ctx_2'=2,'head'=8] {'head'}, dimensions={0} | all-to-all | bytes 262144 | tf_op jit(solution)/shard_map/all_to_all | solution.py:305
  18.2 1.9 %collective-permute-start.8 = (bf16[256,256]{1,0:T(8,128)(2,1)S(1)}, bf16[256,256]{1,0:T(8,128)(2,1)S(1)}, u32[]{:S(2)}, u32[]{:S(2)}) collective-permute-start(bf16[256,256]{1,0:T(8,128)(2,1)S(1)} %bitcast.26), channel_id=1, source_target_pairs={{0,64},{8,24},{16,80},{24,40},{32,96},{40,56},{48,112},{56,8},{64,... | collective-permute-start | bytes 393224 | tf_op jit(solution)/shard_map/ppermute | solution.py:301
  20.1 2.5 %collective-permute-done.10 = bf16[256,256]{1,0:T(8,128)(2,1)S(1)} collective-permute-done((bf16[256,256]{1,0:T(8,128)(2,1)S(1)}, bf16[256,256]{1,0:T(8,128)(2,1)S(1)}, u32[]{:S(2)}, u32[]{:S(2)}) %collective-permute-start.10) | collective-permute-done | bytes 131104 | tf_op jit(solution)/shard_map/ppermute | solution.py:301
  22.6 2.9 %collective-permute-done.9 = bf16[256,256]{1,0:T(8,128)(2,1)S(1)} collective-permute-done((bf16[256,256]{1,0:T(8,128)(2,1)S(1)}, bf16[256,256]{1,0:T(8,128)(2,1)S(1)}, u32[]{:S(2)}, u32[]{:S(2)}) %collective-permute-start.9) | collective-permute-done | bytes 131104 | tf_op jit(solution)/shard_map/ppermute | solution.py:301
  27.0 5.1 %all-to-all-start = ((bf16[32,8,1024]{2,1,0:T(8,128)(2,1)}), bf16[32,8,1024]{2,1,0:T(8,128)(2,1)S(1)}, u32[]{:S(2)}, u32[]{:S(2)}) async-start(bf16[32,8,1024]{2,1,0:T(8,128)(2,1)} %bitcast.3), calls=%async_computation | async-start | bytes 1048576 | tf_op jit(solution)/shard_map/all_to_all | solution.py:305
  32.2 4.0 %collective-permute-start.15 = (bf16[1024,256]{1,0:T(8,128)(2,1)S(1)}, bf16[1024,256]{1,0:T(8,128)(2,1)S(1)}, u32[]{:S(2)}, u32[]{:S(2)}) collective-permute-start(bf16[1024,256]{1,0:T(8,128)(2,1)S(1)} %pad_maximum_fusion.refs_1_), channel_id=1, source_target_pairs={{0,8},{8,0},{1,9},{9,1},{2,10},{10,2},{3,11},{11,3},{4,12},{12,4},... | collective-permute-start | bytes 1572872 | tf_op jit(solution)/shard_map/ppermute | solution.py:301
  36.4 1.5 %collective-permute-start.14 = (bf16[512,256]{1,0:T(8,128)(2,1)S(1)}, bf16[512,256]{1,0:T(8,128)(2,1)}, u32[]{:S(2)}, u32[]{:S(2)}) collective-permute-start(bf16[512,256]{1,0:T(8,128)(2,1)S(1)} %slice.9), channel_id=1, source_target_pairs={{0,48},{8,200},{16,0},{24,216},{32,16},{40,232},{48,32},{56,248},{... | collective-permute-start | bytes 786440 | tf_op jit(solution)/shard_map/ppermute | solution.py:301
  37.9 2.9 %collective-permute-start.16 = (bf16[1024,256]{1,0:T(8,128)(2,1)S(1)}, bf16[1024,256]{1,0:T(8,128)(2,1)S(1)}, u32[]{:S(2)}, u32[]{:S(2)}) collective-permute-start(bf16[1024,256]{1,0:T(8,128)(2,1)S(1)} %collective-permute-done.11.refs_2_), channel_id=1, source_target_pairs={{0,8},{8,0},{1,9},{9,1},{2,10},{10,2},{3,11},{11,3},{4,12},{12,4},... | collective-permute-start | bytes 1572872 | tf_op jit(solution)/shard_map/ppermute | solution.py:301
  40.8 3.4 %collective-permute-done.13.refs_4_ = bf16[512,256]{1,0:T(8,128)(2,1)S(1)} collective-permute-done((bf16[512,256]{1,0:T(8,128)(2,1)S(1)}, bf16[512,256]{1,0:T(8,128)(2,1)S(1)}, u32[]{:S(2)}, u32[]{:S(2)}) %collective-permute-start.13) | collective-permute-done | bytes 262176 | tf_op jit(solution)/shard_map/ppermute | solution.py:301
  45.6 2.3 %collective-permute-start.19 = (bf16[512,256]{1,0:T(8,128)(2,1)}, bf16[512,256]{1,0:T(8,128)(2,1)}, u32[]{:S(2)}, u32[]{:S(2)}) collective-permute-start(bf16[512,256]{1,0:T(8,128)(2,1)} %collective-permute-done.14.refs_5_), channel_id=1, source_target_pairs={{0,8},{8,0},{1,9},{9,1},{2,10},{10,2},{3,11},{11,3},{4,12},{12,4},... | collective-permute-start | bytes 786440 | tf_op jit(solution)/shard_map/ppermute | solution.py:301
  47.9 1.5 %collective-permute-done.19.refs_10_ = bf16[512,256]{1,0:T(8,128)(2,1)} collective-permute-done((bf16[512,256]{1,0:T(8,128)(2,1)}, bf16[512,256]{1,0:T(8,128)(2,1)}, u32[]{:S(2)}, u32[]{:S(2)}) %collective-permute-start.19) | collective-permute-done | bytes 262176 | tf_op jit(solution)/shard_map/ppermute | solution.py:301
  49.4 21.1 %shard_map.91 = bf16[256,1024]{1,0:T(8,128)(2,1)} custom-call(bf16[256,1024]{1,0:T(8,128)(2,1)S(1)} %bitcast.21, bf16[1024,256]{1,0:T(8,128)(2,1)S(1)} %pad_maximum_fusion.refs_1_, bf16[1024,256]{1,0:T(8,128)(2,1)S(1)} %collective-permute-done.11.refs_2_, bf16[1024,256]{1,0:T(8,128)(2,1)S(1)} %collective-permute-done.12.refs_3_, ...), custom_call_target="tpu_custom_call" | custom-call | flops 17179869184 | bytes 2097152 | tf_op jit(solution)/shard_map/pallas_call | solution.py:349
  70.5 7.6 %all-to-all-start.2 = ((bf16[32,8,1024]{2,1,0:T(8,128)(2,1)}), bf16[32,8,1024]{2,1,0:T(8,128)(2,1)S(1)}, u32[]{:S(2)}, u32[]{:S(2)}) async-start(bf16[32,8,1024]{2,1,0:T(8,128)(2,1)} %bitcast.7), calls=%async_computation.2 | async-start | bytes 1048576 | tf_op jit(solution)/shard_map/all_to_all | solution.py:305
  78.1 1.6 %shard_map.86 = (bf16[4,144,128]{2,1,0:T(8,128)(2,1)S(1)}, bf16[4,144,128]{2,1,0:T(8,128)(2,1)S(1)}) custom-call(bf16[256,1024]{1,0:T(8,128)(2,1)S(1)} %copy-done, bf16[256,1024]{1,0:T(8,128)(2,1)S(1)} %copy-done.1, f32[8,256]{1,0:T(8,128)S(1)} %copy-done.3), custom_call_target="tpu_custom_call" | custom-call | flops 268435456 | bytes 2097152 | tf_op jit(solution)/shard_map/pallas_call | solution.py:333
  81.8 2.0 %collective-permute-start.2 = (bf16[4,144,128]{2,1,0:T(8,128)(2,1)S(1)}, bf16[4,144,128]{2,1,0:T(8,128)(2,1)S(1)}, u32[]{:S(2)}, u32[]{:S(2)}) collective-permute-start(bf16[4,144,128]{2,1,0:T(8,128)(2,1)S(1)} %shard_map.87.own_ref), channel_id=1, source_target_pairs={{0,32},{16,48},{32,0},{48,16},{1,33},{17,49},{33,1},{49,17},{2,34}... | collective-permute-start | bytes 442376 | tf_op jit(solution)/shard_map/ppermute | solution.py:301
  83.9 2.8 %collective-permute-done.1.a_ref = bf16[4,144,128]{2,1,0:T(8,128)(2,1)S(1)} collective-permute-done((bf16[4,144,128]{2,1,0:T(8,128)(2,1)S(1)}, bf16[4,144,128]{2,1,0:T(8,128)(2,1)S(1)}, u32[]{:S(2)}, u32[]{:S(2)}) %collective-permute-start.1) | collective-permute-done | bytes 147488 | tf_op jit(solution)/shard_map/ppermute | solution.py:301
  86.7 1.4 %collective-permute-done.2.b_ref = bf16[4,144,128]{2,1,0:T(8,128)(2,1)S(1)} collective-permute-done((bf16[4,144,128]{2,1,0:T(8,128)(2,1)S(1)}, bf16[4,144,128]{2,1,0:T(8,128)(2,1)S(1)}, u32[]{:S(2)}, u32[]{:S(2)}) %collective-permute-start.2) | collective-permute-done | bytes 147488 | tf_op jit(solution)/shard_map/ppermute | solution.py:301
  88.1 3.7 %collective-permute-done.3.c_ref = bf16[4,144,128]{2,1,0:T(8,128)(2,1)S(1)} collective-permute-done((bf16[4,144,128]{2,1,0:T(8,128)(2,1)S(1)}, bf16[4,144,128]{2,1,0:T(8,128)(2,1)S(1)}, u32[]{:S(2)}, u32[]{:S(2)}) %collective-permute-start.3) | collective-permute-done | bytes 147488 | tf_op jit(solution)/shard_map/ppermute | solution.py:301
  92.1 1.4 %collective-permute-start.4 = (bf16[4,144,128]{2,1,0:T(8,128)(2,1)S(1)}, bf16[4,144,128]{2,1,0:T(8,128)(2,1)S(1)}, u32[]{:S(2)}, u32[]{:S(2)}) collective-permute-start(bf16[4,144,128]{2,1,0:T(8,128)(2,1)S(1)} %get-tuple-element.10), channel_id=1, source_target_pairs={{0,64},{64,128},{128,192},{1,65},{65,129},{129,193},{2,66},{66,130... | collective-permute-start | bytes 442376 | tf_op jit(solution)/shard_map/ppermute | solution.py:301
  96.1 2.5 %collective-permute-done.4.a_ref = bf16[4,144,128]{2,1,0:T(8,128)(2,1)S(1)} collective-permute-done((bf16[4,144,128]{2,1,0:T(8,128)(2,1)S(1)}, bf16[4,144,128]{2,1,0:T(8,128)(2,1)S(1)}, u32[]{:S(2)}, u32[]{:S(2)}) %collective-permute-start.4) | collective-permute-done | bytes 147488 | tf_op jit(solution)/shard_map/ppermute | solution.py:301
  98.6 2.8 %collective-permute-done.5.b_ref = bf16[4,144,128]{2,1,0:T(8,128)(2,1)S(1)} collective-permute-done((bf16[4,144,128]{2,1,0:T(8,128)(2,1)S(1)}, bf16[4,144,128]{2,1,0:T(8,128)(2,1)S(1)}, u32[]{:S(2)}, u32[]{:S(2)}) %collective-permute-start.5) | collective-permute-done | bytes 147488 | tf_op jit(solution)/shard_map/ppermute | solution.py:301
  101.4 3.2 %collective-permute-done.6.c_ref = bf16[4,144,128]{2,1,0:T(8,128)(2,1)S(1)} collective-permute-done((bf16[4,144,128]{2,1,0:T(8,128)(2,1)S(1)}, bf16[4,144,128]{2,1,0:T(8,128)(2,1)S(1)}, u32[]{:S(2)}, u32[]{:S(2)}) %collective-permute-start.6) | collective-permute-done | bytes 147488 | tf_op jit(solution)/shard_map/ppermute | solution.py:301
  104.8 1.8 %collective-permute-start.7 = (bf16[4,128,128]{2,1,0:T(8,128)(2,1)S(1)}, bf16[4,128,128]{2,1,0:T(8,128)(2,1)S(1)}, u32[]{:S(2)}, u32[]{:S(2)}) collective-permute-start(bf16[4,128,128]{2,1,0:T(8,128)(2,1)S(1)} %get-tuple-element.13), channel_id=1, source_target_pairs={{0,8},{8,0},{1,9},{9,1},{2,10},{10,2},{3,11},{11,3},{4,12},{12,4},... | collective-permute-start | bytes 393224 | tf_op jit(solution)/shard_map/ppermute | solution.py:301
  107.6 2.6 %shard_map.90 = bf16[256,1024]{1,0:T(8,128)(2,1)} custom-call(bf16[256,1024]{1,0:T(8,128)(2,1)S(1)} %copy-done.2, bf16[256,1024]{1,0:T(8,128)(2,1)S(1)} %copy-done, bf16[256,1024]{1,0:T(8,128)(2,1)S(1)} %copy-done.1, f32[8,256]{1,0:T(8,128)S(1)} %copy-done.3, f32[1,1024]{1,0:T(1,128)S(1)} %bitcast.22, bf16[4,128,128]{2,1,0:T(8,128)(2,1)S(1)} %get-tuple-element.12.keep_ref, ...), custom_call_target="tpu_custom_call" | custom-call | flops 536870912 | bytes 2097152 | tf_op jit(solution)/shard_map/pallas_call | solution.py:371
  (42 shorter events, 11.9 us)
Async XLA Ops:
  17.3 5.3 %collective-permute-start.10 = (bf16[256,256]{1,0:T(8,128)(2,1)S(1)}, bf16[256,256]{1,0:T(8,128)(2,1)S(1)}, u32[]{:S(2)}, u32[]{:S(2)}) collective-permute-start(bf16[256,256]{1,0:T(8,128)(2,1)S(1)} %bitcast.25), channel_id=1, source_target_pairs={{0,128},{8,40},{16,144},{24,56},{32,160},{40,8},{48,176},{56,24},{... | collective-permute-start | bytes 393224 | tf_op jit(solution)/shard_map/ppermute | solution.py:301
  18.2 4.4 %collective-permute-start.8 = (bf16[256,256]{1,0:T(8,128)(2,1)S(1)}, bf16[256,256]{1,0:T(8,128)(2,1)S(1)}, u32[]{:S(2)}, u32[]{:S(2)}) collective-permute-start(bf16[256,256]{1,0:T(8,128)(2,1)S(1)} %bitcast.26), channel_id=1, source_target_pairs={{0,64},{8,24},{16,80},{24,40},{32,96},{40,56},{48,112},{56,8},{64,... | collective-permute-start | bytes 393224 | tf_op jit(solution)/shard_map/ppermute | solution.py:301
  20.1 5.3 %collective-permute-start.9 = (bf16[256,256]{1,0:T(8,128)(2,1)S(1)}, bf16[256,256]{1,0:T(8,128)(2,1)S(1)}, u32[]{:S(2)}, u32[]{:S(2)}) collective-permute-start(bf16[256,256]{1,0:T(8,128)(2,1)S(1)} %bitcast.27), channel_id=1, source_target_pairs={{0,192},{8,56},{16,208},{24,8},{32,224},{40,24},{48,240},{56,40},{... | collective-permute-start | bytes 393224 | tf_op jit(solution)/shard_map/ppermute | solution.py:301
  25.5 10.7 %collective-permute-start.11 = (bf16[1024,256]{1,0:T(8,128)(2,1)S(1)}, bf16[1024,256]{1,0:T(8,128)(2,1)S(1)}, u32[]{:S(2)}, u32[]{:S(2)}) collective-permute-start(bf16[1024,256]{1,0:T(8,128)(2,1)S(1)} %pad_maximum_fusion.refs_1_), channel_id=1, source_target_pairs={{0,16},{8,72},{16,32},{24,88},{32,48},{40,104},{48,0},{56,120},{64... | collective-permute-start | bytes 1572872 | tf_op jit(solution)/shard_map/ppermute | solution.py:301
  25.8 10.6 %collective-permute-start.12 = (bf16[1024,256]{1,0:T(8,128)(2,1)S(1)}, bf16[1024,256]{1,0:T(8,128)(2,1)S(1)}, u32[]{:S(2)}, u32[]{:S(2)}) collective-permute-start(bf16[1024,256]{1,0:T(8,128)(2,1)S(1)} %pad_maximum_fusion.refs_1_), channel_id=1, source_target_pairs={{0,48},{8,200},{16,0},{24,216},{32,16},{40,232},{48,32},{56,248},{... | collective-permute-start | bytes 1572872 | tf_op jit(solution)/shard_map/ppermute | solution.py:301
  27.0 20.8 %all-to-all-start = ((bf16[32,8,1024]{2,1,0:T(8,128)(2,1)}), bf16[32,8,1024]{2,1,0:T(8,128)(2,1)S(1)}, u32[]{:S(2)}, u32[]{:S(2)}) async-start(bf16[32,8,1024]{2,1,0:T(8,128)(2,1)} %bitcast.3), calls=%async_computation | async-start | bytes 1048576 | tf_op jit(solution)/shard_map/all_to_all | solution.py:305
  32.2 15.7 %collective-permute-start.15 = (bf16[1024,256]{1,0:T(8,128)(2,1)S(1)}, bf16[1024,256]{1,0:T(8,128)(2,1)S(1)}, u32[]{:S(2)}, u32[]{:S(2)}) collective-permute-start(bf16[1024,256]{1,0:T(8,128)(2,1)S(1)} %pad_maximum_fusion.refs_1_), channel_id=1, source_target_pairs={{0,8},{8,0},{1,9},{9,1},{2,10},{10,2},{3,11},{11,3},{4,12},{12,4},... | collective-permute-start | bytes 1572872 | tf_op jit(solution)/shard_map/ppermute | solution.py:301
  36.2 8.0 %collective-permute-start.13 = (bf16[512,256]{1,0:T(8,128)(2,1)S(1)}, bf16[512,256]{1,0:T(8,128)(2,1)S(1)}, u32[]{:S(2)}, u32[]{:S(2)}) collective-permute-start(bf16[512,256]{1,0:T(8,128)(2,1)S(1)} %slice.8), channel_id=1, source_target_pairs={{0,16},{8,72},{16,32},{24,88},{32,48},{40,104},{48,0},{56,120},{64... | collective-permute-start | bytes 786440 | tf_op jit(solution)/shard_map/ppermute | solution.py:301
  36.4 9.2 %collective-permute-start.14 = (bf16[512,256]{1,0:T(8,128)(2,1)S(1)}, bf16[512,256]{1,0:T(8,128)(2,1)}, u32[]{:S(2)}, u32[]{:S(2)}) collective-permute-start(bf16[512,256]{1,0:T(8,128)(2,1)S(1)} %slice.9), channel_id=1, source_target_pairs={{0,48},{8,200},{16,0},{24,216},{32,16},{40,232},{48,32},{56,248},{... | collective-permute-start | bytes 786440 | tf_op jit(solution)/shard_map/ppermute | solution.py:301
  37.9 11.5 %collective-permute-start.16 = (bf16[1024,256]{1,0:T(8,128)(2,1)S(1)}, bf16[1024,256]{1,0:T(8,128)(2,1)S(1)}, u32[]{:S(2)}, u32[]{:S(2)}) collective-permute-start(bf16[1024,256]{1,0:T(8,128)(2,1)S(1)} %collective-permute-done.11.refs_2_), channel_id=1, source_target_pairs={{0,8},{8,0},{1,9},{9,1},{2,10},{10,2},{3,11},{11,3},{4,12},{12,4},... | collective-permute-start | bytes 1572872 | tf_op jit(solution)/shard_map/ppermute | solution.py:301
  40.8 8.6 %collective-permute-start.17 = (bf16[1024,256]{1,0:T(8,128)(2,1)S(1)}, bf16[1024,256]{1,0:T(8,128)(2,1)}, u32[]{:S(2)}, u32[]{:S(2)}) collective-permute-start(bf16[1024,256]{1,0:T(8,128)(2,1)S(1)} %collective-permute-done.12.refs_3_), channel_id=1, source_target_pairs={{0,8},{8,0},{1,9},{9,1},{2,10},{10,2},{3,11},{11,3},{4,12},{12,4},... | collective-permute-start | bytes 1572872 | tf_op jit(solution)/shard_map/ppermute | solution.py:301
  44.2 3.7 %collective-permute-start.18 = (bf16[512,256]{1,0:T(8,128)(2,1)S(1)}, bf16[512,256]{1,0:T(8,128)(2,1)}, u32[]{:S(2)}, u32[]{:S(2)}) collective-permute-start(bf16[512,256]{1,0:T(8,128)(2,1)S(1)} %collective-permute-done.13.refs_4_), channel_id=1, source_target_pairs={{0,8},{8,0},{1,9},{9,1},{2,10},{10,2},{3,11},{11,3},{4,12},{12,4},... | collective-permute-start | bytes 786440 | tf_op jit(solution)/shard_map/ppermute | solution.py:301
  45.6 3.8 %collective-permute-start.19 = (bf16[512,256]{1,0:T(8,128)(2,1)}, bf16[512,256]{1,0:T(8,128)(2,1)}, u32[]{:S(2)}, u32[]{:S(2)}) collective-permute-start(bf16[512,256]{1,0:T(8,128)(2,1)} %collective-permute-done.14.refs_5_), channel_id=1, source_target_pairs={{0,8},{8,0},{1,9},{9,1},{2,10},{10,2},{3,11},{11,3},{4,12},{12,4},... | collective-permute-start | bytes 786440 | tf_op jit(solution)/shard_map/ppermute | solution.py:301
  49.4 28.7 %copy-start.3 = (f32[8,256]{1,0:T(8,128)S(1)}, f32[8,256]{1,0:T(8,128)}, u32[]{:S(2)}) copy-start(f32[8,256]{1,0:T(8,128)} %g_ref.3) | copy-start | bytes 24580
  70.5 39.7 %all-to-all-start.2 = ((bf16[32,8,1024]{2,1,0:T(8,128)(2,1)}), bf16[32,8,1024]{2,1,0:T(8,128)(2,1)S(1)}, u32[]{:S(2)}, u32[]{:S(2)}) async-start(bf16[32,8,1024]{2,1,0:T(8,128)(2,1)} %bitcast.7), calls=%async_computation.2 | async-start | bytes 1048576 | tf_op jit(solution)/shard_map/all_to_all | solution.py:305
  79.7 1.8 %collective-permute-start = (bf16[4,144,128]{2,1,0:T(8,128)(2,1)S(1)}, bf16[4,144,128]{2,1,0:T(8,128)(2,1)S(1)}, u32[]{:S(2)}, u32[]{:S(2)}) collective-permute-start(bf16[4,144,128]{2,1,0:T(8,128)(2,1)S(1)} %get-tuple-element.9), channel_id=1, source_target_pairs={{0,8},{8,0},{1,9},{9,1},{2,10},{10,2},{3,11},{11,3},{4,12},{12,4},... | collective-permute-start | bytes 442376 | tf_op jit(solution)/shard_map/ppermute | solution.py:301
  81.6 5.1 %collective-permute-start.1 = (bf16[4,144,128]{2,1,0:T(8,128)(2,1)S(1)}, bf16[4,144,128]{2,1,0:T(8,128)(2,1)S(1)}, u32[]{:S(2)}, u32[]{:S(2)}) collective-permute-start(bf16[4,144,128]{2,1,0:T(8,128)(2,1)S(1)} %shard_map.87.own_ref), channel_id=1, source_target_pairs={{0,16},{16,32},{32,48},{48,0},{1,17},{17,33},{33,49},{49,1},{2,18}... | collective-permute-start | bytes 442376 | tf_op jit(solution)/shard_map/ppermute | solution.py:301
  81.8 6.3 %collective-permute-start.2 = (bf16[4,144,128]{2,1,0:T(8,128)(2,1)S(1)}, bf16[4,144,128]{2,1,0:T(8,128)(2,1)S(1)}, u32[]{:S(2)}, u32[]{:S(2)}) collective-permute-start(bf16[4,144,128]{2,1,0:T(8,128)(2,1)S(1)} %shard_map.87.own_ref), channel_id=1, source_target_pairs={{0,32},{16,48},{32,0},{48,16},{1,33},{17,49},{33,1},{49,17},{2,34}... | collective-permute-start | bytes 442376 | tf_op jit(solution)/shard_map/ppermute | solution.py:301
  83.9 8.0 %collective-permute-start.3 = (bf16[4,144,128]{2,1,0:T(8,128)(2,1)S(1)}, bf16[4,144,128]{2,1,0:T(8,128)(2,1)S(1)}, u32[]{:S(2)}, u32[]{:S(2)}) collective-permute-start(bf16[4,144,128]{2,1,0:T(8,128)(2,1)S(1)} %shard_map.87.own_ref), channel_id=1, source_target_pairs={{0,48},{16,0},{32,16},{48,32},{1,49},{17,1},{33,17},{49,33},{2,50}... | collective-permute-start | bytes 442376 | tf_op jit(solution)/shard_map/ppermute | solution.py:301
  92.1 15.6 %copy-start.2 = (bf16[256,1024]{1,0:T(8,128)(2,1)S(1)}, bf16[256,1024]{1,0:T(8,128)(2,1)}, u32[]{:S(2)}) copy-start(bf16[256,1024]{1,0:T(8,128)(2,1)} %q_ref.1) | copy-start | bytes 1572868
  92.1 6.5 %collective-permute-start.4 = (bf16[4,144,128]{2,1,0:T(8,128)(2,1)S(1)}, bf16[4,144,128]{2,1,0:T(8,128)(2,1)S(1)}, u32[]{:S(2)}, u32[]{:S(2)}) collective-permute-start(bf16[4,144,128]{2,1,0:T(8,128)(2,1)S(1)} %get-tuple-element.10), channel_id=1, source_target_pairs={{0,64},{64,128},{128,192},{1,65},{65,129},{129,193},{2,66},{66,130... | collective-permute-start | bytes 442376 | tf_op jit(solution)/shard_map/ppermute | solution.py:301
  93.5 7.9 %collective-permute-start.5 = (bf16[4,144,128]{2,1,0:T(8,128)(2,1)S(1)}, bf16[4,144,128]{2,1,0:T(8,128)(2,1)S(1)}, u32[]{:S(2)}, u32[]{:S(2)}) collective-permute-start(bf16[4,144,128]{2,1,0:T(8,128)(2,1)S(1)} %get-tuple-element.10), channel_id=1, source_target_pairs={{0,128},{64,192},{1,129},{65,193},{2,130},{66,194},{3,131},{67,195... | collective-permute-start | bytes 442376 | tf_op jit(solution)/shard_map/ppermute | solution.py:301
  94.8 9.8 %collective-permute-start.6 = (bf16[4,144,128]{2,1,0:T(8,128)(2,1)S(1)}, bf16[4,144,128]{2,1,0:T(8,128)(2,1)S(1)}, u32[]{:S(2)}, u32[]{:S(2)}) collective-permute-start(bf16[4,144,128]{2,1,0:T(8,128)(2,1)S(1)} %get-tuple-element.10), channel_id=1, source_target_pairs={{0,192},{1,193},{2,194},{3,195},{4,196},{5,197},{6,198},{7,199},{8... | collective-permute-start | bytes 442376 | tf_op jit(solution)/shard_map/ppermute | solution.py:301
  104.8 2.8 %collective-permute-start.7 = (bf16[4,128,128]{2,1,0:T(8,128)(2,1)S(1)}, bf16[4,128,128]{2,1,0:T(8,128)(2,1)S(1)}, u32[]{:S(2)}, u32[]{:S(2)}) collective-permute-start(bf16[4,128,128]{2,1,0:T(8,128)(2,1)S(1)} %get-tuple-element.13), channel_id=1, source_target_pairs={{0,8},{8,0},{1,9},{9,1},{2,10},{10,2},{3,11},{11,3},{4,12},{12,4},... | collective-permute-start | bytes 393224 | tf_op jit(solution)/shard_map/ppermute | solution.py:301
  (3 other events, 18.0 us)

commit v5 on v4

--- a/solution.py
+++ b/solution.py
@@ -47,18 +47,18 @@
     return jnp.where(row == 0, high, jnp.where(row == 1, total - high, 0.0)).astype(jnp.bfloat16)
 
 
-def read_total(ref, h):
-    rows = ref[h, DIM : DIM + TOTAL, :].astype(jnp.float32)
+def read_total(ref):
+    rows = ref[DIM : DIM + TOTAL, :].astype(jnp.float32)
     return rows[0:1] + rows[1:2]
 
 
-def read_state(ref, h):
-    return ref[h, 0:DIM, :].astype(jnp.float32)
-
-
-def write(ref, h, state, total):
-    ref[h, 0:DIM, :] = state.astype(jnp.bfloat16)
-    ref[h, DIM : DIM + TOTAL, :] = total_rows(total)
+def read_state(ref):
+    return ref[0:DIM, :].astype(jnp.float32)
+
+
+def write(ref, state, total):
+    ref[0:DIM, :] = state.astype(jnp.bfloat16)
+    ref[DIM : DIM + TOTAL, :] = total_rows(total)
 
 
 def local_state_kernel(k_ref, v_ref, g_ref, mine_ref, theirs_ref):
@@ -77,59 +77,69 @@
         low, low_total = local(h)
         high, high_total = local(HALF + h)
         write(
-            mine_ref, h, jnp.where(first, low, high), jnp.where(first, low_total, high_total)
+            mine_ref.at[h], jnp.where(first, low, high), jnp.where(first, low_total, high_total)
         )
         write(
-            theirs_ref, h, jnp.where(first, high, low), jnp.where(first, high_total, low_total)
+            theirs_ref.at[h], jnp.where(first, high, low), jnp.where(first, high_total, low_total)
         )
 
 
-def in_order(core, mine_ref, other_ref, h):
-    a, b = read_state(mine_ref, h), read_state(other_ref, h)
-    ta, tb = read_total(mine_ref, h), read_total(other_ref, h)
-    own = core == 0
-    return jnp.where(own, a, b), jnp.where(own, ta, tb), jnp.where(own, b, a), jnp.where(own, tb, ta)
-
-
-def chip_state_kernel(mine_ref, other_ref, chip_ref):
-    core = lax.axis_index("ctx_2")
-    for h in range(HALF):
-        s0, t0, s1, t1 = in_order(core, mine_ref, other_ref, h)
-        write(chip_ref, h, jnp.exp(t1) * s0 + s1, t0 + t1)
+def in_order(first, mine_ref, other_ref):
+    a, b = read_state(mine_ref), read_state(other_ref)
+    ta, tb = read_total(mine_ref), read_total(other_ref)
+    return (
+        jnp.where(first, a, b),
+        jnp.where(first, ta, tb),
+        jnp.where(first, b, a),
+        jnp.where(first, tb, ta),
+    )
+
+
+def chip_state_kernel(mine_ref, other_ref, *chip_refs):
+    my, first = lax.axis_index("ctx_1"), lax.axis_index("ctx_2") == 0
+    for d, chip_ref in enumerate(chip_refs):
+        h = (my + d) % NY
+        s0, t0, s1, t1 = in_order(first, mine_ref.at[h], other_ref.at[h])
+        write(chip_ref, jnp.exp(t1) * s0 + s1, t0 + t1)
 
 
 def row_state_kernel(own_ref, a_ref, b_ref, c_ref, row_ref, before_ref, all_ref):
     my = lax.axis_index("ctx_1")
     for d, ref in enumerate((own_ref, a_ref, b_ref, c_ref)):
         all_ref[(my + NY - d) % NY] = ref[...]
-    for h in range(HALF):
-        state = jnp.zeros((DIM, DIM), jnp.float32)
-        total = jnp.zeros((1, DIM), jnp.float32)
-        before, before_total = state, total
-        for y in range(NY):
-            here = my == y
-            before = jnp.where(here, state, before)
-            before_total = jnp.where(here, total, before_total)
-            t = read_total(all_ref.at[y], h)
-            state = jnp.exp(t) * state + read_state(all_ref.at[y], h)
-            total = total + t
-        write(row_ref, h, state, total)
-        before_ref[h, 0:DIM, :] = before
-        before_ref[h, DIM : DIM + 8, :] = jnp.broadcast_to(before_total, (8, DIM))
-
-
-def entering_kernel(a_ref, b_ref, c_ref, before_ref, mine_ref, other_ref, keep_ref, send_ref):
-    mx, core = lax.axis_index("ctx_0"), lax.axis_index("ctx_2")
-    for h in range(HALF):
-        state = jnp.zeros((DIM, DIM), jnp.float32)
-        for d, ref in ((3, c_ref), (2, b_ref), (1, a_ref)):
-            new = jnp.exp(read_total(ref, h)) * state + read_state(ref, h)
-            state = jnp.where(mx >= d, new, state)
-        state = jnp.exp(before_ref[h, DIM : DIM + 1, :]) * state + before_ref[h, 0:DIM, :]
-        s0, t0, _, _ = in_order(core, mine_ref, other_ref, h)
+    state = jnp.zeros((DIM, DIM), jnp.float32)
+    total = jnp.zeros((1, DIM), jnp.float32)
+    for y in range(NY):
+        before_ref[y, 0:DIM, :] = state
+        before_ref[y, DIM : DIM + 8, :] = jnp.broadcast_to(total, (8, DIM))
+        t = read_total(all_ref.at[y])
+        state = jnp.exp(t) * state + read_state(all_ref.at[y])
+        total = total + t
+    write(row_ref, state, total)
+
+
+def enter_row_kernel(a_ref, b_ref, c_ref, before_ref, *out_refs):
+    mx, my = lax.axis_index("ctx_0"), lax.axis_index("ctx_1")
+    state = jnp.zeros((DIM, DIM), jnp.float32)
+    for d, ref in ((3, c_ref), (2, b_ref), (1, a_ref)):
+        new = jnp.exp(read_total(ref)) * state + read_state(ref)
+        state = jnp.where(mx >= d, new, state)
+    for d, out_ref in enumerate(out_refs):
+        y = (my + d) % NY
+        before = before_ref[y]
+        out = jnp.exp(before[DIM : DIM + 1]) * state + before[0:DIM]
+        out_ref[...] = out.astype(jnp.bfloat16)
+
+
+def enter_chunk_kernel(e0_ref, e1_ref, e2_ref, e3_ref, mine_ref, other_ref, keep_ref, send_ref):
+    my, first = lax.axis_index("ctx_1"), lax.axis_index("ctx_2") == 0
+    for d, ref in enumerate((e0_ref, e1_ref, e2_ref, e3_ref)):
+        h = (my + NY - d) % NY
+        state = ref[...].astype(jnp.float32)
+        s0, t0, _, _ = in_order(first, mine_ref.at[h], other_ref.at[h])
         later = jnp.exp(t0) * state + s0
-        keep_ref[h] = jnp.where(core == 0, state, later).astype(jnp.bfloat16)
-        send_ref[h] = jnp.where(core == 0, later, state).astype(jnp.bfloat16)
+        keep_ref[h] = jnp.where(first, state, later).astype(jnp.bfloat16)
+        send_ref[h] = jnp.where(first, later, state).astype(jnp.bfloat16)
 
 
 def lightning_kernel(q_ref, k_ref, v_ref, g_ref, gain_ref, keep_ref, got_ref, out_ref):
@@ -327,22 +337,33 @@
     pieces = gather_kv(kv)
 
     swap = [(0, 1), (1, 0)]
-    msg = (HALF, DIM + TOTAL, DIM)
-    msg16 = (msg, jnp.bfloat16)
-    entering = ((HALF, DIM, DIM), jnp.bfloat16)
-    mine, theirs = call(local_state_kernel, [msg16] * 2, 3, 1 << 28)(lin_k, lin_v, log_decay)
+    head = (DIM + TOTAL, DIM)
+    heads = ((HALF, *head), jnp.bfloat16)
+    one = (head, jnp.bfloat16)
+
+    def send_y(values):
+        return [
+            permute(v, [(y, (y + d) % NY) for y in range(NY)], "ctx_1")
+            for d, v in enumerate(values)
+            if d > 0
+        ]
+
+    mine, theirs = call(local_state_kernel, [heads] * 2, 3, 1 << 28)(lin_k, lin_v, log_decay)
     other = permute(theirs, swap, "ctx_2")
-    (chip,) = call(chip_state_kernel, [msg16], 2, 1 << 20)(mine, other)
-    around = [permute(chip, [(y, (y + d) % NY) for y in range(NY)], "ctx_1") for d in (1, 2, 3)]
+    chip = call(chip_state_kernel, [one] * NY, 2, 1 << 20)(mine, other)
     row_state, before = call(
         row_state_kernel,
-        [msg16, (msg, jnp.float32)],
+        [one, ((NY, DIM + 8, DIM), jnp.float32)],
         4,
         1 << 20,
-        scratch_shapes=[pltpu.VMEM((NY, *msg), jnp.bfloat16)],
-    )(chip, *around)
+        scratch_shapes=[pltpu.VMEM((NY, *head), jnp.bfloat16)],
+    )(chip[0], *send_y(chip))
     earlier = [permute(row_state, [(x, x + d) for x in range(NX - d)], "ctx_0") for d in (1, 2, 3)]
-    keep, send = call(entering_kernel, [entering] * 2, 6, 1 << 20)(*earlier, before, mine, other)
+    enter = call(enter_row_kernel, [((DIM, DIM), jnp.bfloat16)] * NY, 4, 1 << 20)(*earlier, before)
+    entering = ((HALF, DIM, DIM), jnp.bfloat16)
+    keep, send = call(enter_chunk_kernel, [entering] * 2, 6, 1 << 20)(
+        enter[0], *send_y(enter), mine, other
+    )
     got = permute(send, swap, "ctx_2")
 
     block = ((CH, HEADS * DIM), jnp.bfloat16)

time: 112 us -> 114 us (1.018)
  starting transfers between devices: 37.6 us -> 40.5 us
    ppermute x20 -> x23, starting transfers between devices: 25 us -> 27.4 us  [permute(): return lax.ppermute(value, axes, pairs)]
    ppermute x20 -> x23, waiting for transfers between devices: 29.2 us -> 28.3 us  [permute(): return lax.ppermute(value, axes, pairs)]
  transfers between devices with their start and end apart: 22 -> 25, of which waited for: 13 -> 17; matrix products, arithmetic and copies ran while one was open for 0% -> 0% of each run, Pallas kernels for 4% -> 4%
where the time goes in v5:
time: 114 us; the launch traced here: 113 us
  starting transfers between devices  40.5 us (36%)
  waiting for transfers between devices  28.3 us (25%)
  Pallas kernels  25.6 us (22%)
  blocking collectives  15.7 us (14%)
  local copies, waits for them, and re-layouts  1.77 us (2%)
    ppermute x23, waiting for transfers between devices, permute(): return lax.ppermute(value, axes, pairs)  28.3 us
    ppermute x23, starting transfers between devices, permute(): return lax.ppermute(value, axes, pairs)  27.4 us
    pallas_call x1, Pallas kernels, both(): call(softmax_kernel, [block], 11, 1 << 34, in_specs=vmem(1) + [pl.BlockSp...  21.1 us
    all_to_all x1, blocking collectives, exchange(): return lax.all_to_all(value, axes, 0, 0, tiled=True)  15.7 us
    all_to_all x2, starting transfers between devices, exchange(): return lax.all_to_all(value, axes, 0, 0, tiled=True)  13.1 us
    pallas_call x1, Pallas kernels, both(): call(lightning_kernel, [block], 7, 1 << 29)  2.6 us
  transfers between devices with their start and end apart: 25, of which 17 were waited for; matrix products, arithmetic and copies ran while one was open for 0% of the time, Pallas kernels for 4%

profile of v5, /device:TPU:31, one launch (start us, length us, event | category | flops | bytes accessed | tf_op | source)
XLA Modules:
  0.0 112.8 jit_solution(5317968777211826880)
XLA Ops:
  1.5 15.7 %all_to_all.15 = bf16[8,32,256]{2,1,0:T(8,128)(2,1)S(1)} all-to-all(bf16[8,32,256]{2,1,0:T(8,128)(2,1)S(1)} %bitcast.24), channel_id=1, replica_groups=mesh['ctx_0'=4,'ctx_1'=4,'ctx_2'=2,'head'=8] {'head'}, dimensions={0} | all-to-all | bytes 262144 | tf_op jit(solution)/shard_map/all_to_all | solution.py:315
  17.3 1.5 %collective-permute-start.12 = (bf16[256,256]{1,0:T(8,128)(2,1)S(1)}, bf16[256,256]{1,0:T(8,128)(2,1)S(1)}, u32[]{:S(2)}, u32[]{:S(2)}) collective-permute-start(bf16[256,256]{1,0:T(8,128)(2,1)S(1)} %bitcast.26), channel_id=1, source_target_pairs={{0,192},{8,56},{16,208},{24,8},{32,224},{40,24},{48,240},{56,40},{... | collective-permute-start | bytes 393224 | tf_op jit(solution)/shard_map/ppermute | solution.py:311
  19.7 1.4 %collective-permute-done.11 = bf16[256,256]{1,0:T(8,128)(2,1)S(1)} collective-permute-done((bf16[256,256]{1,0:T(8,128)(2,1)S(1)}, bf16[256,256]{1,0:T(8,128)(2,1)S(1)}, u32[]{:S(2)}, u32[]{:S(2)}) %collective-permute-start.11) | collective-permute-done | bytes 131104 | tf_op jit(solution)/shard_map/ppermute | solution.py:311
  22.3 1.8 %collective-permute-done.13 = bf16[256,256]{1,0:T(8,128)(2,1)S(1)} collective-permute-done((bf16[256,256]{1,0:T(8,128)(2,1)S(1)}, bf16[256,256]{1,0:T(8,128)(2,1)S(1)}, u32[]{:S(2)}, u32[]{:S(2)}) %collective-permute-start.13) | collective-permute-done | bytes 131104 | tf_op jit(solution)/shard_map/ppermute | solution.py:311
  25.7 5.1 %all-to-all-start = ((bf16[32,8,1024]{2,1,0:T(8,128)(2,1)}), bf16[32,8,1024]{2,1,0:T(8,128)(2,1)S(1)}, u32[]{:S(2)}, u32[]{:S(2)}) async-start(bf16[32,8,1024]{2,1,0:T(8,128)(2,1)} %bitcast.3), calls=%async_computation | async-start | bytes 1048576 | tf_op jit(solution)/shard_map/all_to_all | solution.py:315
  30.8 5.3 %collective-permute-start.18 = (bf16[1024,256]{1,0:T(8,128)(2,1)S(1)}, bf16[1024,256]{1,0:T(8,128)(2,1)S(1)}, u32[]{:S(2)}, u32[]{:S(2)}) collective-permute-start(bf16[1024,256]{1,0:T(8,128)(2,1)S(1)} %pad_maximum_fusion.refs_1_), channel_id=1, source_target_pairs={{0,8},{8,0},{1,9},{9,1},{2,10},{10,2},{3,11},{11,3},{4,12},{12,4},... | collective-permute-start | bytes 1572872 | tf_op jit(solution)/shard_map/ppermute | solution.py:311
  36.3 1.5 %collective-permute-start.17 = (bf16[512,256]{1,0:T(8,128)(2,1)S(1)}, bf16[512,256]{1,0:T(8,128)(2,1)}, u32[]{:S(2)}, u32[]{:S(2)}) collective-permute-start(bf16[512,256]{1,0:T(8,128)(2,1)S(1)} %slice.9), channel_id=1, source_target_pairs={{0,48},{8,200},{16,0},{24,216},{32,16},{40,232},{48,32},{56,248},{... | collective-permute-start | bytes 786440 | tf_op jit(solution)/shard_map/ppermute | solution.py:311
  37.8 1.8 %collective-permute-start.19 = (bf16[1024,256]{1,0:T(8,128)(2,1)S(1)}, bf16[1024,256]{1,0:T(8,128)(2,1)S(1)}, u32[]{:S(2)}, u32[]{:S(2)}) collective-permute-start(bf16[1024,256]{1,0:T(8,128)(2,1)S(1)} %collective-permute-done.14.refs_2_), channel_id=1, source_target_pairs={{0,8},{8,0},{1,9},{9,1},{2,10},{10,2},{3,11},{11,3},{4,12},{12,4},... | collective-permute-start | bytes 1572872 | tf_op jit(solution)/shard_map/ppermute | solution.py:311
  39.6 4.4 %collective-permute-done.16.refs_4_ = bf16[512,256]{1,0:T(8,128)(2,1)S(1)} collective-permute-done((bf16[512,256]{1,0:T(8,128)(2,1)S(1)}, bf16[512,256]{1,0:T(8,128)(2,1)S(1)}, u32[]{:S(2)}, u32[]{:S(2)}) %collective-permute-start.16) | collective-permute-done | bytes 262176 | tf_op jit(solution)/shard_map/ppermute | solution.py:311
  45.1 1.6 %collective-permute-start.22 = (bf16[512,256]{1,0:T(8,128)(2,1)}, bf16[512,256]{1,0:T(8,128)(2,1)}, u32[]{:S(2)}, u32[]{:S(2)}) collective-permute-start(bf16[512,256]{1,0:T(8,128)(2,1)} %collective-permute-done.17.refs_5_), channel_id=1, source_target_pairs={{0,8},{8,0},{1,9},{9,1},{2,10},{10,2},{3,11},{11,3},{4,12},{12,4},... | collective-permute-start | bytes 786440 | tf_op jit(solution)/shard_map/ppermute | solution.py:311
  46.7 1.5 %collective-permute-done.22.refs_10_ = bf16[512,256]{1,0:T(8,128)(2,1)} collective-permute-done((bf16[512,256]{1,0:T(8,128)(2,1)}, bf16[512,256]{1,0:T(8,128)(2,1)}, u32[]{:S(2)}, u32[]{:S(2)}) %collective-permute-start.22) | collective-permute-done | bytes 262176 | tf_op jit(solution)/shard_map/ppermute | solution.py:311
  48.2 21.1 %shard_map.92 = bf16[256,1024]{1,0:T(8,128)(2,1)} custom-call(bf16[256,1024]{1,0:T(8,128)(2,1)S(1)} %bitcast.21, bf16[1024,256]{1,0:T(8,128)(2,1)S(1)} %pad_maximum_fusion.refs_1_, bf16[1024,256]{1,0:T(8,128)(2,1)S(1)} %collective-permute-done.14.refs_2_, bf16[1024,256]{1,0:T(8,128)(2,1)S(1)} %collective-permute-done.15.refs_3_, ...), custom_call_target="tpu_custom_call" | custom-call | flops 17179869184 | bytes 2097152 | tf_op jit(solution)/shard_map/pallas_call | solution.py:370
  69.4 8.0 %all-to-all-start.2 = ((bf16[32,8,1024]{2,1,0:T(8,128)(2,1)}), bf16[32,8,1024]{2,1,0:T(8,128)(2,1)S(1)}, u32[]{:S(2)}, u32[]{:S(2)}) async-start(bf16[32,8,1024]{2,1,0:T(8,128)(2,1)} %bitcast.7), calls=%async_computation.2 | async-start | bytes 1048576 | tf_op jit(solution)/shard_map/all_to_all | solution.py:315
  77.4 1.6 %shard_map.86 = (bf16[4,144,128]{2,1,0:T(8,128)(2,1)S(1)}, bf16[4,144,128]{2,1,0:T(8,128)(2,1)S(1)}) custom-call(bf16[256,1024]{1,0:T(8,128)(2,1)S(1)} %copy-done, bf16[256,1024]{1,0:T(8,128)(2,1)S(1)} %copy-done.1, f32[8,256]{1,0:T(8,128)S(1)} %copy-done.3), custom_call_target="tpu_custom_call" | custom-call | flops 268435456 | bytes 2097152 | tf_op jit(solution)/shard_map/pallas_call | solution.py:351
  83.0 1.3 %collective-permute-done.1.a_ref = bf16[144,128]{1,0:T(8,128)(2,1)S(1)} collective-permute-done((bf16[144,128]{1,0:T(8,128)(2,1)S(1)}, bf16[144,128]{1,0:T(8,128)(2,1)S(1)}, u32[]{:S(2)}, u32[]{:S(2)}) %collective-permute-start.1) | collective-permute-done | bytes 36896 | tf_op jit(solution)/shard_map/ppermute | solution.py:311
  84.3 2.0 %collective-permute-done.2.b_ref = bf16[144,128]{1,0:T(8,128)(2,1)S(1)} collective-permute-done((bf16[144,128]{1,0:T(8,128)(2,1)S(1)}, bf16[144,128]{1,0:T(8,128)(2,1)S(1)}, u32[]{:S(2)}, u32[]{:S(2)}) %collective-permute-start.2) | collective-permute-done | bytes 36896 | tf_op jit(solution)/shard_map/ppermute | solution.py:311
  86.3 1.4 %collective-permute-done.3.c_ref = bf16[144,128]{1,0:T(8,128)(2,1)S(1)} collective-permute-done((bf16[144,128]{1,0:T(8,128)(2,1)S(1)}, bf16[144,128]{1,0:T(8,128)(2,1)S(1)}, u32[]{:S(2)}, u32[]{:S(2)}) %collective-permute-start.3) | collective-permute-done | bytes 36896 | tf_op jit(solution)/shard_map/ppermute | solution.py:311
  87.7 1.3 %collective-permute-start.4 = (bf16[144,128]{1,0:T(8,128)(2,1)S(1)}, bf16[144,128]{1,0:T(8,128)(2,1)S(1)}, u32[]{:S(2)}, u32[]{:S(2)}) collective-permute-start(bf16[144,128]{1,0:T(8,128)(2,1)S(1)} %get-tuple-element.22), channel_id=1, source_target_pairs={{0,64},{64,128},{128,192},{1,65},{65,129},{129,193},{2,66},{66,130... | collective-permute-start | bytes 110600 | tf_op jit(solution)/shard_map/ppermute | solution.py:311
  92.8 2.4 %collective-permute-done.5.b_ref = bf16[144,128]{1,0:T(8,128)(2,1)S(1)} collective-permute-done((bf16[144,128]{1,0:T(8,128)(2,1)S(1)}, bf16[144,128]{1,0:T(8,128)(2,1)S(1)}, u32[]{:S(2)}, u32[]{:S(2)}) %collective-permute-start.5) | collective-permute-done | bytes 36896 | tf_op jit(solution)/shard_map/ppermute | solution.py:311
  95.2 2.8 %collective-permute-done.6.c_ref = bf16[144,128]{1,0:T(8,128)(2,1)S(1)} collective-permute-done((bf16[144,128]{1,0:T(8,128)(2,1)S(1)}, bf16[144,128]{1,0:T(8,128)(2,1)S(1)}, u32[]{:S(2)}, u32[]{:S(2)}) %collective-permute-start.6) | collective-permute-done | bytes 36896 | tf_op jit(solution)/shard_map/ppermute | solution.py:311
  99.7 1.3 %collective-permute-done.7.e1_ref = bf16[128,128]{1,0:T(8,128)(2,1)S(1)} collective-permute-done((bf16[128,128]{1,0:T(8,128)(2,1)S(1)}, bf16[128,128]{1,0:T(8,128)(2,1)S(1)}, u32[]{:S(2)}, u32[]{:S(2)}) %collective-permute-start.7) | collective-permute-done | bytes 32800 | tf_op jit(solution)/shard_map/ppermute | solution.py:311
  100.9 2.0 %collective-permute-done.8.e2_ref = bf16[128,128]{1,0:T(8,128)(2,1)S(1)} collective-permute-done((bf16[128,128]{1,0:T(8,128)(2,1)S(1)}, bf16[128,128]{1,0:T(8,128)(2,1)S(1)}, u32[]{:S(2)}, u32[]{:S(2)}) %collective-permute-start.8) | collective-permute-done | bytes 32800 | tf_op jit(solution)/shard_map/ppermute | solution.py:311
  103.7 4.7 %collective-permute-start.10 = (bf16[4,128,128]{2,1,0:T(8,128)(2,1)S(1)}, bf16[4,128,128]{2,1,0:T(8,128)(2,1)S(1)}, u32[]{:S(2)}, u32[]{:S(2)}) collective-permute-start(bf16[4,128,128]{2,1,0:T(8,128)(2,1)S(1)} %get-tuple-element.29), channel_id=1, source_target_pairs={{0,8},{8,0},{1,9},{9,1},{2,10},{10,2},{3,11},{11,3},{4,12},{12,4},... | collective-permute-start | bytes 393224 | tf_op jit(solution)/shard_map/ppermute | solution.py:311
  109.4 2.6 %shard_map.91 = bf16[256,1024]{1,0:T(8,128)(2,1)} custom-call(bf16[256,1024]{1,0:T(8,128)(2,1)S(1)} %copy-done.2, bf16[256,1024]{1,0:T(8,128)(2,1)S(1)} %copy-done, bf16[256,1024]{1,0:T(8,128)(2,1)S(1)} %copy-done.1, f32[8,256]{1,0:T(8,128)S(1)} %copy-done.3, f32[1,1024]{1,0:T(1,128)S(1)} %bitcast.22, bf16[4,128,128]{2,1,0:T(8,128)(2,1)S(1)} %get-tuple-element.28.keep_ref, ...), custom_call_target="tpu_custom_call" | custom-call | flops 536870912 | bytes 2097152 | tf_op jit(solution)/shard_map/pallas_call | solution.py:392
  (49 shorter events, 17.8 us)
Async XLA Ops:
  17.3 3.8 %collective-permute-start.11 = (bf16[256,256]{1,0:T(8,128)(2,1)S(1)}, bf16[256,256]{1,0:T(8,128)(2,1)S(1)}, u32[]{:S(2)}, u32[]{:S(2)}) collective-permute-start(bf16[256,256]{1,0:T(8,128)(2,1)S(1)} %bitcast.25), channel_id=1, source_target_pairs={{0,64},{8,24},{16,80},{24,40},{32,96},{40,56},{48,112},{56,8},{64,... | collective-permute-start | bytes 393224 | tf_op jit(solution)/shard_map/ppermute | solution.py:311
  17.3 5.0 %collective-permute-start.12 = (bf16[256,256]{1,0:T(8,128)(2,1)S(1)}, bf16[256,256]{1,0:T(8,128)(2,1)S(1)}, u32[]{:S(2)}, u32[]{:S(2)}) collective-permute-start(bf16[256,256]{1,0:T(8,128)(2,1)S(1)} %bitcast.26), channel_id=1, source_target_pairs={{0,192},{8,56},{16,208},{24,8},{32,224},{40,24},{48,240},{56,40},{... | collective-permute-start | bytes 393224 | tf_op jit(solution)/shard_map/ppermute | solution.py:311
  18.7 5.3 %collective-permute-start.13 = (bf16[256,256]{1,0:T(8,128)(2,1)S(1)}, bf16[256,256]{1,0:T(8,128)(2,1)S(1)}, u32[]{:S(2)}, u32[]{:S(2)}) collective-permute-start(bf16[256,256]{1,0:T(8,128)(2,1)S(1)} %bitcast.27), channel_id=1, source_target_pairs={{0,128},{8,40},{16,144},{24,56},{32,160},{40,8},{48,176},{56,24},{... | collective-permute-start | bytes 393224 | tf_op jit(solution)/shard_map/ppermute | solution.py:311
  24.1 12.0 %collective-permute-start.14 = (bf16[1024,256]{1,0:T(8,128)(2,1)S(1)}, bf16[1024,256]{1,0:T(8,128)(2,1)S(1)}, u32[]{:S(2)}, u32[]{:S(2)}) collective-permute-start(bf16[1024,256]{1,0:T(8,128)(2,1)S(1)} %pad_maximum_fusion.refs_1_), channel_id=1, source_target_pairs={{0,16},{8,72},{16,32},{24,88},{32,48},{40,104},{48,0},{56,120},{64... | collective-permute-start | bytes 1572872 | tf_op jit(solution)/shard_map/ppermute | solution.py:311
  24.4 11.8 %collective-permute-start.15 = (bf16[1024,256]{1,0:T(8,128)(2,1)S(1)}, bf16[1024,256]{1,0:T(8,128)(2,1)S(1)}, u32[]{:S(2)}, u32[]{:S(2)}) collective-permute-start(bf16[1024,256]{1,0:T(8,128)(2,1)S(1)} %pad_maximum_fusion.refs_1_), channel_id=1, source_target_pairs={{0,48},{8,200},{16,0},{24,216},{32,16},{40,232},{48,32},{56,248},{... | collective-permute-start | bytes 1572872 | tf_op jit(solution)/shard_map/ppermute | solution.py:311
  25.7 21.1 %all-to-all-start = ((bf16[32,8,1024]{2,1,0:T(8,128)(2,1)}), bf16[32,8,1024]{2,1,0:T(8,128)(2,1)S(1)}, u32[]{:S(2)}, u32[]{:S(2)}) async-start(bf16[32,8,1024]{2,1,0:T(8,128)(2,1)} %bitcast.3), calls=%async_computation | async-start | bytes 1048576 | tf_op jit(solution)/shard_map/all_to_all | solution.py:315
  30.8 15.9 %collective-permute-start.18 = (bf16[1024,256]{1,0:T(8,128)(2,1)S(1)}, bf16[1024,256]{1,0:T(8,128)(2,1)S(1)}, u32[]{:S(2)}, u32[]{:S(2)}) collective-permute-start(bf16[1024,256]{1,0:T(8,128)(2,1)S(1)} %pad_maximum_fusion.refs_1_), channel_id=1, source_target_pairs={{0,8},{8,0},{1,9},{9,1},{2,10},{10,2},{3,11},{11,3},{4,12},{12,4},... | collective-permute-start | bytes 1572872 | tf_op jit(solution)/shard_map/ppermute | solution.py:311
  36.1 7.9 %collective-permute-start.16 = (bf16[512,256]{1,0:T(8,128)(2,1)S(1)}, bf16[512,256]{1,0:T(8,128)(2,1)S(1)}, u32[]{:S(2)}, u32[]{:S(2)}) collective-permute-start(bf16[512,256]{1,0:T(8,128)(2,1)S(1)} %slice.8), channel_id=1, source_target_pairs={{0,16},{8,72},{16,32},{24,88},{32,48},{40,104},{48,0},{56,120},{64... | collective-permute-start | bytes 786440 | tf_op jit(solution)/shard_map/ppermute | solution.py:311
  36.3 8.8 %collective-permute-start.17 = (bf16[512,256]{1,0:T(8,128)(2,1)S(1)}, bf16[512,256]{1,0:T(8,128)(2,1)}, u32[]{:S(2)}, u32[]{:S(2)}) collective-permute-start(bf16[512,256]{1,0:T(8,128)(2,1)S(1)} %slice.9), channel_id=1, source_target_pairs={{0,48},{8,200},{16,0},{24,216},{32,16},{40,232},{48,32},{56,248},{... | collective-permute-start | bytes 786440 | tf_op jit(solution)/shard_map/ppermute | solution.py:311
  37.8 10.4 %collective-permute-start.19 = (bf16[1024,256]{1,0:T(8,128)(2,1)S(1)}, bf16[1024,256]{1,0:T(8,128)(2,1)S(1)}, u32[]{:S(2)}, u32[]{:S(2)}) collective-permute-start(bf16[1024,256]{1,0:T(8,128)(2,1)S(1)} %collective-permute-done.14.refs_2_), channel_id=1, source_target_pairs={{0,8},{8,0},{1,9},{9,1},{2,10},{10,2},{3,11},{11,3},{4,12},{12,4},... | collective-permute-start | bytes 1572872 | tf_op jit(solution)/shard_map/ppermute | solution.py:311
  39.6 8.6 %collective-permute-start.20 = (bf16[1024,256]{1,0:T(8,128)(2,1)S(1)}, bf16[1024,256]{1,0:T(8,128)(2,1)}, u32[]{:S(2)}, u32[]{:S(2)}) collective-permute-start(bf16[1024,256]{1,0:T(8,128)(2,1)S(1)} %collective-permute-done.15.refs_3_), channel_id=1, source_target_pairs={{0,8},{8,0},{1,9},{9,1},{2,10},{10,2},{3,11},{11,3},{4,12},{12,4},... | collective-permute-start | bytes 1572872 | tf_op jit(solution)/shard_map/ppermute | solution.py:311
  44.0 2.7 %collective-permute-start.21 = (bf16[512,256]{1,0:T(8,128)(2,1)S(1)}, bf16[512,256]{1,0:T(8,128)(2,1)}, u32[]{:S(2)}, u32[]{:S(2)}) collective-permute-start(bf16[512,256]{1,0:T(8,128)(2,1)S(1)} %collective-permute-done.16.refs_4_), channel_id=1, source_target_pairs={{0,8},{8,0},{1,9},{9,1},{2,10},{10,2},{3,11},{11,3},{4,12},{12,4},... | collective-permute-start | bytes 786440 | tf_op jit(solution)/shard_map/ppermute | solution.py:311
  45.1 3.1 %collective-permute-start.22 = (bf16[512,256]{1,0:T(8,128)(2,1)}, bf16[512,256]{1,0:T(8,128)(2,1)}, u32[]{:S(2)}, u32[]{:S(2)}) collective-permute-start(bf16[512,256]{1,0:T(8,128)(2,1)} %collective-permute-done.17.refs_5_), channel_id=1, source_target_pairs={{0,8},{8,0},{1,9},{9,1},{2,10},{10,2},{3,11},{11,3},{4,12},{12,4},... | collective-permute-start | bytes 786440 | tf_op jit(solution)/shard_map/ppermute | solution.py:311
  69.4 42.6 %all-to-all-start.2 = ((bf16[32,8,1024]{2,1,0:T(8,128)(2,1)}), bf16[32,8,1024]{2,1,0:T(8,128)(2,1)S(1)}, u32[]{:S(2)}, u32[]{:S(2)}) async-start(bf16[32,8,1024]{2,1,0:T(8,128)(2,1)} %bitcast.7), calls=%async_computation.2 | async-start | bytes 1048576 | tf_op jit(solution)/shard_map/all_to_all | solution.py:315
  81.1 3.2 %collective-permute-start.1 = (bf16[144,128]{1,0:T(8,128)(2,1)S(1)}, bf16[144,128]{1,0:T(8,128)(2,1)S(1)}, u32[]{:S(2)}, u32[]{:S(2)}) collective-permute-start(bf16[144,128]{1,0:T(8,128)(2,1)S(1)} %get-tuple-element.19), channel_id=1, source_target_pairs={{0,16},{16,32},{32,48},{48,0},{1,17},{17,33},{33,49},{49,1},{2,18}... | collective-permute-start | bytes 110600 | tf_op jit(solution)/shard_map/ppermute | solution.py:311
  81.7 4.6 %collective-permute-start.2 = (bf16[144,128]{1,0:T(8,128)(2,1)S(1)}, bf16[144,128]{1,0:T(8,128)(2,1)S(1)}, u32[]{:S(2)}, u32[]{:S(2)}) collective-permute-start(bf16[144,128]{1,0:T(8,128)(2,1)S(1)} %get-tuple-element.20), channel_id=1, source_target_pairs={{0,32},{16,48},{32,0},{48,16},{1,33},{17,49},{33,1},{49,17},{2,34}... | collective-permute-start | bytes 110600 | tf_op jit(solution)/shard_map/ppermute | solution.py:311
  83.0 4.7 %collective-permute-start.3 = (bf16[144,128]{1,0:T(8,128)(2,1)S(1)}, bf16[144,128]{1,0:T(8,128)(2,1)S(1)}, u32[]{:S(2)}, u32[]{:S(2)}) collective-permute-start(bf16[144,128]{1,0:T(8,128)(2,1)S(1)} %get-tuple-element.21), channel_id=1, source_target_pairs={{0,48},{16,0},{32,16},{48,32},{1,49},{17,1},{33,17},{49,33},{2,50}... | collective-permute-start | bytes 110600 | tf_op jit(solution)/shard_map/ppermute | solution.py:311
  87.7 5.1 %collective-permute-start.4 = (bf16[144,128]{1,0:T(8,128)(2,1)S(1)}, bf16[144,128]{1,0:T(8,128)(2,1)S(1)}, u32[]{:S(2)}, u32[]{:S(2)}) collective-permute-start(bf16[144,128]{1,0:T(8,128)(2,1)S(1)} %get-tuple-element.22), channel_id=1, source_target_pairs={{0,64},{64,128},{128,192},{1,65},{65,129},{129,193},{2,66},{66,130... | collective-permute-start | bytes 110600 | tf_op jit(solution)/shard_map/ppermute | solution.py:311
  89.0 6.2 %collective-permute-start.5 = (bf16[144,128]{1,0:T(8,128)(2,1)S(1)}, bf16[144,128]{1,0:T(8,128)(2,1)S(1)}, u32[]{:S(2)}, u32[]{:S(2)}) collective-permute-start(bf16[144,128]{1,0:T(8,128)(2,1)S(1)} %get-tuple-element.22), channel_id=1, source_target_pairs={{0,128},{64,192},{1,129},{65,193},{2,130},{66,194},{3,131},{67,195... | collective-permute-start | bytes 110600 | tf_op jit(solution)/shard_map/ppermute | solution.py:311
  90.3 7.7 %collective-permute-start.6 = (bf16[144,128]{1,0:T(8,128)(2,1)S(1)}, bf16[144,128]{1,0:T(8,128)(2,1)S(1)}, u32[]{:S(2)}, u32[]{:S(2)}) collective-permute-start(bf16[144,128]{1,0:T(8,128)(2,1)S(1)} %get-tuple-element.22), channel_id=1, source_target_pairs={{0,192},{1,193},{2,194},{3,195},{4,196},{5,197},{6,198},{7,199},{8... | collective-permute-start | bytes 110600 | tf_op jit(solution)/shard_map/ppermute | solution.py:311
  98.1 2.8 %collective-permute-start.7 = (bf16[128,128]{1,0:T(8,128)(2,1)S(1)}, bf16[128,128]{1,0:T(8,128)(2,1)S(1)}, u32[]{:S(2)}, u32[]{:S(2)}) collective-permute-start(bf16[128,128]{1,0:T(8,128)(2,1)S(1)} %get-tuple-element.25), channel_id=1, source_target_pairs={{0,16},{16,32},{32,48},{48,0},{1,17},{17,33},{33,49},{49,1},{2,18}... | collective-permute-start | bytes 98312 | tf_op jit(solution)/shard_map/ppermute | solution.py:311
  98.7 4.3 %collective-permute-start.8 = (bf16[128,128]{1,0:T(8,128)(2,1)S(1)}, bf16[128,128]{1,0:T(8,128)(2,1)S(1)}, u32[]{:S(2)}, u32[]{:S(2)}) collective-permute-start(bf16[128,128]{1,0:T(8,128)(2,1)S(1)} %get-tuple-element.26), channel_id=1, source_target_pairs={{0,32},{16,48},{32,0},{48,16},{1,33},{17,49},{33,1},{49,17},{2,34}... | collective-permute-start | bytes 98312 | tf_op jit(solution)/shard_map/ppermute | solution.py:311
  99.6 4.0 %collective-permute-start.9 = (bf16[128,128]{1,0:T(8,128)(2,1)S(1)}, bf16[128,128]{1,0:T(8,128)(2,1)S(1)}, u32[]{:S(2)}, u32[]{:S(2)}) collective-permute-start(bf16[128,128]{1,0:T(8,128)(2,1)S(1)} %get-tuple-element.27), channel_id=1, source_target_pairs={{0,48},{16,0},{32,16},{48,32},{1,49},{17,1},{33,17},{49,33},{2,50}... | collective-permute-start | bytes 98312 | tf_op jit(solution)/shard_map/ppermute | solution.py:311
  103.7 5.7 %collective-permute-start.10 = (bf16[4,128,128]{2,1,0:T(8,128)(2,1)S(1)}, bf16[4,128,128]{2,1,0:T(8,128)(2,1)S(1)}, u32[]{:S(2)}, u32[]{:S(2)}) collective-permute-start(bf16[4,128,128]{2,1,0:T(8,128)(2,1)S(1)} %get-tuple-element.29), channel_id=1, source_target_pairs={{0,8},{8,0},{1,9},{9,1},{2,10},{10,2},{3,11},{11,3},{4,12},{12,4},... | collective-permute-start | bytes 393224 | tf_op jit(solution)/shard_map/ppermute | solution.py:311
  (6 other events, 81.3 us)

commit v6 on v5

--- a/solution.py
+++ b/solution.py
@@ -160,6 +160,21 @@
         mix = dot(probs, v, NN) + jnp.exp(col) * dot(q, state, NN)
         norm = lax.rsqrt(jnp.mean(mix * mix, axis=1, keepdims=True) + 1e-05)
         out_ref[:, cols] = (mix * norm * gain_ref[:, cols]).astype(jnp.bfloat16)
+
+
+def cut_kernel(kv_ref, *out_refs):
+    mz = lax.axis_index("head")
+    for d, out_ref in enumerate(out_refs):
+        z = (mz + d) % NZ
+        out_ref[...] = kv_ref[:, pl.ds(pl.multiple_of(z * 2 * DIM, 2 * DIM), 2 * DIM)]
+
+
+def join_kernel(*refs):
+    mz = lax.axis_index("head")
+    out_ref = refs[-1]
+    for d, ref in enumerate(refs[:-1]):
+        z = (mz + NZ - d) % NZ
+        out_ref[pl.ds(pl.multiple_of(z * 32, 32), 32), :] = ref[...]
 
 
 ROWS = HEADS * 64
@@ -330,8 +345,13 @@
 
 
 def both(lin_q, lin_k, lin_v, log_decay, lin_gain, soft_q, soft_kv):
-    kv = soft_kv.reshape(32, NZ, 2 * DIM).swapaxes(0, 1)
-    kv = exchange(kv, "head").reshape(CH, 2 * DIM)
+    part = ((32, 2 * DIM), jnp.bfloat16)
+    parts = call(cut_kernel, [part] * NZ, 1, 1 << 18)(soft_kv)
+    parts = [parts[0]] + [
+        permute(parts[d], [(z, (z + d) % NZ) for z in range(NZ)], "head")
+        for d in range(1, NZ)
+    ]
+    (kv,) = call(join_kernel, [((CH, 2 * DIM), jnp.bfloat16)], NZ, 1 << 18)(*parts)
     q = soft_q.reshape(NX, 8, NZ, HEADS * DIM).swapaxes(1, 2).reshape(NX * NZ, 8, HEADS * DIM)
     q = exchange(q, ("ctx_0", "head")).reshape(CH, HEADS * DIM)
     pieces = gather_kv(kv)

time: 114 us -> 121 us (1.061)
  starting transfers between devices: 40.5 us -> 58.8 us
  blocking collectives: 15.7 us -> 0 us
  waiting for transfers between devices: 28.3 us -> 32.8 us
    ppermute x23 -> x30, starting transfers between devices: 27.4 us -> 43.5 us  [permute(): return lax.ppermute(value, axes, pairs)]
    all_to_all x1 -> x0, blocking collectives: 15.7 us -> none  [exchange(): return lax.all_to_all(value, axes, 0, 0, tiled=True)]
    ppermute x23 -> x30, waiting for transfers between devices: 28.3 us -> 32.8 us  [permute(): return lax.ppermute(value, axes, pairs)]
    all_to_all x2, starting transfers between devices: 13.1 us -> 15.3 us  [exchange(): return lax.all_to_all(value, axes, 0, 0, tiled=True)]
  transfers between devices with their start and end apart: 25 -> 32, of which waited for: 17 -> 19; matrix products, arithmetic and copies ran while one was open for 0% -> 0% of each run, Pallas kernels for 4% -> 4%
where the time goes in v6:
time: 121 us; the launch traced here: 120 us
  starting transfers between devices  58.8 us (49%)
  waiting for transfers between devices  32.8 us (27%)
  Pallas kernels  25.6 us (21%)
  local copies, waits for them, and re-layouts  1.76 us (1%)
    ppermute x30, starting transfers between devices, permute(): return lax.ppermute(value, axes, pairs)  43.5 us
    ppermute x30, waiting for transfers between devices, permute(): return lax.ppermute(value, axes, pairs)  32.8 us
    pallas_call x1, Pallas kernels, both(): call(softmax_kernel, [block], 11, 1 << 34, in_specs=vmem(1) + [pl.BlockSp...  21.1 us
    all_to_all x2, starting transfers between devices, exchange(): return lax.all_to_all(value, axes, 0, 0, tiled=True)  15.3 us
    pallas_call x1, Pallas kernels, both(): call(lightning_kernel, [block], 7, 1 << 29)  2.6 us
  transfers between devices with their start and end apart: 32, of which 19 were waited for; matrix products, arithmetic and copies ran while one was open for 0% of the time, Pallas kernels for 4%

profile of v6, /device:TPU:31, one launch (start us, length us, event | category | flops | bytes accessed | tf_op | source)
XLA Modules:
  0.0 119.8 jit_solution(11885537102381547695)
XLA Ops:
  1.6 1.7 %collective-permute-start.11 = (bf16[32,256]{1,0:T(8,128)(2,1)S(1)}, bf16[32,256]{1,0:T(8,128)(2,1)S(1)}, u32[]{:S(2)}, u32[]{:S(2)}) collective-permute-start(bf16[32,256]{1,0:T(8,128)(2,1)S(1)} %get-tuple-element.39), channel_id=1, source_target_pairs={{0,1},{1,2},{2,3},{3,4},{4,5},{5,6},{6,7},{7,0},{8,9},{9,10},{10,1... | collective-permute-start | bytes 49160 | tf_op jit(solution)/shard_map/ppermute | solution.py:326
  3.3 3.0 %collective-permute-start.12 = (bf16[32,256]{1,0:T(8,128)(2,1)S(1)}, bf16[32,256]{1,0:T(8,128)(2,1)S(1)}, u32[]{:S(2)}, u32[]{:S(2)}) collective-permute-start(bf16[32,256]{1,0:T(8,128)(2,1)S(1)} %get-tuple-element.40), channel_id=1, source_target_pairs={{0,2},{1,3},{2,4},{3,5},{4,6},{5,7},{6,0},{7,1},{8,10},{9,11},{10,... | collective-permute-start | bytes 49160 | tf_op jit(solution)/shard_map/ppermute | solution.py:326
  6.3 3.8 %collective-permute-start.13 = (bf16[32,256]{1,0:T(8,128)(2,1)S(1)}, bf16[32,256]{1,0:T(8,128)(2,1)S(1)}, u32[]{:S(2)}, u32[]{:S(2)}) collective-permute-start(bf16[32,256]{1,0:T(8,128)(2,1)S(1)} %get-tuple-element.41), channel_id=1, source_target_pairs={{0,3},{1,4},{2,5},{3,6},{4,7},{5,0},{6,1},{7,2},{8,11},{9,12},{10,... | collective-permute-start | bytes 49160 | tf_op jit(solution)/shard_map/ppermute | solution.py:326
  10.5 4.5 %collective-permute-start.15 = (bf16[32,256]{1,0:T(8,128)(2,1)S(1)}, bf16[32,256]{1,0:T(8,128)(2,1)S(1)}, u32[]{:S(2)}, u32[]{:S(2)}) collective-permute-start(bf16[32,256]{1,0:T(8,128)(2,1)S(1)} %get-tuple-element.43), channel_id=1, source_target_pairs={{0,5},{1,6},{2,7},{3,0},{4,1},{5,2},{6,3},{7,4},{8,13},{9,14},{10,... | collective-permute-start | bytes 49160 | tf_op jit(solution)/shard_map/ppermute | solution.py:326
  15.0 2.4 %collective-permute-start.16 = (bf16[32,256]{1,0:T(8,128)(2,1)S(1)}, bf16[32,256]{1,0:T(8,128)(2,1)S(1)}, u32[]{:S(2)}, u32[]{:S(2)}) collective-permute-start(bf16[32,256]{1,0:T(8,128)(2,1)S(1)} %get-tuple-element.44), channel_id=1, source_target_pairs={{0,6},{1,7},{2,0},{3,1},{4,2},{5,3},{6,4},{7,5},{8,14},{9,15},{10,... | collective-permute-start | bytes 49160 | tf_op jit(solution)/shard_map/ppermute | solution.py:326
  20.0 1.5 %collective-permute-start.19 = (bf16[256,256]{1,0:T(8,128)(2,1)S(1)}, bf16[256,256]{1,0:T(8,128)(2,1)S(1)}, u32[]{:S(2)}, u32[]{:S(2)}) collective-permute-start(bf16[256,256]{1,0:T(8,128)(2,1)S(1)} %shard_map.93), channel_id=1, source_target_pairs={{0,192},{8,56},{16,208},{24,8},{32,224},{40,24},{48,240},{56,40},{... | collective-permute-start | bytes 393224 | tf_op jit(solution)/shard_map/ppermute | solution.py:326
  25.2 1.7 %collective-permute-done.20 = bf16[256,256]{1,0:T(8,128)(2,1)S(1)} collective-permute-done((bf16[256,256]{1,0:T(8,128)(2,1)S(1)}, bf16[256,256]{1,0:T(8,128)(2,1)S(1)}, u32[]{:S(2)}, u32[]{:S(2)}) %collective-permute-start.20) | collective-permute-done | bytes 131104 | tf_op jit(solution)/shard_map/ppermute | solution.py:326
  28.4 6.7 %all-to-all-start = ((bf16[32,8,1024]{2,1,0:T(8,128)(2,1)}), bf16[32,8,1024]{2,1,0:T(8,128)(2,1)S(1)}, u32[]{:S(2)}, u32[]{:S(2)}) async-start(bf16[32,8,1024]{2,1,0:T(8,128)(2,1)} %bitcast.3), calls=%async_computation | async-start | bytes 1048576 | tf_op jit(solution)/shard_map/all_to_all | solution.py:330
  35.1 7.2 %collective-permute-start.25 = (bf16[1024,256]{1,0:T(8,128)(2,1)S(1)}, bf16[1024,256]{1,0:T(8,128)(2,1)S(1)}, u32[]{:S(2)}, u32[]{:S(2)}) collective-permute-start(bf16[1024,256]{1,0:T(8,128)(2,1)S(1)} %pad_maximum_fusion.refs_1_), channel_id=1, source_target_pairs={{0,8},{8,0},{1,9},{9,1},{2,10},{10,2},{3,11},{11,3},{4,12},{12,4},... | collective-permute-start | bytes 1572872 | tf_op jit(solution)/shard_map/ppermute | solution.py:326
  44.9 4.4 %collective-permute-done.23.refs_4_ = bf16[512,256]{1,0:T(8,128)(2,1)S(1)} collective-permute-done((bf16[512,256]{1,0:T(8,128)(2,1)S(1)}, bf16[512,256]{1,0:T(8,128)(2,1)S(1)}, u32[]{:S(2)}, u32[]{:S(2)}) %collective-permute-start.23) | collective-permute-done | bytes 262176 | tf_op jit(solution)/shard_map/ppermute | solution.py:326
  49.3 3.3 %collective-permute-done.24.refs_5_ = bf16[512,256]{1,0:T(8,128)(2,1)} collective-permute-done((bf16[512,256]{1,0:T(8,128)(2,1)S(1)}, bf16[512,256]{1,0:T(8,128)(2,1)}, u32[]{:S(2)}, u32[]{:S(2)}) %collective-permute-start.24) | collective-permute-done | bytes 262176 | tf_op jit(solution)/shard_map/ppermute | solution.py:326
  52.6 1.8 %collective-permute-done.29.refs_10_ = bf16[512,256]{1,0:T(8,128)(2,1)} collective-permute-done((bf16[512,256]{1,0:T(8,128)(2,1)}, bf16[512,256]{1,0:T(8,128)(2,1)}, u32[]{:S(2)}, u32[]{:S(2)}) %collective-permute-start.29) | collective-permute-done | bytes 262176 | tf_op jit(solution)/shard_map/ppermute | solution.py:326
  54.4 21.1 %shard_map.94 = bf16[256,1024]{1,0:T(8,128)(2,1)} custom-call(bf16[256,1024]{1,0:T(8,128)(2,1)S(1)} %bitcast.13, bf16[1024,256]{1,0:T(8,128)(2,1)S(1)} %pad_maximum_fusion.refs_1_, bf16[1024,256]{1,0:T(8,128)(2,1)S(1)} %collective-permute-done.21.refs_2_, bf16[1024,256]{1,0:T(8,128)(2,1)S(1)} %collective-permute-done.22.refs_3_, ...), custom_call_target="tpu_custom_call" | custom-call | flops 17179869184 | bytes 2097152 | tf_op jit(solution)/shard_map/pallas_call | solution.py:390
  75.5 8.7 %all-to-all-start.1 = ((bf16[32,8,1024]{2,1,0:T(8,128)(2,1)}), bf16[32,8,1024]{2,1,0:T(8,128)(2,1)S(1)}, u32[]{:S(2)}, u32[]{:S(2)}) async-start(bf16[32,8,1024]{2,1,0:T(8,128)(2,1)} %bitcast.5), calls=%async_computation.1 | async-start | bytes 1048576 | tf_op jit(solution)/shard_map/all_to_all | solution.py:330
  84.2 1.6 %shard_map.86 = (bf16[4,144,128]{2,1,0:T(8,128)(2,1)S(1)}, bf16[4,144,128]{2,1,0:T(8,128)(2,1)S(1)}) custom-call(bf16[256,1024]{1,0:T(8,128)(2,1)S(1)} %copy-done, bf16[256,1024]{1,0:T(8,128)(2,1)S(1)} %copy-done.1, f32[8,256]{1,0:T(8,128)S(1)} %copy-done.4), custom_call_target="tpu_custom_call" | custom-call | flops 268435456 | bytes 2097152 | tf_op jit(solution)/shard_map/pallas_call | solution.py:371
  88.1 1.4 %collective-permute-start.2 = (bf16[144,128]{1,0:T(8,128)(2,1)S(1)}, bf16[144,128]{1,0:T(8,128)(2,1)S(1)}, u32[]{:S(2)}, u32[]{:S(2)}) collective-permute-start(bf16[144,128]{1,0:T(8,128)(2,1)S(1)} %get-tuple-element.28), channel_id=1, source_target_pairs={{0,32},{16,48},{32,0},{48,16},{1,33},{17,49},{33,1},{49,17},{2,34}... | collective-permute-start | bytes 110600 | tf_op jit(solution)/shard_map/ppermute | solution.py:326
  89.5 1.6 %collective-permute-done.1.a_ref = bf16[144,128]{1,0:T(8,128)(2,1)S(1)} collective-permute-done((bf16[144,128]{1,0:T(8,128)(2,1)S(1)}, bf16[144,128]{1,0:T(8,128)(2,1)S(1)}, u32[]{:S(2)}, u32[]{:S(2)}) %collective-permute-start.1) | collective-permute-done | bytes 36896 | tf_op jit(solution)/shard_map/ppermute | solution.py:326
  91.1 1.6 %collective-permute-done.2.b_ref = bf16[144,128]{1,0:T(8,128)(2,1)S(1)} collective-permute-done((bf16[144,128]{1,0:T(8,128)(2,1)S(1)}, bf16[144,128]{1,0:T(8,128)(2,1)S(1)}, u32[]{:S(2)}, u32[]{:S(2)}) %collective-permute-start.2) | collective-permute-done | bytes 36896 | tf_op jit(solution)/shard_map/ppermute | solution.py:326
  92.7 1.5 %collective-permute-done.3.c_ref = bf16[144,128]{1,0:T(8,128)(2,1)S(1)} collective-permute-done((bf16[144,128]{1,0:T(8,128)(2,1)S(1)}, bf16[144,128]{1,0:T(8,128)(2,1)S(1)}, u32[]{:S(2)}, u32[]{:S(2)}) %collective-permute-start.3) | collective-permute-done | bytes 36896 | tf_op jit(solution)/shard_map/ppermute | solution.py:326
  99.4 2.3 %collective-permute-done.5.b_ref = bf16[144,128]{1,0:T(8,128)(2,1)S(1)} collective-permute-done((bf16[144,128]{1,0:T(8,128)(2,1)S(1)}, bf16[144,128]{1,0:T(8,128)(2,1)S(1)}, u32[]{:S(2)}, u32[]{:S(2)}) %collective-permute-start.5) | collective-permute-done | bytes 36896 | tf_op jit(solution)/shard_map/ppermute | solution.py:326
  101.8 2.8 %collective-permute-done.6.c_ref = bf16[144,128]{1,0:T(8,128)(2,1)S(1)} collective-permute-done((bf16[144,128]{1,0:T(8,128)(2,1)S(1)}, bf16[144,128]{1,0:T(8,128)(2,1)S(1)}, u32[]{:S(2)}, u32[]{:S(2)}) %collective-permute-start.6) | collective-permute-done | bytes 36896 | tf_op jit(solution)/shard_map/ppermute | solution.py:326
  107.7 2.3 %collective-permute-done.8.e2_ref = bf16[128,128]{1,0:T(8,128)(2,1)S(1)} collective-permute-done((bf16[128,128]{1,0:T(8,128)(2,1)S(1)}, bf16[128,128]{1,0:T(8,128)(2,1)S(1)}, u32[]{:S(2)}, u32[]{:S(2)}) %collective-permute-start.8) | collective-permute-done | bytes 32800 | tf_op jit(solution)/shard_map/ppermute | solution.py:326
  110.7 4.7 %collective-permute-start.10 = (bf16[4,128,128]{2,1,0:T(8,128)(2,1)S(1)}, bf16[4,128,128]{2,1,0:T(8,128)(2,1)S(1)}, u32[]{:S(2)}, u32[]{:S(2)}) collective-permute-start(bf16[4,128,128]{2,1,0:T(8,128)(2,1)S(1)} %get-tuple-element.37), channel_id=1, source_target_pairs={{0,8},{8,0},{1,9},{9,1},{2,10},{10,2},{3,11},{11,3},{4,12},{12,4},... | collective-permute-start | bytes 393224 | tf_op jit(solution)/shard_map/ppermute | solution.py:326
  116.5 2.6 %shard_map.91 = bf16[256,1024]{1,0:T(8,128)(2,1)} custom-call(bf16[256,1024]{1,0:T(8,128)(2,1)S(1)} %copy-done.2, bf16[256,1024]{1,0:T(8,128)(2,1)S(1)} %copy-done, bf16[256,1024]{1,0:T(8,128)(2,1)S(1)} %copy-done.1, f32[8,256]{1,0:T(8,128)S(1)} %copy-done.4, f32[1,1024]{1,0:T(1,128)S(1)} %bitcast.14, bf16[4,128,128]{2,1,0:T(8,128)(2,1)S(1)} %get-tuple-element.36.keep_ref, ...), custom_call_target="tpu_custom_call" | custom-call | flops 536870912 | bytes 2097152 | tf_op jit(solution)/shard_map/pallas_call | solution.py:412
  (65 shorter events, 25.0 us)
Async XLA Ops:
  1.6 13.4 %collective-permute-start.11 = (bf16[32,256]{1,0:T(8,128)(2,1)S(1)}, bf16[32,256]{1,0:T(8,128)(2,1)S(1)}, u32[]{:S(2)}, u32[]{:S(2)}) collective-permute-start(bf16[32,256]{1,0:T(8,128)(2,1)S(1)} %get-tuple-element.39), channel_id=1, source_target_pairs={{0,1},{1,2},{2,3},{3,4},{4,5},{5,6},{6,7},{7,0},{8,9},{9,10},{10,1... | collective-permute-start | bytes 49160 | tf_op jit(solution)/shard_map/ppermute | solution.py:326
  3.3 14.1 %collective-permute-start.12 = (bf16[32,256]{1,0:T(8,128)(2,1)S(1)}, bf16[32,256]{1,0:T(8,128)(2,1)S(1)}, u32[]{:S(2)}, u32[]{:S(2)}) collective-permute-start(bf16[32,256]{1,0:T(8,128)(2,1)S(1)} %get-tuple-element.40), channel_id=1, source_target_pairs={{0,2},{1,3},{2,4},{3,5},{4,6},{5,7},{6,0},{7,1},{8,10},{9,11},{10,... | collective-permute-start | bytes 49160 | tf_op jit(solution)/shard_map/ppermute | solution.py:326
  6.3 11.8 %collective-permute-start.13 = (bf16[32,256]{1,0:T(8,128)(2,1)S(1)}, bf16[32,256]{1,0:T(8,128)(2,1)S(1)}, u32[]{:S(2)}, u32[]{:S(2)}) collective-permute-start(bf16[32,256]{1,0:T(8,128)(2,1)S(1)} %get-tuple-element.41), channel_id=1, source_target_pairs={{0,3},{1,4},{2,5},{3,6},{4,7},{5,0},{6,1},{7,2},{8,11},{9,12},{10,... | collective-permute-start | bytes 49160 | tf_op jit(solution)/shard_map/ppermute | solution.py:326
  10.0 8.1 %collective-permute-start.14 = (bf16[32,256]{1,0:T(8,128)(2,1)S(1)}, bf16[32,256]{1,0:T(8,128)(2,1)S(1)}, u32[]{:S(2)}, u32[]{:S(2)}) collective-permute-start(bf16[32,256]{1,0:T(8,128)(2,1)S(1)} %get-tuple-element.42), channel_id=1, source_target_pairs={{0,4},{1,5},{2,6},{3,7},{4,0},{5,1},{6,2},{7,3},{8,12},{9,13},{10,... | collective-permute-start | bytes 49160 | tf_op jit(solution)/shard_map/ppermute | solution.py:326
  10.5 7.6 %collective-permute-start.15 = (bf16[32,256]{1,0:T(8,128)(2,1)S(1)}, bf16[32,256]{1,0:T(8,128)(2,1)S(1)}, u32[]{:S(2)}, u32[]{:S(2)}) collective-permute-start(bf16[32,256]{1,0:T(8,128)(2,1)S(1)} %get-tuple-element.43), channel_id=1, source_target_pairs={{0,5},{1,6},{2,7},{3,0},{4,1},{5,2},{6,3},{7,4},{8,13},{9,14},{10,... | collective-permute-start | bytes 49160 | tf_op jit(solution)/shard_map/ppermute | solution.py:326
  20.0 5.1 %collective-permute-start.19 = (bf16[256,256]{1,0:T(8,128)(2,1)S(1)}, bf16[256,256]{1,0:T(8,128)(2,1)S(1)}, u32[]{:S(2)}, u32[]{:S(2)}) collective-permute-start(bf16[256,256]{1,0:T(8,128)(2,1)S(1)} %shard_map.93), channel_id=1, source_target_pairs={{0,192},{8,56},{16,208},{24,8},{32,224},{40,24},{48,240},{56,40},{... | collective-permute-start | bytes 393224 | tf_op jit(solution)/shard_map/ppermute | solution.py:326
  21.5 5.3 %collective-permute-start.20 = (bf16[256,256]{1,0:T(8,128)(2,1)S(1)}, bf16[256,256]{1,0:T(8,128)(2,1)S(1)}, u32[]{:S(2)}, u32[]{:S(2)}) collective-permute-start(bf16[256,256]{1,0:T(8,128)(2,1)S(1)} %shard_map.93), channel_id=1, source_target_pairs={{0,128},{8,40},{16,144},{24,56},{32,160},{40,8},{48,176},{56,24},{... | collective-permute-start | bytes 393224 | tf_op jit(solution)/shard_map/ppermute | solution.py:326
  26.9 15.4 %collective-permute-start.21 = (bf16[1024,256]{1,0:T(8,128)(2,1)S(1)}, bf16[1024,256]{1,0:T(8,128)(2,1)S(1)}, u32[]{:S(2)}, u32[]{:S(2)}) collective-permute-start(bf16[1024,256]{1,0:T(8,128)(2,1)S(1)} %pad_maximum_fusion.refs_1_), channel_id=1, source_target_pairs={{0,16},{8,72},{16,32},{24,88},{32,48},{40,104},{48,0},{56,120},{64... | collective-permute-start | bytes 1572872 | tf_op jit(solution)/shard_map/ppermute | solution.py:326
  27.1 16.6 %collective-permute-start.22 = (bf16[1024,256]{1,0:T(8,128)(2,1)S(1)}, bf16[1024,256]{1,0:T(8,128)(2,1)S(1)}, u32[]{:S(2)}, u32[]{:S(2)}) collective-permute-start(bf16[1024,256]{1,0:T(8,128)(2,1)S(1)} %pad_maximum_fusion.refs_1_), channel_id=1, source_target_pairs={{0,48},{8,200},{16,0},{24,216},{32,16},{40,232},{48,32},{56,248},{... | collective-permute-start | bytes 1572872 | tf_op jit(solution)/shard_map/ppermute | solution.py:326
  28.4 24.1 %all-to-all-start = ((bf16[32,8,1024]{2,1,0:T(8,128)(2,1)}), bf16[32,8,1024]{2,1,0:T(8,128)(2,1)S(1)}, u32[]{:S(2)}, u32[]{:S(2)}) async-start(bf16[32,8,1024]{2,1,0:T(8,128)(2,1)} %bitcast.3), calls=%async_computation | async-start | bytes 1048576 | tf_op jit(solution)/shard_map/all_to_all | solution.py:330
  35.1 17.4 %collective-permute-start.25 = (bf16[1024,256]{1,0:T(8,128)(2,1)S(1)}, bf16[1024,256]{1,0:T(8,128)(2,1)S(1)}, u32[]{:S(2)}, u32[]{:S(2)}) collective-permute-start(bf16[1024,256]{1,0:T(8,128)(2,1)S(1)} %pad_maximum_fusion.refs_1_), channel_id=1, source_target_pairs={{0,8},{8,0},{1,9},{9,1},{2,10},{10,2},{3,11},{11,3},{4,12},{12,4},... | collective-permute-start | bytes 1572872 | tf_op jit(solution)/shard_map/ppermute | solution.py:326
  42.3 6.9 %collective-permute-start.23 = (bf16[512,256]{1,0:T(8,128)(2,1)S(1)}, bf16[512,256]{1,0:T(8,128)(2,1)S(1)}, u32[]{:S(2)}, u32[]{:S(2)}) collective-permute-start(bf16[512,256]{1,0:T(8,128)(2,1)S(1)} %slice.8), channel_id=1, source_target_pairs={{0,16},{8,72},{16,32},{24,88},{32,48},{40,104},{48,0},{56,120},{64... | collective-permute-start | bytes 786440 | tf_op jit(solution)/shard_map/ppermute | solution.py:326
  42.4 10.1 %collective-permute-start.26 = (bf16[1024,256]{1,0:T(8,128)(2,1)S(1)}, bf16[1024,256]{1,0:T(8,128)(2,1)S(1)}, u32[]{:S(2)}, u32[]{:S(2)}) collective-permute-start(bf16[1024,256]{1,0:T(8,128)(2,1)S(1)} %collective-permute-done.21.refs_2_), channel_id=1, source_target_pairs={{0,8},{8,0},{1,9},{9,1},{2,10},{10,2},{3,11},{11,3},{4,12},{12,4},... | collective-permute-start | bytes 1572872 | tf_op jit(solution)/shard_map/ppermute | solution.py:326
  43.7 8.8 %collective-permute-start.27 = (bf16[1024,256]{1,0:T(8,128)(2,1)S(1)}, bf16[1024,256]{1,0:T(8,128)(2,1)}, u32[]{:S(2)}, u32[]{:S(2)}) collective-permute-start(bf16[1024,256]{1,0:T(8,128)(2,1)S(1)} %collective-permute-done.22.refs_3_), channel_id=1, source_target_pairs={{0,8},{8,0},{1,9},{9,1},{2,10},{10,2},{3,11},{11,3},{4,12},{12,4},... | collective-permute-start | bytes 1572872 | tf_op jit(solution)/shard_map/ppermute | solution.py:326
  43.8 8.8 %collective-permute-start.24 = (bf16[512,256]{1,0:T(8,128)(2,1)S(1)}, bf16[512,256]{1,0:T(8,128)(2,1)}, u32[]{:S(2)}, u32[]{:S(2)}) collective-permute-start(bf16[512,256]{1,0:T(8,128)(2,1)S(1)} %slice.9), channel_id=1, source_target_pairs={{0,48},{8,200},{16,0},{24,216},{32,16},{40,232},{48,32},{56,248},{... | collective-permute-start | bytes 786440 | tf_op jit(solution)/shard_map/ppermute | solution.py:326
  75.5 43.5 %all-to-all-start.1 = ((bf16[32,8,1024]{2,1,0:T(8,128)(2,1)}), bf16[32,8,1024]{2,1,0:T(8,128)(2,1)S(1)}, u32[]{:S(2)}, u32[]{:S(2)}) async-start(bf16[32,8,1024]{2,1,0:T(8,128)(2,1)} %bitcast.5), calls=%async_computation.1 | async-start | bytes 1048576 | tf_op jit(solution)/shard_map/all_to_all | solution.py:330
  88.1 4.7 %collective-permute-start.2 = (bf16[144,128]{1,0:T(8,128)(2,1)S(1)}, bf16[144,128]{1,0:T(8,128)(2,1)S(1)}, u32[]{:S(2)}, u32[]{:S(2)}) collective-permute-start(bf16[144,128]{1,0:T(8,128)(2,1)S(1)} %get-tuple-element.28), channel_id=1, source_target_pairs={{0,32},{16,48},{32,0},{48,16},{1,33},{17,49},{33,1},{49,17},{2,34}... | collective-permute-start | bytes 110600 | tf_op jit(solution)/shard_map/ppermute | solution.py:326
  89.5 4.7 %collective-permute-start.3 = (bf16[144,128]{1,0:T(8,128)(2,1)S(1)}, bf16[144,128]{1,0:T(8,128)(2,1)S(1)}, u32[]{:S(2)}, u32[]{:S(2)}) collective-permute-start(bf16[144,128]{1,0:T(8,128)(2,1)S(1)} %get-tuple-element.29), channel_id=1, source_target_pairs={{0,48},{16,0},{32,16},{48,32},{1,49},{17,1},{33,17},{49,33},{2,50}... | collective-permute-start | bytes 110600 | tf_op jit(solution)/shard_map/ppermute | solution.py:326
  94.3 5.2 %collective-permute-start.4 = (bf16[144,128]{1,0:T(8,128)(2,1)S(1)}, bf16[144,128]{1,0:T(8,128)(2,1)S(1)}, u32[]{:S(2)}, u32[]{:S(2)}) collective-permute-start(bf16[144,128]{1,0:T(8,128)(2,1)S(1)} %get-tuple-element.30), channel_id=1, source_target_pairs={{0,64},{64,128},{128,192},{1,65},{65,129},{129,193},{2,66},{66,130... | collective-permute-start | bytes 110600 | tf_op jit(solution)/shard_map/ppermute | solution.py:326
  95.6 6.2 %collective-permute-start.5 = (bf16[144,128]{1,0:T(8,128)(2,1)S(1)}, bf16[144,128]{1,0:T(8,128)(2,1)S(1)}, u32[]{:S(2)}, u32[]{:S(2)}) collective-permute-start(bf16[144,128]{1,0:T(8,128)(2,1)S(1)} %get-tuple-element.30), channel_id=1, source_target_pairs={{0,128},{64,192},{1,129},{65,193},{2,130},{66,194},{3,131},{67,195... | collective-permute-start | bytes 110600 | tf_op jit(solution)/shard_map/ppermute | solution.py:326
  96.9 7.7 %collective-permute-start.6 = (bf16[144,128]{1,0:T(8,128)(2,1)S(1)}, bf16[144,128]{1,0:T(8,128)(2,1)S(1)}, u32[]{:S(2)}, u32[]{:S(2)}) collective-permute-start(bf16[144,128]{1,0:T(8,128)(2,1)S(1)} %get-tuple-element.30), channel_id=1, source_target_pairs={{0,192},{1,193},{2,194},{3,195},{4,196},{5,197},{6,198},{7,199},{8... | collective-permute-start | bytes 110600 | tf_op jit(solution)/shard_map/ppermute | solution.py:326
  105.7 4.3 %collective-permute-start.8 = (bf16[128,128]{1,0:T(8,128)(2,1)S(1)}, bf16[128,128]{1,0:T(8,128)(2,1)S(1)}, u32[]{:S(2)}, u32[]{:S(2)}) collective-permute-start(bf16[128,128]{1,0:T(8,128)(2,1)S(1)} %get-tuple-element.34), channel_id=1, source_target_pairs={{0,32},{16,48},{32,0},{48,16},{1,33},{17,49},{33,1},{49,17},{2,34}... | collective-permute-start | bytes 98312 | tf_op jit(solution)/shard_map/ppermute | solution.py:326
  106.6 4.0 %collective-permute-start.9 = (bf16[128,128]{1,0:T(8,128)(2,1)S(1)}, bf16[128,128]{1,0:T(8,128)(2,1)S(1)}, u32[]{:S(2)}, u32[]{:S(2)}) collective-permute-start(bf16[128,128]{1,0:T(8,128)(2,1)S(1)} %get-tuple-element.35), channel_id=1, source_target_pairs={{0,48},{16,0},{32,16},{48,32},{1,49},{17,1},{33,17},{49,33},{2,50}... | collective-permute-start | bytes 98312 | tf_op jit(solution)/shard_map/ppermute | solution.py:326
  110.7 5.7 %collective-permute-start.10 = (bf16[4,128,128]{2,1,0:T(8,128)(2,1)S(1)}, bf16[4,128,128]{2,1,0:T(8,128)(2,1)S(1)}, u32[]{:S(2)}, u32[]{:S(2)}) collective-permute-start(bf16[4,128,128]{2,1,0:T(8,128)(2,1)S(1)} %get-tuple-element.37), channel_id=1, source_target_pairs={{0,8},{8,0},{1,9},{9,1},{2,10},{10,2},{3,11},{11,3},{4,12},{12,4},... | collective-permute-start | bytes 393224 | tf_op jit(solution)/shard_map/ppermute | solution.py:326
  (14 other events, 106.2 us)

commit v7 on v5

--- a/solution.py
+++ b/solution.py
@@ -174,12 +174,27 @@
     mx, my, mc = (lax.axis_index(a) for a in CTX)
     yc = my * NC + mc
 
-    copies = []
-    for n, ref in enumerate(pieces):
-        other, part = divmod(n, 5)
-        rows = pl.ds((other * 16 + (0, 4, 8, 12, 14)[part]) * CH, ref.shape[0])
-        copies.append(pltpu.make_async_copy(ref, kv_ref.at[rows, :], sems.at[n]))
-        copies[-1].start()
+    def copies_of(parts):
+        found = []
+        for other in range(2):
+            for part, at, size in parts:
+                ref = pieces[5 * other + part]
+                to = other * 16 + (0, 4, 8, 12, 14)[part] + at
+                n = other * 8 + len(found) % 4 + (0 if parts is first_parts else 4)
+                found.append(
+                    pltpu.make_async_copy(
+                        ref.at[pl.ds(at * CH, size * CH), :],
+                        kv_ref.at[pl.ds(to * CH, size * CH), :],
+                        sems.at[n],
+                    )
+                )
+        for copy in found:
+            copy.start()
+        return found
+
+    first_parts = ((0, 0, 4), (1, 0, 1), (2, 0, 1), (3, 0, 1))
+    first_copies = copies_of(first_parts)
+    other_copies = copies_of(((1, 1, 3), (2, 1, 3), (3, 1, 1), (4, 0, 2)))
 
     def chunk(kx, k):
         other, i = divmod(k, 4)
@@ -195,15 +210,19 @@
             rows = slice(x * ROWS + g * 64, x * ROWS + (g + 1) * 64)
             qq_ref[rows, :] = q_ref[x * 64 : (x + 1) * 64, g * DIM : (g + 1) * DIM]
     acc_ref[...] = jnp.zeros_like(acc_ref)
-    for copy in copies:
-        copy.wait()
-
+
+    starts = [jnp.int32(0)]
+    for i in range(NX - 1):
+        starts.append(starts[-1] + (mx + i) % NX + 1)
     tiles = NX * (NX + 1) // 2
 
     def tile(t):
         t = jnp.int32(t)
-        x = sum((t >= n).astype(jnp.int32) for n in (1, 3, 6))
-        u = t - x * (x + 1) // 2
+        x, begin = mx, starts[0]
+        for i in range(1, NX):
+            x = jnp.where(t >= starts[i], (mx + i) % NX, x)
+            begin = jnp.where(t >= starts[i], starts[i], begin)
+        u = t - begin
         return x, u, jnp.where(u == 0, x, u - 1), t % 2
 
     def scores(t):
@@ -259,8 +278,12 @@
                     jnp.bfloat16
                 )
 
+    for copy in first_copies:
+        copy.wait()
     scores(0)
     weights(0)
+    for copy in other_copies:
+        copy.wait()
     scores(1)
 
     @pl.loop(0, tiles - 2)
@@ -272,6 +295,7 @@
 
     mix(tiles - 2)
     weights(tiles - 1)
+    finish(tiles - 2)
     mix(tiles - 1)
     finish(tiles - 1)
 
@@ -383,7 +407,7 @@
             pltpu.VMEM((2, ROWS, DIM), jnp.float32),
             pltpu.VMEM((ROWS, DIM), jnp.float32),
             pltpu.VMEM((ROWS, 2 * DIM), jnp.float32),
-            pltpu.SemaphoreType.DMA((10,)),
+            pltpu.SemaphoreType.DMA((16,)),
         ],
     )(q, *pieces)
     soft = exchange(soft.reshape(NX * NZ, 8, HEADS * DIM), ("ctx_0", "head"))

time: 114 us -> 117 us (1.026)
  Pallas kernels: 25.6 us -> 27.6 us
    pallas_call x1, Pallas kernels: 21.1 us -> 23.2 us  [both(): call(softmax_kernel, [block], 11, 1 << 34, in_specs=vmem(1) + [pl.BlockSp...]
where the time goes in v7:
time: 117 us; the launch traced here: 115 us
  starting transfers between devices  40.5 us (35%)
  waiting for transfers between devices  28.3 us (24%)
  Pallas kernels  27.6 us (24%)
  blocking collectives  15.7 us (13%)
  local copies, waits for them, and re-layouts  1.77 us (2%)
    ppermute x23, waiting for transfers between devices, permute(): return lax.ppermute(value, axes, pairs)  28.3 us
    ppermute x23, starting transfers between devices, permute(): return lax.ppermute(value, axes, pairs)  27.4 us
    pallas_call x1, Pallas kernels, both(): call(softmax_kernel, [block], 11, 1 << 34, in_specs=vmem(1) + [pl.BlockSp...  23.2 us
    all_to_all x1, blocking collectives, exchange(): return lax.all_to_all(value, axes, 0, 0, tiled=True)  15.7 us
    all_to_all x2, starting transfers between devices, exchange(): return lax.all_to_all(value, axes, 0, 0, tiled=True)  13.1 us
    pallas_call x1, Pallas kernels, both(): call(lightning_kernel, [block], 7, 1 << 29)  2.6 us
  transfers between devices with their start and end apart: 25, of which 17 were waited for; matrix products, arithmetic and copies ran while one was open for 0% of the time, Pallas kernels for 4%

profile of v7, /device:TPU:31, one launch (start us, length us, event | category | flops | bytes accessed | tf_op | source)
XLA Modules:
  0.0 114.8 jit_solution(8782685867251527635)
XLA Ops:
  1.5 15.7 %all_to_all.15 = bf16[8,32,256]{2,1,0:T(8,128)(2,1)S(1)} all-to-all(bf16[8,32,256]{2,1,0:T(8,128)(2,1)S(1)} %bitcast.24), channel_id=1, replica_groups=mesh['ctx_0'=4,'ctx_1'=4,'ctx_2'=2,'head'=8] {'head'}, dimensions={0} | all-to-all | bytes 262144 | tf_op jit(solution)/shard_map/all_to_all | solution.py:339
  17.3 1.5 %collective-permute-start.12 = (bf16[256,256]{1,0:T(8,128)(2,1)S(1)}, bf16[256,256]{1,0:T(8,128)(2,1)S(1)}, u32[]{:S(2)}, u32[]{:S(2)}) collective-permute-start(bf16[256,256]{1,0:T(8,128)(2,1)S(1)} %bitcast.26), channel_id=1, source_target_pairs={{0,192},{8,56},{16,208},{24,8},{32,224},{40,24},{48,240},{56,40},{... | collective-permute-start | bytes 393224 | tf_op jit(solution)/shard_map/ppermute | solution.py:335
  19.7 1.4 %collective-permute-done.11 = bf16[256,256]{1,0:T(8,128)(2,1)S(1)} collective-permute-done((bf16[256,256]{1,0:T(8,128)(2,1)S(1)}, bf16[256,256]{1,0:T(8,128)(2,1)S(1)}, u32[]{:S(2)}, u32[]{:S(2)}) %collective-permute-start.11) | collective-permute-done | bytes 131104 | tf_op jit(solution)/shard_map/ppermute | solution.py:335
  22.3 1.8 %collective-permute-done.13 = bf16[256,256]{1,0:T(8,128)(2,1)S(1)} collective-permute-done((bf16[256,256]{1,0:T(8,128)(2,1)S(1)}, bf16[256,256]{1,0:T(8,128)(2,1)S(1)}, u32[]{:S(2)}, u32[]{:S(2)}) %collective-permute-start.13) | collective-permute-done | bytes 131104 | tf_op jit(solution)/shard_map/ppermute | solution.py:335
  25.7 5.1 %all-to-all-start = ((bf16[32,8,1024]{2,1,0:T(8,128)(2,1)}), bf16[32,8,1024]{2,1,0:T(8,128)(2,1)S(1)}, u32[]{:S(2)}, u32[]{:S(2)}) async-start(bf16[32,8,1024]{2,1,0:T(8,128)(2,1)} %bitcast.3), calls=%async_computation | async-start | bytes 1048576 | tf_op jit(solution)/shard_map/all_to_all | solution.py:339
  30.8 5.3 %collective-permute-start.18 = (bf16[1024,256]{1,0:T(8,128)(2,1)S(1)}, bf16[1024,256]{1,0:T(8,128)(2,1)S(1)}, u32[]{:S(2)}, u32[]{:S(2)}) collective-permute-start(bf16[1024,256]{1,0:T(8,128)(2,1)S(1)} %pad_maximum_fusion.refs_1_), channel_id=1, source_target_pairs={{0,8},{8,0},{1,9},{9,1},{2,10},{10,2},{3,11},{11,3},{4,12},{12,4},... | collective-permute-start | bytes 1572872 | tf_op jit(solution)/shard_map/ppermute | solution.py:335
  36.3 1.5 %collective-permute-start.17 = (bf16[512,256]{1,0:T(8,128)(2,1)S(1)}, bf16[512,256]{1,0:T(8,128)(2,1)}, u32[]{:S(2)}, u32[]{:S(2)}) collective-permute-start(bf16[512,256]{1,0:T(8,128)(2,1)S(1)} %slice.9), channel_id=1, source_target_pairs={{0,48},{8,200},{16,0},{24,216},{32,16},{40,232},{48,32},{56,248},{... | collective-permute-start | bytes 786440 | tf_op jit(solution)/shard_map/ppermute | solution.py:335
  37.8 1.8 %collective-permute-start.19 = (bf16[1024,256]{1,0:T(8,128)(2,1)S(1)}, bf16[1024,256]{1,0:T(8,128)(2,1)S(1)}, u32[]{:S(2)}, u32[]{:S(2)}) collective-permute-start(bf16[1024,256]{1,0:T(8,128)(2,1)S(1)} %collective-permute-done.14.refs_2_), channel_id=1, source_target_pairs={{0,8},{8,0},{1,9},{9,1},{2,10},{10,2},{3,11},{11,3},{4,12},{12,4},... | collective-permute-start | bytes 1572872 | tf_op jit(solution)/shard_map/ppermute | solution.py:335
  39.6 4.4 %collective-permute-done.16.refs_4_ = bf16[512,256]{1,0:T(8,128)(2,1)S(1)} collective-permute-done((bf16[512,256]{1,0:T(8,128)(2,1)S(1)}, bf16[512,256]{1,0:T(8,128)(2,1)S(1)}, u32[]{:S(2)}, u32[]{:S(2)}) %collective-permute-start.16) | collective-permute-done | bytes 262176 | tf_op jit(solution)/shard_map/ppermute | solution.py:335
  45.1 1.6 %collective-permute-start.22 = (bf16[512,256]{1,0:T(8,128)(2,1)}, bf16[512,256]{1,0:T(8,128)(2,1)}, u32[]{:S(2)}, u32[]{:S(2)}) collective-permute-start(bf16[512,256]{1,0:T(8,128)(2,1)} %collective-permute-done.17.refs_5_), channel_id=1, source_target_pairs={{0,8},{8,0},{1,9},{9,1},{2,10},{10,2},{3,11},{11,3},{4,12},{12,4},... | collective-permute-start | bytes 786440 | tf_op jit(solution)/shard_map/ppermute | solution.py:335
  46.7 1.5 %collective-permute-done.22.refs_10_ = bf16[512,256]{1,0:T(8,128)(2,1)} collective-permute-done((bf16[512,256]{1,0:T(8,128)(2,1)}, bf16[512,256]{1,0:T(8,128)(2,1)}, u32[]{:S(2)}, u32[]{:S(2)}) %collective-permute-start.22) | collective-permute-done | bytes 262176 | tf_op jit(solution)/shard_map/ppermute | solution.py:335
  48.2 23.2 %shard_map.92 = bf16[256,1024]{1,0:T(8,128)(2,1)} custom-call(bf16[256,1024]{1,0:T(8,128)(2,1)S(1)} %bitcast.21, bf16[1024,256]{1,0:T(8,128)(2,1)S(1)} %pad_maximum_fusion.refs_1_, bf16[1024,256]{1,0:T(8,128)(2,1)S(1)} %collective-permute-done.14.refs_2_, bf16[1024,256]{1,0:T(8,128)(2,1)S(1)} %collective-permute-done.15.refs_3_, ...), custom_call_target="tpu_custom_call" | custom-call | flops 17179869184 | bytes 2097152 | tf_op jit(solution)/shard_map/pallas_call | solution.py:394
  71.4 8.0 %all-to-all-start.2 = ((bf16[32,8,1024]{2,1,0:T(8,128)(2,1)}), bf16[32,8,1024]{2,1,0:T(8,128)(2,1)S(1)}, u32[]{:S(2)}, u32[]{:S(2)}) async-start(bf16[32,8,1024]{2,1,0:T(8,128)(2,1)} %bitcast.7), calls=%async_computation.2 | async-start | bytes 1048576 | tf_op jit(solution)/shard_map/all_to_all | solution.py:339
  79.5 1.6 %shard_map.86 = (bf16[4,144,128]{2,1,0:T(8,128)(2,1)S(1)}, bf16[4,144,128]{2,1,0:T(8,128)(2,1)S(1)}) custom-call(bf16[256,1024]{1,0:T(8,128)(2,1)S(1)} %copy-done, bf16[256,1024]{1,0:T(8,128)(2,1)S(1)} %copy-done.1, f32[8,256]{1,0:T(8,128)S(1)} %copy-done.3), custom_call_target="tpu_custom_call" | custom-call | flops 268435456 | bytes 2097152 | tf_op jit(solution)/shard_map/pallas_call | solution.py:375
  85.0 1.3 %collective-permute-done.1.a_ref = bf16[144,128]{1,0:T(8,128)(2,1)S(1)} collective-permute-done((bf16[144,128]{1,0:T(8,128)(2,1)S(1)}, bf16[144,128]{1,0:T(8,128)(2,1)S(1)}, u32[]{:S(2)}, u32[]{:S(2)}) %collective-permute-start.1) | collective-permute-done | bytes 36896 | tf_op jit(solution)/shard_map/ppermute | solution.py:335
  86.3 2.0 %collective-permute-done.2.b_ref = bf16[144,128]{1,0:T(8,128)(2,1)S(1)} collective-permute-done((bf16[144,128]{1,0:T(8,128)(2,1)S(1)}, bf16[144,128]{1,0:T(8,128)(2,1)S(1)}, u32[]{:S(2)}, u32[]{:S(2)}) %collective-permute-start.2) | collective-permute-done | bytes 36896 | tf_op jit(solution)/shard_map/ppermute | solution.py:335
  88.3 1.4 %collective-permute-done.3.c_ref = bf16[144,128]{1,0:T(8,128)(2,1)S(1)} collective-permute-done((bf16[144,128]{1,0:T(8,128)(2,1)S(1)}, bf16[144,128]{1,0:T(8,128)(2,1)S(1)}, u32[]{:S(2)}, u32[]{:S(2)}) %collective-permute-start.3) | collective-permute-done | bytes 36896 | tf_op jit(solution)/shard_map/ppermute | solution.py:335
  89.8 1.3 %collective-permute-start.4 = (bf16[144,128]{1,0:T(8,128)(2,1)S(1)}, bf16[144,128]{1,0:T(8,128)(2,1)S(1)}, u32[]{:S(2)}, u32[]{:S(2)}) collective-permute-start(bf16[144,128]{1,0:T(8,128)(2,1)S(1)} %get-tuple-element.22), channel_id=1, source_target_pairs={{0,64},{64,128},{128,192},{1,65},{65,129},{129,193},{2,66},{66,130... | collective-permute-start | bytes 110600 | tf_op jit(solution)/shard_map/ppermute | solution.py:335
  94.8 2.4 %collective-permute-done.5.b_ref = bf16[144,128]{1,0:T(8,128)(2,1)S(1)} collective-permute-done((bf16[144,128]{1,0:T(8,128)(2,1)S(1)}, bf16[144,128]{1,0:T(8,128)(2,1)S(1)}, u32[]{:S(2)}, u32[]{:S(2)}) %collective-permute-start.5) | collective-permute-done | bytes 36896 | tf_op jit(solution)/shard_map/ppermute | solution.py:335
  97.3 2.8 %collective-permute-done.6.c_ref = bf16[144,128]{1,0:T(8,128)(2,1)S(1)} collective-permute-done((bf16[144,128]{1,0:T(8,128)(2,1)S(1)}, bf16[144,128]{1,0:T(8,128)(2,1)S(1)}, u32[]{:S(2)}, u32[]{:S(2)}) %collective-permute-start.6) | collective-permute-done | bytes 36896 | tf_op jit(solution)/shard_map/ppermute | solution.py:335
  101.7 1.3 %collective-permute-done.7.e1_ref = bf16[128,128]{1,0:T(8,128)(2,1)S(1)} collective-permute-done((bf16[128,128]{1,0:T(8,128)(2,1)S(1)}, bf16[128,128]{1,0:T(8,128)(2,1)S(1)}, u32[]{:S(2)}, u32[]{:S(2)}) %collective-permute-start.7) | collective-permute-done | bytes 32800 | tf_op jit(solution)/shard_map/ppermute | solution.py:335
  103.0 2.0 %collective-permute-done.8.e2_ref = bf16[128,128]{1,0:T(8,128)(2,1)S(1)} collective-permute-done((bf16[128,128]{1,0:T(8,128)(2,1)S(1)}, bf16[128,128]{1,0:T(8,128)(2,1)S(1)}, u32[]{:S(2)}, u32[]{:S(2)}) %collective-permute-start.8) | collective-permute-done | bytes 32800 | tf_op jit(solution)/shard_map/ppermute | solution.py:335
  105.7 4.7 %collective-permute-start.10 = (bf16[4,128,128]{2,1,0:T(8,128)(2,1)S(1)}, bf16[4,128,128]{2,1,0:T(8,128)(2,1)S(1)}, u32[]{:S(2)}, u32[]{:S(2)}) collective-permute-start(bf16[4,128,128]{2,1,0:T(8,128)(2,1)S(1)} %get-tuple-element.29), channel_id=1, source_target_pairs={{0,8},{8,0},{1,9},{9,1},{2,10},{10,2},{3,11},{11,3},{4,12},{12,4},... | collective-permute-start | bytes 393224 | tf_op jit(solution)/shard_map/ppermute | solution.py:335
  111.4 2.6 %shard_map.91 = bf16[256,1024]{1,0:T(8,128)(2,1)} custom-call(bf16[256,1024]{1,0:T(8,128)(2,1)S(1)} %copy-done.2, bf16[256,1024]{1,0:T(8,128)(2,1)S(1)} %copy-done, bf16[256,1024]{1,0:T(8,128)(2,1)S(1)} %copy-done.1, f32[8,256]{1,0:T(8,128)S(1)} %copy-done.3, f32[1,1024]{1,0:T(1,128)S(1)} %bitcast.22, bf16[4,128,128]{2,1,0:T(8,128)(2,1)S(1)} %get-tuple-element.28.keep_ref, ...), custom_call_target="tpu_custom_call" | custom-call | flops 536870912 | bytes 2097152 | tf_op jit(solution)/shard_map/pallas_call | solution.py:416
  (49 shorter events, 17.7 us)
Async XLA Ops:
  17.3 3.8 %collective-permute-start.11 = (bf16[256,256]{1,0:T(8,128)(2,1)S(1)}, bf16[256,256]{1,0:T(8,128)(2,1)S(1)}, u32[]{:S(2)}, u32[]{:S(2)}) collective-permute-start(bf16[256,256]{1,0:T(8,128)(2,1)S(1)} %bitcast.25), channel_id=1, source_target_pairs={{0,64},{8,24},{16,80},{24,40},{32,96},{40,56},{48,112},{56,8},{64,... | collective-permute-start | bytes 393224 | tf_op jit(solution)/shard_map/ppermute | solution.py:335
  17.3 5.0 %collective-permute-start.12 = (bf16[256,256]{1,0:T(8,128)(2,1)S(1)}, bf16[256,256]{1,0:T(8,128)(2,1)S(1)}, u32[]{:S(2)}, u32[]{:S(2)}) collective-permute-start(bf16[256,256]{1,0:T(8,128)(2,1)S(1)} %bitcast.26), channel_id=1, source_target_pairs={{0,192},{8,56},{16,208},{24,8},{32,224},{40,24},{48,240},{56,40},{... | collective-permute-start | bytes 393224 | tf_op jit(solution)/shard_map/ppermute | solution.py:335
  18.7 5.3 %collective-permute-start.13 = (bf16[256,256]{1,0:T(8,128)(2,1)S(1)}, bf16[256,256]{1,0:T(8,128)(2,1)S(1)}, u32[]{:S(2)}, u32[]{:S(2)}) collective-permute-start(bf16[256,256]{1,0:T(8,128)(2,1)S(1)} %bitcast.27), channel_id=1, source_target_pairs={{0,128},{8,40},{16,144},{24,56},{32,160},{40,8},{48,176},{56,24},{... | collective-permute-start | bytes 393224 | tf_op jit(solution)/shard_map/ppermute | solution.py:335
  24.1 12.0 %collective-permute-start.14 = (bf16[1024,256]{1,0:T(8,128)(2,1)S(1)}, bf16[1024,256]{1,0:T(8,128)(2,1)S(1)}, u32[]{:S(2)}, u32[]{:S(2)}) collective-permute-start(bf16[1024,256]{1,0:T(8,128)(2,1)S(1)} %pad_maximum_fusion.refs_1_), channel_id=1, source_target_pairs={{0,16},{8,72},{16,32},{24,88},{32,48},{40,104},{48,0},{56,120},{64... | collective-permute-start | bytes 1572872 | tf_op jit(solution)/shard_map/ppermute | solution.py:335
  24.4 11.8 %collective-permute-start.15 = (bf16[1024,256]{1,0:T(8,128)(2,1)S(1)}, bf16[1024,256]{1,0:T(8,128)(2,1)S(1)}, u32[]{:S(2)}, u32[]{:S(2)}) collective-permute-start(bf16[1024,256]{1,0:T(8,128)(2,1)S(1)} %pad_maximum_fusion.refs_1_), channel_id=1, source_target_pairs={{0,48},{8,200},{16,0},{24,216},{32,16},{40,232},{48,32},{56,248},{... | collective-permute-start | bytes 1572872 | tf_op jit(solution)/shard_map/ppermute | solution.py:335
  25.7 21.1 %all-to-all-start = ((bf16[32,8,1024]{2,1,0:T(8,128)(2,1)}), bf16[32,8,1024]{2,1,0:T(8,128)(2,1)S(1)}, u32[]{:S(2)}, u32[]{:S(2)}) async-start(bf16[32,8,1024]{2,1,0:T(8,128)(2,1)} %bitcast.3), calls=%async_computation | async-start | bytes 1048576 | tf_op jit(solution)/shard_map/all_to_all | solution.py:339
  30.8 15.9 %collective-permute-start.18 = (bf16[1024,256]{1,0:T(8,128)(2,1)S(1)}, bf16[1024,256]{1,0:T(8,128)(2,1)S(1)}, u32[]{:S(2)}, u32[]{:S(2)}) collective-permute-start(bf16[1024,256]{1,0:T(8,128)(2,1)S(1)} %pad_maximum_fusion.refs_1_), channel_id=1, source_target_pairs={{0,8},{8,0},{1,9},{9,1},{2,10},{10,2},{3,11},{11,3},{4,12},{12,4},... | collective-permute-start | bytes 1572872 | tf_op jit(solution)/shard_map/ppermute | solution.py:335
  36.1 7.9 %collective-permute-start.16 = (bf16[512,256]{1,0:T(8,128)(2,1)S(1)}, bf16[512,256]{1,0:T(8,128)(2,1)S(1)}, u32[]{:S(2)}, u32[]{:S(2)}) collective-permute-start(bf16[512,256]{1,0:T(8,128)(2,1)S(1)} %slice.8), channel_id=1, source_target_pairs={{0,16},{8,72},{16,32},{24,88},{32,48},{40,104},{48,0},{56,120},{64... | collective-permute-start | bytes 786440 | tf_op jit(solution)/shard_map/ppermute | solution.py:335
  36.3 8.8 %collective-permute-start.17 = (bf16[512,256]{1,0:T(8,128)(2,1)S(1)}, bf16[512,256]{1,0:T(8,128)(2,1)}, u32[]{:S(2)}, u32[]{:S(2)}) collective-permute-start(bf16[512,256]{1,0:T(8,128)(2,1)S(1)} %slice.9), channel_id=1, source_target_pairs={{0,48},{8,200},{16,0},{24,216},{32,16},{40,232},{48,32},{56,248},{... | collective-permute-start | bytes 786440 | tf_op jit(solution)/shard_map/ppermute | solution.py:335
  37.8 10.4 %collective-permute-start.19 = (bf16[1024,256]{1,0:T(8,128)(2,1)S(1)}, bf16[1024,256]{1,0:T(8,128)(2,1)S(1)}, u32[]{:S(2)}, u32[]{:S(2)}) collective-permute-start(bf16[1024,256]{1,0:T(8,128)(2,1)S(1)} %collective-permute-done.14.refs_2_), channel_id=1, source_target_pairs={{0,8},{8,0},{1,9},{9,1},{2,10},{10,2},{3,11},{11,3},{4,12},{12,4},... | collective-permute-start | bytes 1572872 | tf_op jit(solution)/shard_map/ppermute | solution.py:335
  39.6 8.6 %collective-permute-start.20 = (bf16[1024,256]{1,0:T(8,128)(2,1)S(1)}, bf16[1024,256]{1,0:T(8,128)(2,1)}, u32[]{:S(2)}, u32[]{:S(2)}) collective-permute-start(bf16[1024,256]{1,0:T(8,128)(2,1)S(1)} %collective-permute-done.15.refs_3_), channel_id=1, source_target_pairs={{0,8},{8,0},{1,9},{9,1},{2,10},{10,2},{3,11},{11,3},{4,12},{12,4},... | collective-permute-start | bytes 1572872 | tf_op jit(solution)/shard_map/ppermute | solution.py:335
  44.0 2.7 %collective-permute-start.21 = (bf16[512,256]{1,0:T(8,128)(2,1)S(1)}, bf16[512,256]{1,0:T(8,128)(2,1)}, u32[]{:S(2)}, u32[]{:S(2)}) collective-permute-start(bf16[512,256]{1,0:T(8,128)(2,1)S(1)} %collective-permute-done.16.refs_4_), channel_id=1, source_target_pairs={{0,8},{8,0},{1,9},{9,1},{2,10},{10,2},{3,11},{11,3},{4,12},{12,4},... | collective-permute-start | bytes 786440 | tf_op jit(solution)/shard_map/ppermute | solution.py:335
  45.1 3.1 %collective-permute-start.22 = (bf16[512,256]{1,0:T(8,128)(2,1)}, bf16[512,256]{1,0:T(8,128)(2,1)}, u32[]{:S(2)}, u32[]{:S(2)}) collective-permute-start(bf16[512,256]{1,0:T(8,128)(2,1)} %collective-permute-done.17.refs_5_), channel_id=1, source_target_pairs={{0,8},{8,0},{1,9},{9,1},{2,10},{10,2},{3,11},{11,3},{4,12},{12,4},... | collective-permute-start | bytes 786440 | tf_op jit(solution)/shard_map/ppermute | solution.py:335
  71.4 42.6 %all-to-all-start.2 = ((bf16[32,8,1024]{2,1,0:T(8,128)(2,1)}), bf16[32,8,1024]{2,1,0:T(8,128)(2,1)S(1)}, u32[]{:S(2)}, u32[]{:S(2)}) async-start(bf16[32,8,1024]{2,1,0:T(8,128)(2,1)} %bitcast.7), calls=%async_computation.2 | async-start | bytes 1048576 | tf_op jit(solution)/shard_map/all_to_all | solution.py:339
  83.1 3.2 %collective-permute-start.1 = (bf16[144,128]{1,0:T(8,128)(2,1)S(1)}, bf16[144,128]{1,0:T(8,128)(2,1)S(1)}, u32[]{:S(2)}, u32[]{:S(2)}) collective-permute-start(bf16[144,128]{1,0:T(8,128)(2,1)S(1)} %get-tuple-element.19), channel_id=1, source_target_pairs={{0,16},{16,32},{32,48},{48,0},{1,17},{17,33},{33,49},{49,1},{2,18}... | collective-permute-start | bytes 110600 | tf_op jit(solution)/shard_map/ppermute | solution.py:335
  83.7 4.6 %collective-permute-start.2 = (bf16[144,128]{1,0:T(8,128)(2,1)S(1)}, bf16[144,128]{1,0:T(8,128)(2,1)S(1)}, u32[]{:S(2)}, u32[]{:S(2)}) collective-permute-start(bf16[144,128]{1,0:T(8,128)(2,1)S(1)} %get-tuple-element.20), channel_id=1, source_target_pairs={{0,32},{16,48},{32,0},{48,16},{1,33},{17,49},{33,1},{49,17},{2,34}... | collective-permute-start | bytes 110600 | tf_op jit(solution)/shard_map/ppermute | solution.py:335
  85.0 4.7 %collective-permute-start.3 = (bf16[144,128]{1,0:T(8,128)(2,1)S(1)}, bf16[144,128]{1,0:T(8,128)(2,1)S(1)}, u32[]{:S(2)}, u32[]{:S(2)}) collective-permute-start(bf16[144,128]{1,0:T(8,128)(2,1)S(1)} %get-tuple-element.21), channel_id=1, source_target_pairs={{0,48},{16,0},{32,16},{48,32},{1,49},{17,1},{33,17},{49,33},{2,50}... | collective-permute-start | bytes 110600 | tf_op jit(solution)/shard_map/ppermute | solution.py:335
  89.8 5.1 %collective-permute-start.4 = (bf16[144,128]{1,0:T(8,128)(2,1)S(1)}, bf16[144,128]{1,0:T(8,128)(2,1)S(1)}, u32[]{:S(2)}, u32[]{:S(2)}) collective-permute-start(bf16[144,128]{1,0:T(8,128)(2,1)S(1)} %get-tuple-element.22), channel_id=1, source_target_pairs={{0,64},{64,128},{128,192},{1,65},{65,129},{129,193},{2,66},{66,130... | collective-permute-start | bytes 110600 | tf_op jit(solution)/shard_map/ppermute | solution.py:335
  91.1 6.2 %collective-permute-start.5 = (bf16[144,128]{1,0:T(8,128)(2,1)S(1)}, bf16[144,128]{1,0:T(8,128)(2,1)S(1)}, u32[]{:S(2)}, u32[]{:S(2)}) collective-permute-start(bf16[144,128]{1,0:T(8,128)(2,1)S(1)} %get-tuple-element.22), channel_id=1, source_target_pairs={{0,128},{64,192},{1,129},{65,193},{2,130},{66,194},{3,131},{67,195... | collective-permute-start | bytes 110600 | tf_op jit(solution)/shard_map/ppermute | solution.py:335
  92.4 7.7 %collective-permute-start.6 = (bf16[144,128]{1,0:T(8,128)(2,1)S(1)}, bf16[144,128]{1,0:T(8,128)(2,1)S(1)}, u32[]{:S(2)}, u32[]{:S(2)}) collective-permute-start(bf16[144,128]{1,0:T(8,128)(2,1)S(1)} %get-tuple-element.22), channel_id=1, source_target_pairs={{0,192},{1,193},{2,194},{3,195},{4,196},{5,197},{6,198},{7,199},{8... | collective-permute-start | bytes 110600 | tf_op jit(solution)/shard_map/ppermute | solution.py:335
  100.2 2.8 %collective-permute-start.7 = (bf16[128,128]{1,0:T(8,128)(2,1)S(1)}, bf16[128,128]{1,0:T(8,128)(2,1)S(1)}, u32[]{:S(2)}, u32[]{:S(2)}) collective-permute-start(bf16[128,128]{1,0:T(8,128)(2,1)S(1)} %get-tuple-element.25), channel_id=1, source_target_pairs={{0,16},{16,32},{32,48},{48,0},{1,17},{17,33},{33,49},{49,1},{2,18}... | collective-permute-start | bytes 98312 | tf_op jit(solution)/shard_map/ppermute | solution.py:335
  100.7 4.3 %collective-permute-start.8 = (bf16[128,128]{1,0:T(8,128)(2,1)S(1)}, bf16[128,128]{1,0:T(8,128)(2,1)S(1)}, u32[]{:S(2)}, u32[]{:S(2)}) collective-permute-start(bf16[128,128]{1,0:T(8,128)(2,1)S(1)} %get-tuple-element.26), channel_id=1, source_target_pairs={{0,32},{16,48},{32,0},{48,16},{1,33},{17,49},{33,1},{49,17},{2,34}... | collective-permute-start | bytes 98312 | tf_op jit(solution)/shard_map/ppermute | solution.py:335
  101.6 4.0 %collective-permute-start.9 = (bf16[128,128]{1,0:T(8,128)(2,1)S(1)}, bf16[128,128]{1,0:T(8,128)(2,1)S(1)}, u32[]{:S(2)}, u32[]{:S(2)}) collective-permute-start(bf16[128,128]{1,0:T(8,128)(2,1)S(1)} %get-tuple-element.27), channel_id=1, source_target_pairs={{0,48},{16,0},{32,16},{48,32},{1,49},{17,1},{33,17},{49,33},{2,50}... | collective-permute-start | bytes 98312 | tf_op jit(solution)/shard_map/ppermute | solution.py:335
  105.7 5.7 %collective-permute-start.10 = (bf16[4,128,128]{2,1,0:T(8,128)(2,1)S(1)}, bf16[4,128,128]{2,1,0:T(8,128)(2,1)S(1)}, u32[]{:S(2)}, u32[]{:S(2)}) collective-permute-start(bf16[4,128,128]{2,1,0:T(8,128)(2,1)S(1)} %get-tuple-element.29), channel_id=1, source_target_pairs={{0,8},{8,0},{1,9},{9,1},{2,10},{10,2},{3,11},{11,3},{4,12},{12,4},... | collective-permute-start | bytes 393224 | tf_op jit(solution)/shard_map/ppermute | solution.py:335
  (6 other events, 83.3 us)
